TPU v7x, 128 devices: a whole 4x4x4 slice. The times are simulated.
128 devices in a mesh: ctx: 32 (over y, x, core), head: 4 (over z).
Axes of the slice: x: 4, y: 4, z: 4, core: 2. Of those that a mesh axis runs over, the one named last changes fastest.
Arguments:
- queries: bfloat16 [65536, 4096], P('ctx', 'head'), may hold values from -2 to 2
- key_rows: bfloat16 [65536, 4096], P('ctx', 'head'), may hold values from -2 to 2
- value_rows: bfloat16 [65536, 4096], P('ctx', 'head'), may hold values from -6 to 6
- log_decay: bfloat16 [65536, 32], P('ctx', 'head'), may hold values from -0.4 to 0, as said below
- norm_gain: float32 [4096], P('head'), may hold values from 0.1 to 1.9
- doc_lengths: int32 [64], replicated, may hold values from 1 to 32768, 65536 in all
- packing: int32 [512], replicated, may hold values from 0 to 511, as said below
Outputs:
- mixed: bfloat16 [65536, 4096], P('ctx', 'head')
Inputs may be any that keep to these rules, and one draw needn't show every extreme that they name: packing is a permutation of the blocks. Loader block b is block b % 16 of ctx device b // 16; packed block p belongs to owner p // 16. Of the blocks of one loader, each owner receives none or exactly 1. `doc_lengths`: the lengths sum to 65536; the longest is 32768. `log_decay`: negative logarithms of decays.
All inputs are finite; a program needn't handle non-finite values.
Results may differ from a plain program's by a relative error of at most 0.0055.
Values may be sent and summed in bfloat16 or wider, within the bound.
No kernel may reach another device: no remote copies, remote signals or barrier semaphores. Data moves between devices by JAX's collectives and lax.ppermute only.
A program may use at most 192 MiB of HBM per device.

v0:
```python
import jax
import jax.numpy as jnp
from jax import lax
from jax.sharding import PartitionSpec as P

BLOCK = 128


def from_behind(x, axis, by):
    count = lax.axis_size(axis)
    pairs = [(i, i + by) for i in range(count) if 0 <= i + by < count]
    return lax.ppermute(x, axis, pairs)


def state_pass(key_blocks, value_blocks, decay_blocks, first, docid):
    block_log = jnp.cumsum(decay_blocks.astype(jnp.float32), axis=1)
    block_total = block_log[:, -1, :]
    seen = jnp.cumsum(first, axis=1)
    reach_block = (seen == 0).astype(jnp.float32)
    unbroken = (seen[:, -1] == 0).astype(jnp.float32)
    same_last = (docid == docid[:, -1:]).astype(jnp.float32)
    keep = jnp.exp(block_total[:, None, :] - block_log) * same_last[:, :, None]
    key_decayed = (key_blocks.astype(jnp.float32) * keep[..., None]).astype(jnp.bfloat16)
    own = jnp.einsum(
        "nshd,nshe->nhde", key_decayed, value_blocks, preferred_element_type=jnp.float32
    )
    gate = jnp.exp(block_total) * unbroken[:, None]

    def advance(state, item):
        factor, term = item
        return (factor[:, None, None] * state + term, state)

    start = jnp.zeros(own.shape[1:], jnp.float32)
    s_end, states = lax.scan(advance, start, (gate, own))
    prior = jnp.cumsum(block_total, axis=0) - block_total
    segment_log = block_log + prior[:, None, :]
    block_starts = seen[:, -1]
    before = jnp.cumsum(block_starts) - block_starts
    reach_segment = (seen + before[:, None] == 0).astype(jnp.float32)
    clean = (jnp.sum(first) == 0).astype(jnp.float32)
    decay_all = jnp.exp(segment_log[-1, -1]) * clean
    return (block_log, reach_block, states, segment_log, reach_segment, decay_all, s_end)


def query_pass(query_blocks, key_blocks, value_blocks, block_log, reach_block, states, docid):
    length = docid.shape[1]
    order = jnp.arange(length)
    causal = order[:, None] >= order[None, :]
    allowed = causal[None] & (docid[:, :, None] == docid[:, None, :])
    by_head = jnp.transpose(block_log, (0, 2, 1))
    gaps = by_head[:, :, :, None] - by_head[:, :, None, :]
    weight = jnp.where(allowed[:, None], jnp.exp(jnp.minimum(gaps, 0.0)), 0.0)
    scores = jnp.einsum(
        "nthd,nshd->nhts", query_blocks, key_blocks, preferred_element_type=jnp.float32
    )
    weights = (scores * weight).astype(jnp.bfloat16)
    intra = jnp.einsum("nhts,nshd->nthd", weights, value_blocks, preferred_element_type=jnp.float32)
    query_decayed = (
        query_blocks.astype(jnp.float32) * (jnp.exp(block_log) * reach_block[:, :, None])[..., None]
    ).astype(jnp.bfloat16)
    inter = jnp.einsum(
        "nthd,nhde->nthe",
        query_decayed,
        states.astype(jnp.bfloat16),
        preferred_element_type=jnp.float32,
    )
    return intra + inter


def carry_in(decay_all, s_end, devices):
    zero_state = jnp.zeros(s_end.shape, jnp.float32)

    def forward(index, pair):
        arrived = from_behind(pair[1], "ctx", 1)
        return (arrived, decay_all[:, None, None] * arrived + s_end)

    arrival, leaving = lax.fori_loop(0, devices - 1, forward, (zero_state, s_end))
    return arrival


def body(queries, key_rows, value_rows, log_decay, norm_gain, doc_lengths, packing):
    rows, width = queries.shape
    heads = log_decay.shape[1]
    head_size = width // heads
    blocks = rows // BLOCK
    devices = lax.axis_size("ctx")
    mine = lax.axis_index("ctx")
    total_blocks = packing.shape[0]
    capacity = (2 * blocks + devices - 1) // devices
    owners = (packing // blocks).reshape(devices, blocks)
    local = jnp.arange(blocks, dtype=jnp.int32)
    earlier_mask = local[:, None] < local[None, :]
    same_owner = owners[:, :, None] == owners[:, None, :]
    ranks = jnp.sum((same_owner & earlier_mask[None]).astype(jnp.int32), axis=1)
    my_owner = lax.dynamic_index_in_dim(owners, mine, 0, keepdims=False)
    my_rank = lax.dynamic_index_in_dim(ranks, mine, 0, keepdims=False)
    slot_of = my_owner * capacity + my_rank
    slot_ids = jnp.arange(devices * capacity, dtype=jnp.int32)
    matched = slot_of[None, :] == slot_ids[:, None]
    source = jnp.sum(matched.astype(jnp.int32) * local[None, :], axis=1)
    filled = jnp.any(matched, axis=1)

    def outgoing(values):
        columns = values.shape[1]
        picked = jnp.take(values.reshape(blocks, BLOCK, columns), source, axis=0)
        kept = jnp.where(filled[:, None, None], picked, jnp.zeros((), values.dtype))
        return kept

    target = mine * blocks + local
    block_index = jnp.arange(total_blocks, dtype=jnp.int32)
    wanted = packing[None, :] == target[:, None]
    loader_block = jnp.sum(wanted.astype(jnp.int32) * block_index[None, :], axis=1)
    column = loader_block // blocks * capacity + jnp.take(ranks.reshape(-1), loader_block)

    def arriving(values):
        return jnp.take(values, column, axis=0)

    starts = jnp.cumsum(doc_lengths) - doc_lengths
    positions = mine * rows + jnp.arange(rows, dtype=jnp.int32)
    first = (
        jnp.any(positions[:, None] == starts[None, :], axis=1)
        .astype(jnp.int32)
        .reshape(blocks, BLOCK)
    )
    docid = (
        jnp.sum((starts[None, :] <= positions[:, None]).astype(jnp.int32), axis=1) - 1
    ).reshape(blocks, BLOCK)
    got_queries, got_keys, got_values, received_decay = (
        lax.all_to_all(outgoing(queries), "ctx", split_axis=0, concat_axis=0, tiled=True),
        lax.all_to_all(outgoing(key_rows), "ctx", split_axis=0, concat_axis=0, tiled=True),
        lax.all_to_all(outgoing(value_rows), "ctx", split_axis=0, concat_axis=0, tiled=True),
        lax.all_to_all(outgoing(log_decay), "ctx", split_axis=0, concat_axis=0, tiled=True),
    )
    key_blocks = arriving(got_keys).reshape(blocks, BLOCK, heads, head_size)
    value_blocks = arriving(got_values).reshape(blocks, BLOCK, heads, head_size)
    decay_blocks = arriving(received_decay)
    block_log, reach_block, states, segment_log, reach_segment, decay_all, s_end = state_pass(
        key_blocks, value_blocks, decay_blocks, first, docid
    )
    arrival = carry_in(decay_all, s_end, devices)
    query_blocks = arriving(got_queries).reshape(blocks, BLOCK, heads, head_size)
    local_out = query_pass(
        query_blocks, key_blocks, value_blocks, block_log, reach_block, states, docid
    )
    scaled = (
        query_blocks.astype(jnp.float32)
        * (jnp.exp(segment_log) * reach_segment[:, :, None])[..., None]
    ).astype(jnp.bfloat16)
    carried = jnp.einsum(
        "nthd,hde->nthe", scaled, arrival.astype(jnp.bfloat16), preferred_element_type=jnp.float32
    )
    total = (local_out + carried).reshape(rows, width)
    squares = lax.psum(jnp.sum(total * total, axis=1), "head")
    columns_all = width * lax.axis_size("head")
    scale = lax.rsqrt(squares / columns_all + 1e-05)
    return (total * scale[:, None] * norm_gain[None, :]).astype(jnp.bfloat16)


def solution(mesh):
    placed = (
        P("ctx", "head"),
        P("ctx", "head"),
        P("ctx", "head"),
        P("ctx", "head"),
        P("head"),
        P(),
        P(),
    )
    return jax.shard_map(
        body, mesh=mesh, in_specs=placed, out_specs=P("ctx", "head"), check_vma=False
    )
```

profile of v0, /device:TPU:16, one launch (start us, length us, event | category | flops | bytes accessed | tf_op | source)
XLA Modules:
  0.0 911.6 jit_solution(6602307076440885109)
XLA Ops:
  2.8 7.4 all-to-all-start.3
  10.2 7.1 gather_fusion.7
  17.3 7.1 gather_fusion.5
  24.5 7.1 gather_fusion.3
  31.6 16.5 %select_select_fusion = (bf16[32,128,1024]{2,1,0:T(8,128)(2,1)}, bf16[32,128,1024]{2,1,0:T(8,128)(2,1)}, bf16[32,128,1024]{2,1,0:T(8,128)(2,1)}) fusion(bf16[32,128,1024]{2,1,0:T(8,128)(2,1)} %gather_fusion.7, pred[32]{0:T(512)(128)(4,1)S(1)} %compare_and_fusion.2, pred[32]{0:T(512)(128)(4,1)S(1)} %fusion.28, bf16[32,128,1024]{2,1,0:T(8,128)(2,1)} %gather_fusion.5, ...), kind=kLoop, calls=%fused_computation.22 | loop fusion | flops 25165824 | bytes 50331712 | tf_op jit(solution)/shard_map/jit(_where)/select_n | solution.py:106
  48.1 101.1 %all_to_all.20 = bf16[32,128,1024]{2,1,0:T(8,128)(2,1)} all-to-all(bf16[32,128,1024]{2,1,0:T(8,128)(2,1)} %get-tuple-element.142), channel_id=1, replica_groups=mesh['ctx'=32,'head'=4] {'ctx'}, dimensions={0} | all-to-all | bytes 16777216 | tf_op jit(solution)/shard_map/all_to_all | solution.py:130
  149.2 99.6 %all_to_all.21 = bf16[32,128,1024]{2,1,0:T(8,128)(2,1)} all-to-all(bf16[32,128,1024]{2,1,0:T(8,128)(2,1)S(1)} %copy-done.2), channel_id=1, replica_groups=mesh['ctx'=32,'head'=4] {'ctx'}, dimensions={0} | all-to-all | bytes 16777216 | tf_op jit(solution)/shard_map/all_to_all | solution.py:129
  248.8 8.2 all-to-all-start
  263.4 23.3 %fusion.40 = f32[16,128,8]{2,0,1:T(8,128)S(1)} fusion(f32[16,128,8]{2,0,1:T(8,128)S(1)} %copy.199), kind=kOutput, calls=%fused_computation.121 | output fusion | flops 2080768 | bytes 131072 | tf_op jit(solution)/shard_map/jit(cumsum)/reduce_window_sum | solution.py:16
  286.9 2.1 exponential_multiply_fusion
  293.8 6.2 gather_fusion.8
  300.0 6.2 gather_fusion.6
  306.2 54.6 %all-to-all-done = bf16[32,128,1024]{2,1,0:T(8,128)(2,1)} async-done(((bf16[32,128,1024]{2,1,0:T(8,128)(2,1)}), bf16[32,128,1024]{2,1,0:T(8,128)(2,1)}, u32[]{:S(2)}, u32[]{:S(2)}) %all-to-all-start) | async-done | bytes 8388640 | tf_op jit(solution)/shard_map/all_to_all | solution.py:131
  360.8 6.2 gather_fusion.4
  367.0 8.9 broadcast_select_fusion
  375.9 6.4 copy.191
  382.3 6.4 copy.190
  388.7 6.4 copy.231
  395.0 9.7 %fusion.6 = f32[16,8,128,128]{3,2,1,0:T(8,128)} fusion(bf16[16,128,8,128]{1,3,2,0:T(8,128)(2,1)} %bitcast.80, bf16[16,128,8,128]{1,3,2,0:T(8,128)(2,1)} %bitcast.82, f32[16,128,8]{1,2,0:T(8,128)S(1)} %copy.206), kind=kOutput, calls=%fused_computation.29 | convolution fusion | flops 543162368 | bytes 16842752 | tf_op jit(solution)/shard_map/nshd,nshe->nhde/dot_general | solution.py:24
  404.7 31.0 %while.28 = (s32[]{:T(128)}, f32[8,128,128]{2,1,0:T(8,128)S(1)}, bf16[16,8,128,128]{3,2,1,0:T(8,128)(2,1)}, f32[16,8]{1,0:T(8,128)S(1)}, f32[16,8,128,128]{3,2,1,0:T(8,128)}) while((s32[]{:T(128)}, f32[8,128,128]{2,1,0:T(8,128)S(1)}, bf16[16,8,128,128]{3,2,1,0:T(8,128)(2,1)}, f32[16,8]{1,0:T(8,128)S(1)}, ...), condition=%wide.region_10.13_spmd.clone.clone, body=%wide.region_9.12_spmd.clone.sunk.clone | while | flops 524291 | bytes 2359484 | solution.py:34
  435.8 11.0 %fusion.5 = f32[16,8,128,128]{3,2,1,0:T(8,128)} fusion(bf16[16,128,8,128]{1,3,2,0:T(8,128)(2,1)} %bitcast.81, f32[16,8,128]{2,1,0:T(8,128)S(1)} %copy.200, pred[16,128,128]{2,1,0:T(8,128)(4,1)S(1)} %compare_and_fusion, bf16[16,128,8,128]{1,3,2,0:T(8,128)(2,1)} %bitcast.73, bf16[16,128,8,128]{1,3,2,0:T(8,128)(2,1)} %bitcast.83), kind=kOutput, calls=%fused_computation.28 | convolution fusion | flops 1084227584 | bytes 21299200 | tf_op jit(solution)/shard_map/nhts,nshd->nthd/dot_general | solution.py:57
  446.7 8.4 fusion.9
  455.1 415.9 %while.27 = (s32[]{:T(128)}, f32[8,128,128]{2,1,0:T(8,128)}, f32[8,128,128]{2,1,0:T(8,128)S(1)}, f32[8]{0:T(128)S(1)}, f32[8,128,128]{2,1,0:T(8,128)S(1)}) while((s32[]{:T(128)}, f32[8,128,128]{2,1,0:T(8,128)}, f32[8,128,128]{2,1,0:T(8,128)S(1)}, f32[8]{0:T(128)S(1)}, f32[8,128,128]{2,1,0:T(8,128)S(1)}) %tuple.63), condition=%wide.region_14.17_spmd.clone, body=%wide.region_13.16_spmd.sunk.clone | while | flops 262146 | bytes 5767329 | solution.py:77
  455.1 1.9 collective-permute-start
  457.0 10.7 %collective-permute-done = f32[8,128,128]{2,1,0:T(8,128)S(1)} collective-permute-done((f32[8,128,128]{2,1,0:T(8,128)S(1)}, f32[8,128,128]{2,1,0:T(8,128)S(1)}, u32[]{:S(2)}, u32[]{:S(2)}) %collective-permute-start) | collective-permute-done | bytes 524320 | tf_op jit(solution)/shard_map/while/body/eval_jaxpr/ppermute | solution.py:12
  468.5 1.9 collective-permute-start
  470.4 10.7 %collective-permute-done = f32[8,128,128]{2,1,0:T(8,128)S(1)} collective-permute-done((f32[8,128,128]{2,1,0:T(8,128)S(1)}, f32[8,128,128]{2,1,0:T(8,128)S(1)}, u32[]{:S(2)}, u32[]{:S(2)}) %collective-permute-start) | collective-permute-done | bytes 524320 | tf_op jit(solution)/shard_map/while/body/eval_jaxpr/ppermute | solution.py:12
  481.9 1.9 collective-permute-start
  483.8 10.7 %collective-permute-done = f32[8,128,128]{2,1,0:T(8,128)S(1)} collective-permute-done((f32[8,128,128]{2,1,0:T(8,128)S(1)}, f32[8,128,128]{2,1,0:T(8,128)S(1)}, u32[]{:S(2)}, u32[]{:S(2)}) %collective-permute-start) | collective-permute-done | bytes 524320 | tf_op jit(solution)/shard_map/while/body/eval_jaxpr/ppermute | solution.py:12
  495.3 1.9 collective-permute-start
  497.3 10.7 %collective-permute-done = f32[8,128,128]{2,1,0:T(8,128)S(1)} collective-permute-done((f32[8,128,128]{2,1,0:T(8,128)S(1)}, f32[8,128,128]{2,1,0:T(8,128)S(1)}, u32[]{:S(2)}, u32[]{:S(2)}) %collective-permute-start) | collective-permute-done | bytes 524320 | tf_op jit(solution)/shard_map/while/body/eval_jaxpr/ppermute | solution.py:12
  508.8 1.9 collective-permute-start
  510.7 10.7 %collective-permute-done = f32[8,128,128]{2,1,0:T(8,128)S(1)} collective-permute-done((f32[8,128,128]{2,1,0:T(8,128)S(1)}, f32[8,128,128]{2,1,0:T(8,128)S(1)}, u32[]{:S(2)}, u32[]{:S(2)}) %collective-permute-start) | collective-permute-done | bytes 524320 | tf_op jit(solution)/shard_map/while/body/eval_jaxpr/ppermute | solution.py:12
  524.1 10.7 %collective-permute-done = f32[8,128,128]{2,1,0:T(8,128)S(1)} collective-permute-done((f32[8,128,128]{2,1,0:T(8,128)S(1)}, f32[8,128,128]{2,1,0:T(8,128)S(1)}, u32[]{:S(2)}, u32[]{:S(2)}) %collective-permute-start) | collective-permute-done | bytes 524320 | tf_op jit(solution)/shard_map/while/body/eval_jaxpr/ppermute | solution.py:12
  537.5 10.7 %collective-permute-done = f32[8,128,128]{2,1,0:T(8,128)S(1)} collective-permute-done((f32[8,128,128]{2,1,0:T(8,128)S(1)}, f32[8,128,128]{2,1,0:T(8,128)S(1)}, u32[]{:S(2)}, u32[]{:S(2)}) %collective-permute-start) | collective-permute-done | bytes 524320 | tf_op jit(solution)/shard_map/while/body/eval_jaxpr/ppermute | solution.py:12
  550.9 10.7 %collective-permute-done = f32[8,128,128]{2,1,0:T(8,128)S(1)} collective-permute-done((f32[8,128,128]{2,1,0:T(8,128)S(1)}, f32[8,128,128]{2,1,0:T(8,128)S(1)}, u32[]{:S(2)}, u32[]{:S(2)}) %collective-permute-start) | collective-permute-done | bytes 524320 | tf_op jit(solution)/shard_map/while/body/eval_jaxpr/ppermute | solution.py:12
  564.3 10.7 %collective-permute-done = f32[8,128,128]{2,1,0:T(8,128)S(1)} collective-permute-done((f32[8,128,128]{2,1,0:T(8,128)S(1)}, f32[8,128,128]{2,1,0:T(8,128)S(1)}, u32[]{:S(2)}, u32[]{:S(2)}) %collective-permute-start) | collective-permute-done | bytes 524320 | tf_op jit(solution)/shard_map/while/body/eval_jaxpr/ppermute | solution.py:12
  577.8 10.7 %collective-permute-done = f32[8,128,128]{2,1,0:T(8,128)S(1)} collective-permute-done((f32[8,128,128]{2,1,0:T(8,128)S(1)}, f32[8,128,128]{2,1,0:T(8,128)S(1)}, u32[]{:S(2)}, u32[]{:S(2)}) %collective-permute-start) | collective-permute-done | bytes 524320 | tf_op jit(solution)/shard_map/while/body/eval_jaxpr/ppermute | solution.py:12
  591.2 10.7 %collective-permute-done = f32[8,128,128]{2,1,0:T(8,128)S(1)} collective-permute-done((f32[8,128,128]{2,1,0:T(8,128)S(1)}, f32[8,128,128]{2,1,0:T(8,128)S(1)}, u32[]{:S(2)}, u32[]{:S(2)}) %collective-permute-start) | collective-permute-done | bytes 524320 | tf_op jit(solution)/shard_map/while/body/eval_jaxpr/ppermute | solution.py:12
  604.6 10.7 %collective-permute-done = f32[8,128,128]{2,1,0:T(8,128)S(1)} collective-permute-done((f32[8,128,128]{2,1,0:T(8,128)S(1)}, f32[8,128,128]{2,1,0:T(8,128)S(1)}, u32[]{:S(2)}, u32[]{:S(2)}) %collective-permute-start) | collective-permute-done | bytes 524320 | tf_op jit(solution)/shard_map/while/body/eval_jaxpr/ppermute | solution.py:12
  618.0 10.7 %collective-permute-done = f32[8,128,128]{2,1,0:T(8,128)S(1)} collective-permute-done((f32[8,128,128]{2,1,0:T(8,128)S(1)}, f32[8,128,128]{2,1,0:T(8,128)S(1)}, u32[]{:S(2)}, u32[]{:S(2)}) %collective-permute-start) | collective-permute-done | bytes 524320 | tf_op jit(solution)/shard_map/while/body/eval_jaxpr/ppermute | solution.py:12
  631.4 10.7 %collective-permute-done = f32[8,128,128]{2,1,0:T(8,128)S(1)} collective-permute-done((f32[8,128,128]{2,1,0:T(8,128)S(1)}, f32[8,128,128]{2,1,0:T(8,128)S(1)}, u32[]{:S(2)}, u32[]{:S(2)}) %collective-permute-start) | collective-permute-done | bytes 524320 | tf_op jit(solution)/shard_map/while/body/eval_jaxpr/ppermute | solution.py:12
  644.8 10.7 %collective-permute-done = f32[8,128,128]{2,1,0:T(8,128)S(1)} collective-permute-done((f32[8,128,128]{2,1,0:T(8,128)S(1)}, f32[8,128,128]{2,1,0:T(8,128)S(1)}, u32[]{:S(2)}, u32[]{:S(2)}) %collective-permute-start) | collective-permute-done | bytes 524320 | tf_op jit(solution)/shard_map/while/body/eval_jaxpr/ppermute | solution.py:12
  658.3 10.7 %collective-permute-done = f32[8,128,128]{2,1,0:T(8,128)S(1)} collective-permute-done((f32[8,128,128]{2,1,0:T(8,128)S(1)}, f32[8,128,128]{2,1,0:T(8,128)S(1)}, u32[]{:S(2)}, u32[]{:S(2)}) %collective-permute-start) | collective-permute-done | bytes 524320 | tf_op jit(solution)/shard_map/while/body/eval_jaxpr/ppermute | solution.py:12
  671.7 10.7 %collective-permute-done = f32[8,128,128]{2,1,0:T(8,128)S(1)} collective-permute-done((f32[8,128,128]{2,1,0:T(8,128)S(1)}, f32[8,128,128]{2,1,0:T(8,128)S(1)}, u32[]{:S(2)}, u32[]{:S(2)}) %collective-permute-start) | collective-permute-done | bytes 524320 | tf_op jit(solution)/shard_map/while/body/eval_jaxpr/ppermute | solution.py:12
  685.1 10.7 %collective-permute-done = f32[8,128,128]{2,1,0:T(8,128)S(1)} collective-permute-done((f32[8,128,128]{2,1,0:T(8,128)S(1)}, f32[8,128,128]{2,1,0:T(8,128)S(1)}, u32[]{:S(2)}, u32[]{:S(2)}) %collective-permute-start) | collective-permute-done | bytes 524320 | tf_op jit(solution)/shard_map/while/body/eval_jaxpr/ppermute | solution.py:12
  698.5 10.7 %collective-permute-done = f32[8,128,128]{2,1,0:T(8,128)S(1)} collective-permute-done((f32[8,128,128]{2,1,0:T(8,128)S(1)}, f32[8,128,128]{2,1,0:T(8,128)S(1)}, u32[]{:S(2)}, u32[]{:S(2)}) %collective-permute-start) | collective-permute-done | bytes 524320 | tf_op jit(solution)/shard_map/while/body/eval_jaxpr/ppermute | solution.py:12
  710.0 1.9 collective-permute-start
  711.9 10.7 %collective-permute-done = f32[8,128,128]{2,1,0:T(8,128)S(1)} collective-permute-done((f32[8,128,128]{2,1,0:T(8,128)S(1)}, f32[8,128,128]{2,1,0:T(8,128)S(1)}, u32[]{:S(2)}, u32[]{:S(2)}) %collective-permute-start) | collective-permute-done | bytes 524320 | tf_op jit(solution)/shard_map/while/body/eval_jaxpr/ppermute | solution.py:12
  725.3 10.7 %collective-permute-done = f32[8,128,128]{2,1,0:T(8,128)S(1)} collective-permute-done((f32[8,128,128]{2,1,0:T(8,128)S(1)}, f32[8,128,128]{2,1,0:T(8,128)S(1)}, u32[]{:S(2)}, u32[]{:S(2)}) %collective-permute-start) | collective-permute-done | bytes 524320 | tf_op jit(solution)/shard_map/while/body/eval_jaxpr/ppermute | solution.py:12
  738.8 10.7 %collective-permute-done = f32[8,128,128]{2,1,0:T(8,128)S(1)} collective-permute-done((f32[8,128,128]{2,1,0:T(8,128)S(1)}, f32[8,128,128]{2,1,0:T(8,128)S(1)}, u32[]{:S(2)}, u32[]{:S(2)}) %collective-permute-start) | collective-permute-done | bytes 524320 | tf_op jit(solution)/shard_map/while/body/eval_jaxpr/ppermute | solution.py:12
  752.2 10.7 %collective-permute-done = f32[8,128,128]{2,1,0:T(8,128)S(1)} collective-permute-done((f32[8,128,128]{2,1,0:T(8,128)S(1)}, f32[8,128,128]{2,1,0:T(8,128)S(1)}, u32[]{:S(2)}, u32[]{:S(2)}) %collective-permute-start) | collective-permute-done | bytes 524320 | tf_op jit(solution)/shard_map/while/body/eval_jaxpr/ppermute | solution.py:12
  765.6 10.7 %collective-permute-done = f32[8,128,128]{2,1,0:T(8,128)S(1)} collective-permute-done((f32[8,128,128]{2,1,0:T(8,128)S(1)}, f32[8,128,128]{2,1,0:T(8,128)S(1)}, u32[]{:S(2)}, u32[]{:S(2)}) %collective-permute-start) | collective-permute-done | bytes 524320 | tf_op jit(solution)/shard_map/while/body/eval_jaxpr/ppermute | solution.py:12
  779.0 10.7 %collective-permute-done = f32[8,128,128]{2,1,0:T(8,128)S(1)} collective-permute-done((f32[8,128,128]{2,1,0:T(8,128)S(1)}, f32[8,128,128]{2,1,0:T(8,128)S(1)}, u32[]{:S(2)}, u32[]{:S(2)}) %collective-permute-start) | collective-permute-done | bytes 524320 | tf_op jit(solution)/shard_map/while/body/eval_jaxpr/ppermute | solution.py:12
  792.4 10.7 %collective-permute-done = f32[8,128,128]{2,1,0:T(8,128)S(1)} collective-permute-done((f32[8,128,128]{2,1,0:T(8,128)S(1)}, f32[8,128,128]{2,1,0:T(8,128)S(1)}, u32[]{:S(2)}, u32[]{:S(2)}) %collective-permute-start) | collective-permute-done | bytes 524320 | tf_op jit(solution)/shard_map/while/body/eval_jaxpr/ppermute | solution.py:12
  805.8 10.7 %collective-permute-done = f32[8,128,128]{2,1,0:T(8,128)S(1)} collective-permute-done((f32[8,128,128]{2,1,0:T(8,128)S(1)}, f32[8,128,128]{2,1,0:T(8,128)S(1)}, u32[]{:S(2)}, u32[]{:S(2)}) %collective-permute-start) | collective-permute-done | bytes 524320 | tf_op jit(solution)/shard_map/while/body/eval_jaxpr/ppermute | solution.py:12
  819.3 10.7 %collective-permute-done = f32[8,128,128]{2,1,0:T(8,128)S(1)} collective-permute-done((f32[8,128,128]{2,1,0:T(8,128)S(1)}, f32[8,128,128]{2,1,0:T(8,128)S(1)}, u32[]{:S(2)}, u32[]{:S(2)}) %collective-permute-start) | collective-permute-done | bytes 524320 | tf_op jit(solution)/shard_map/while/body/eval_jaxpr/ppermute | solution.py:12
  832.7 10.7 %collective-permute-done = f32[8,128,128]{2,1,0:T(8,128)S(1)} collective-permute-done((f32[8,128,128]{2,1,0:T(8,128)S(1)}, f32[8,128,128]{2,1,0:T(8,128)S(1)}, u32[]{:S(2)}, u32[]{:S(2)}) %collective-permute-start) | collective-permute-done | bytes 524320 | tf_op jit(solution)/shard_map/while/body/eval_jaxpr/ppermute | solution.py:12
  846.1 10.7 %collective-permute-done = f32[8,128,128]{2,1,0:T(8,128)S(1)} collective-permute-done((f32[8,128,128]{2,1,0:T(8,128)S(1)}, f32[8,128,128]{2,1,0:T(8,128)S(1)}, u32[]{:S(2)}, u32[]{:S(2)}) %collective-permute-start) | collective-permute-done | bytes 524320 | tf_op jit(solution)/shard_map/while/body/eval_jaxpr/ppermute | solution.py:12
  859.5 10.7 %collective-permute-done = f32[8,128,128]{2,1,0:T(8,128)S(1)} collective-permute-done((f32[8,128,128]{2,1,0:T(8,128)S(1)}, f32[8,128,128]{2,1,0:T(8,128)S(1)}, u32[]{:S(2)}, u32[]{:S(2)}) %collective-permute-start) | collective-permute-done | bytes 524320 | tf_op jit(solution)/shard_map/while/body/eval_jaxpr/ppermute | solution.py:12
  871.0 12.6 %multiply_reduce_fusion = (f32[16,128]{1,0:T(8,128)S(1)}, f32[16,128,8,128]{1,3,2,0:T(8,128)}) fusion(bf16[16,128,8,128]{1,3,2,0:T(8,128)(2,1)} %bitcast.75, f32[16,128,8]{1,2,0:T(8,128)S(1)} %copy.217, f32[8,128,128]{2,1,0:T(8,128)} %get-tuple-element.63, f32[16,8,128,128]{3,2,1,0:T(8,128)} %fusion.5, f32[16,8,128,128]{3,2,1,0:T(8,128)} %fusion.9), kind=kOutput, calls=%fused_computation.25 | convolution fusion | flops 551680000 | bytes 29958144 | tf_op jit(solution)/shard_map/nthd,hde->nthe/dot_general | solution.py:149
  883.6 9.3 %copy.220 = f32[16,128,8,128]{3,2,1,0:T(8,128)} copy(f32[16,128,8,128]{1,3,2,0:T(8,128)} %get-tuple-element.149) | data formatting | bytes 16777216 | tf_op jit(solution)/shard_map/add | solution.py:152
  892.9 11.8 %psum.7 = f32[2048]{0:T(1024)S(1)} all-reduce(f32[2048]{0:T(1024)S(1)} %bitcast.86), channel_id=1, replica_groups=mesh['ctx'=32,'head'=4] {'head'}, use_global_device_ids=true, to_apply=%region_17.20 | all-reduce | flops 2048 | bytes 16384 | tf_op jit(solution)/shard_map/psum | solution.py:153
  904.8 6.8 fusion.4
  (251 shorter events, 117.0 us)
Async XLA Ops:
  0.0 1.4 copy-start
  2.8 45.4 %all-to-all-start.3 = ((bf16[32,128,8]{1,2,0:T(8,128)(2,1)}), bf16[32,128,8]{1,2,0:T(8,128)(2,1)S(1)}, u32[]{:S(2)}, u32[]{:S(2)}) async-start(bf16[32,128,8]{1,2,0:T(8,128)(2,1)} %select_select_fusion.3), calls=%async_computation.3 | async-start | bytes 131072 | tf_op jit(solution)/shard_map/all_to_all | solution.py:132
  48.1 101.1 %copy-start.2 = (bf16[32,128,1024]{2,1,0:T(8,128)(2,1)S(1)}, bf16[32,128,1024]{2,1,0:T(8,128)(2,1)}, u32[]{:S(2)}) copy-start(bf16[32,128,1024]{2,1,0:T(8,128)(2,1)} %get-tuple-element.143) | copy-start | bytes 25165828
  248.8 8.4 copy-start.4
  248.8 8.6 copy-start.6
  248.8 112.0 %all-to-all-start = ((bf16[32,128,1024]{2,1,0:T(8,128)(2,1)}), bf16[32,128,1024]{2,1,0:T(8,128)(2,1)}, u32[]{:S(2)}, u32[]{:S(2)}) async-start(bf16[32,128,1024]{2,1,0:T(8,128)(2,1)} %get-tuple-element.144), calls=%async_computation | async-start | bytes 16777216 | tf_op jit(solution)/shard_map/all_to_all | solution.py:131
  455.1 12.6 %collective-permute-start = (f32[8,128,128]{2,1,0:T(8,128)S(1)}, f32[8,128,128]{2,1,0:T(8,128)S(1)}, u32[]{:S(2)}, u32[]{:S(2)}) collective-permute-start(f32[8,128,128]{2,1,0:T(8,128)S(1)} %get-tuple-element.256), channel_id=1, source_target_pairs={{0,4},{4,8},{8,12},{12,16},{16,20},{20,24},{24,28},{28,32},{32,36}... | collective-permute-start | bytes 1572872 | tf_op jit(solution)/shard_map/while/body/eval_jaxpr/ppermute | solution.py:12
  467.7 0.8 copy-start.3
  468.5 12.6 %collective-permute-start = (f32[8,128,128]{2,1,0:T(8,128)S(1)}, f32[8,128,128]{2,1,0:T(8,128)S(1)}, u32[]{:S(2)}, u32[]{:S(2)}) collective-permute-start(f32[8,128,128]{2,1,0:T(8,128)S(1)} %get-tuple-element.256), channel_id=1, source_target_pairs={{0,4},{4,8},{8,12},{12,16},{16,20},{20,24},{24,28},{28,32},{32,36}... | collective-permute-start | bytes 1572872 | tf_op jit(solution)/shard_map/while/body/eval_jaxpr/ppermute | solution.py:12
  481.1 0.8 copy-start.3
  481.9 12.6 %collective-permute-start = (f32[8,128,128]{2,1,0:T(8,128)S(1)}, f32[8,128,128]{2,1,0:T(8,128)S(1)}, u32[]{:S(2)}, u32[]{:S(2)}) collective-permute-start(f32[8,128,128]{2,1,0:T(8,128)S(1)} %get-tuple-element.256), channel_id=1, source_target_pairs={{0,4},{4,8},{8,12},{12,16},{16,20},{20,24},{24,28},{28,32},{32,36}... | collective-permute-start | bytes 1572872 | tf_op jit(solution)/shard_map/while/body/eval_jaxpr/ppermute | solution.py:12
  494.5 0.8 copy-start.3
  495.3 12.6 %collective-permute-start = (f32[8,128,128]{2,1,0:T(8,128)S(1)}, f32[8,128,128]{2,1,0:T(8,128)S(1)}, u32[]{:S(2)}, u32[]{:S(2)}) collective-permute-start(f32[8,128,128]{2,1,0:T(8,128)S(1)} %get-tuple-element.256), channel_id=1, source_target_pairs={{0,4},{4,8},{8,12},{12,16},{16,20},{20,24},{24,28},{28,32},{32,36}... | collective-permute-start | bytes 1572872 | tf_op jit(solution)/shard_map/while/body/eval_jaxpr/ppermute | solution.py:12
  507.9 0.8 copy-start.3
  508.8 12.6 %collective-permute-start = (f32[8,128,128]{2,1,0:T(8,128)S(1)}, f32[8,128,128]{2,1,0:T(8,128)S(1)}, u32[]{:S(2)}, u32[]{:S(2)}) collective-permute-start(f32[8,128,128]{2,1,0:T(8,128)S(1)} %get-tuple-element.256), channel_id=1, source_target_pairs={{0,4},{4,8},{8,12},{12,16},{16,20},{20,24},{24,28},{28,32},{32,36}... | collective-permute-start | bytes 1572872 | tf_op jit(solution)/shard_map/while/body/eval_jaxpr/ppermute | solution.py:12
  521.4 0.8 copy-start.3
  522.2 12.6 %collective-permute-start = (f32[8,128,128]{2,1,0:T(8,128)S(1)}, f32[8,128,128]{2,1,0:T(8,128)S(1)}, u32[]{:S(2)}, u32[]{:S(2)}) collective-permute-start(f32[8,128,128]{2,1,0:T(8,128)S(1)} %get-tuple-element.256), channel_id=1, source_target_pairs={{0,4},{4,8},{8,12},{12,16},{16,20},{20,24},{24,28},{28,32},{32,36}... | collective-permute-start | bytes 1572872 | tf_op jit(solution)/shard_map/while/body/eval_jaxpr/ppermute | solution.py:12
  534.8 0.8 copy-start.3
  535.6 12.6 %collective-permute-start = (f32[8,128,128]{2,1,0:T(8,128)S(1)}, f32[8,128,128]{2,1,0:T(8,128)S(1)}, u32[]{:S(2)}, u32[]{:S(2)}) collective-permute-start(f32[8,128,128]{2,1,0:T(8,128)S(1)} %get-tuple-element.256), channel_id=1, source_target_pairs={{0,4},{4,8},{8,12},{12,16},{16,20},{20,24},{24,28},{28,32},{32,36}... | collective-permute-start | bytes 1572872 | tf_op jit(solution)/shard_map/while/body/eval_jaxpr/ppermute | solution.py:12
  548.2 0.8 copy-start.3
  549.0 12.6 %collective-permute-start = (f32[8,128,128]{2,1,0:T(8,128)S(1)}, f32[8,128,128]{2,1,0:T(8,128)S(1)}, u32[]{:S(2)}, u32[]{:S(2)}) collective-permute-start(f32[8,128,128]{2,1,0:T(8,128)S(1)} %get-tuple-element.256), channel_id=1, source_target_pairs={{0,4},{4,8},{8,12},{12,16},{16,20},{20,24},{24,28},{28,32},{32,36}... | collective-permute-start | bytes 1572872 | tf_op jit(solution)/shard_map/while/body/eval_jaxpr/ppermute | solution.py:12
  561.6 0.8 copy-start.3
  562.4 12.6 %collective-permute-start = (f32[8,128,128]{2,1,0:T(8,128)S(1)}, f32[8,128,128]{2,1,0:T(8,128)S(1)}, u32[]{:S(2)}, u32[]{:S(2)}) collective-permute-start(f32[8,128,128]{2,1,0:T(8,128)S(1)} %get-tuple-element.256), channel_id=1, source_target_pairs={{0,4},{4,8},{8,12},{12,16},{16,20},{20,24},{24,28},{28,32},{32,36}... | collective-permute-start | bytes 1572872 | tf_op jit(solution)/shard_map/while/body/eval_jaxpr/ppermute | solution.py:12
  575.8 12.6 %collective-permute-start = (f32[8,128,128]{2,1,0:T(8,128)S(1)}, f32[8,128,128]{2,1,0:T(8,128)S(1)}, u32[]{:S(2)}, u32[]{:S(2)}) collective-permute-start(f32[8,128,128]{2,1,0:T(8,128)S(1)} %get-tuple-element.256), channel_id=1, source_target_pairs={{0,4},{4,8},{8,12},{12,16},{16,20},{20,24},{24,28},{28,32},{32,36}... | collective-permute-start | bytes 1572872 | tf_op jit(solution)/shard_map/while/body/eval_jaxpr/ppermute | solution.py:12
  588.4 0.8 copy-start.3
  589.3 12.6 %collective-permute-start = (f32[8,128,128]{2,1,0:T(8,128)S(1)}, f32[8,128,128]{2,1,0:T(8,128)S(1)}, u32[]{:S(2)}, u32[]{:S(2)}) collective-permute-start(f32[8,128,128]{2,1,0:T(8,128)S(1)} %get-tuple-element.256), channel_id=1, source_target_pairs={{0,4},{4,8},{8,12},{12,16},{16,20},{20,24},{24,28},{28,32},{32,36}... | collective-permute-start | bytes 1572872 | tf_op jit(solution)/shard_map/while/body/eval_jaxpr/ppermute | solution.py:12
  601.9 0.8 copy-start.3
  602.7 12.6 %collective-permute-start = (f32[8,128,128]{2,1,0:T(8,128)S(1)}, f32[8,128,128]{2,1,0:T(8,128)S(1)}, u32[]{:S(2)}, u32[]{:S(2)}) collective-permute-start(f32[8,128,128]{2,1,0:T(8,128)S(1)} %get-tuple-element.256), channel_id=1, source_target_pairs={{0,4},{4,8},{8,12},{12,16},{16,20},{20,24},{24,28},{28,32},{32,36}... | collective-permute-start | bytes 1572872 | tf_op jit(solution)/shard_map/while/body/eval_jaxpr/ppermute | solution.py:12
  615.3 0.8 copy-start.3
  616.1 12.6 %collective-permute-start = (f32[8,128,128]{2,1,0:T(8,128)S(1)}, f32[8,128,128]{2,1,0:T(8,128)S(1)}, u32[]{:S(2)}, u32[]{:S(2)}) collective-permute-start(f32[8,128,128]{2,1,0:T(8,128)S(1)} %get-tuple-element.256), channel_id=1, source_target_pairs={{0,4},{4,8},{8,12},{12,16},{16,20},{20,24},{24,28},{28,32},{32,36}... | collective-permute-start | bytes 1572872 | tf_op jit(solution)/shard_map/while/body/eval_jaxpr/ppermute | solution.py:12
  629.5 12.6 %collective-permute-start = (f32[8,128,128]{2,1,0:T(8,128)S(1)}, f32[8,128,128]{2,1,0:T(8,128)S(1)}, u32[]{:S(2)}, u32[]{:S(2)}) collective-permute-start(f32[8,128,128]{2,1,0:T(8,128)S(1)} %get-tuple-element.256), channel_id=1, source_target_pairs={{0,4},{4,8},{8,12},{12,16},{16,20},{20,24},{24,28},{28,32},{32,36}... | collective-permute-start | bytes 1572872 | tf_op jit(solution)/shard_map/while/body/eval_jaxpr/ppermute | solution.py:12
  642.1 0.8 copy-start.3
  642.9 12.6 %collective-permute-start = (f32[8,128,128]{2,1,0:T(8,128)S(1)}, f32[8,128,128]{2,1,0:T(8,128)S(1)}, u32[]{:S(2)}, u32[]{:S(2)}) collective-permute-start(f32[8,128,128]{2,1,0:T(8,128)S(1)} %get-tuple-element.256), channel_id=1, source_target_pairs={{0,4},{4,8},{8,12},{12,16},{16,20},{20,24},{24,28},{28,32},{32,36}... | collective-permute-start | bytes 1572872 | tf_op jit(solution)/shard_map/while/body/eval_jaxpr/ppermute | solution.py:12
  655.5 0.8 copy-start.3
  656.3 12.6 %collective-permute-start = (f32[8,128,128]{2,1,0:T(8,128)S(1)}, f32[8,128,128]{2,1,0:T(8,128)S(1)}, u32[]{:S(2)}, u32[]{:S(2)}) collective-permute-start(f32[8,128,128]{2,1,0:T(8,128)S(1)} %get-tuple-element.256), channel_id=1, source_target_pairs={{0,4},{4,8},{8,12},{12,16},{16,20},{20,24},{24,28},{28,32},{32,36}... | collective-permute-start | bytes 1572872 | tf_op jit(solution)/shard_map/while/body/eval_jaxpr/ppermute | solution.py:12
  668.9 0.8 copy-start.3
  669.8 12.6 %collective-permute-start = (f32[8,128,128]{2,1,0:T(8,128)S(1)}, f32[8,128,128]{2,1,0:T(8,128)S(1)}, u32[]{:S(2)}, u32[]{:S(2)}) collective-permute-start(f32[8,128,128]{2,1,0:T(8,128)S(1)} %get-tuple-element.256), channel_id=1, source_target_pairs={{0,4},{4,8},{8,12},{12,16},{16,20},{20,24},{24,28},{28,32},{32,36}... | collective-permute-start | bytes 1572872 | tf_op jit(solution)/shard_map/while/body/eval_jaxpr/ppermute | solution.py:12
  682.4 0.8 copy-start.3
  683.2 12.6 %collective-permute-start = (f32[8,128,128]{2,1,0:T(8,128)S(1)}, f32[8,128,128]{2,1,0:T(8,128)S(1)}, u32[]{:S(2)}, u32[]{:S(2)}) collective-permute-start(f32[8,128,128]{2,1,0:T(8,128)S(1)} %get-tuple-element.256), channel_id=1, source_target_pairs={{0,4},{4,8},{8,12},{12,16},{16,20},{20,24},{24,28},{28,32},{32,36}... | collective-permute-start | bytes 1572872 | tf_op jit(solution)/shard_map/while/body/eval_jaxpr/ppermute | solution.py:12
  696.6 12.6 %collective-permute-start = (f32[8,128,128]{2,1,0:T(8,128)S(1)}, f32[8,128,128]{2,1,0:T(8,128)S(1)}, u32[]{:S(2)}, u32[]{:S(2)}) collective-permute-start(f32[8,128,128]{2,1,0:T(8,128)S(1)} %get-tuple-element.256), channel_id=1, source_target_pairs={{0,4},{4,8},{8,12},{12,16},{16,20},{20,24},{24,28},{28,32},{32,36}... | collective-permute-start | bytes 1572872 | tf_op jit(solution)/shard_map/while/body/eval_jaxpr/ppermute | solution.py:12
  709.2 0.8 copy-start.3
  710.0 12.6 %collective-permute-start = (f32[8,128,128]{2,1,0:T(8,128)S(1)}, f32[8,128,128]{2,1,0:T(8,128)S(1)}, u32[]{:S(2)}, u32[]{:S(2)}) collective-permute-start(f32[8,128,128]{2,1,0:T(8,128)S(1)} %get-tuple-element.256), channel_id=1, source_target_pairs={{0,4},{4,8},{8,12},{12,16},{16,20},{20,24},{24,28},{28,32},{32,36}... | collective-permute-start | bytes 1572872 | tf_op jit(solution)/shard_map/while/body/eval_jaxpr/ppermute | solution.py:12
  722.6 0.8 copy-start.3
  723.4 12.6 %collective-permute-start = (f32[8,128,128]{2,1,0:T(8,128)S(1)}, f32[8,128,128]{2,1,0:T(8,128)S(1)}, u32[]{:S(2)}, u32[]{:S(2)}) collective-permute-start(f32[8,128,128]{2,1,0:T(8,128)S(1)} %get-tuple-element.256), channel_id=1, source_target_pairs={{0,4},{4,8},{8,12},{12,16},{16,20},{20,24},{24,28},{28,32},{32,36}... | collective-permute-start | bytes 1572872 | tf_op jit(solution)/shard_map/while/body/eval_jaxpr/ppermute | solution.py:12
  736.0 0.8 copy-start.3
  736.8 12.6 %collective-permute-start = (f32[8,128,128]{2,1,0:T(8,128)S(1)}, f32[8,128,128]{2,1,0:T(8,128)S(1)}, u32[]{:S(2)}, u32[]{:S(2)}) collective-permute-start(f32[8,128,128]{2,1,0:T(8,128)S(1)} %get-tuple-element.256), channel_id=1, source_target_pairs={{0,4},{4,8},{8,12},{12,16},{16,20},{20,24},{24,28},{28,32},{32,36}... | collective-permute-start | bytes 1572872 | tf_op jit(solution)/shard_map/while/body/eval_jaxpr/ppermute | solution.py:12
  749.4 0.8 copy-start.3
  750.3 12.6 %collective-permute-start = (f32[8,128,128]{2,1,0:T(8,128)S(1)}, f32[8,128,128]{2,1,0:T(8,128)S(1)}, u32[]{:S(2)}, u32[]{:S(2)}) collective-permute-start(f32[8,128,128]{2,1,0:T(8,128)S(1)} %get-tuple-element.256), channel_id=1, source_target_pairs={{0,4},{4,8},{8,12},{12,16},{16,20},{20,24},{24,28},{28,32},{32,36}... | collective-permute-start | bytes 1572872 | tf_op jit(solution)/shard_map/while/body/eval_jaxpr/ppermute | solution.py:12
  763.7 12.6 %collective-permute-start = (f32[8,128,128]{2,1,0:T(8,128)S(1)}, f32[8,128,128]{2,1,0:T(8,128)S(1)}, u32[]{:S(2)}, u32[]{:S(2)}) collective-permute-start(f32[8,128,128]{2,1,0:T(8,128)S(1)} %get-tuple-element.256), channel_id=1, source_target_pairs={{0,4},{4,8},{8,12},{12,16},{16,20},{20,24},{24,28},{28,32},{32,36}... | collective-permute-start | bytes 1572872 | tf_op jit(solution)/shard_map/while/body/eval_jaxpr/ppermute | solution.py:12
  776.3 0.8 copy-start.3
  777.1 12.6 %collective-permute-start = (f32[8,128,128]{2,1,0:T(8,128)S(1)}, f32[8,128,128]{2,1,0:T(8,128)S(1)}, u32[]{:S(2)}, u32[]{:S(2)}) collective-permute-start(f32[8,128,128]{2,1,0:T(8,128)S(1)} %get-tuple-element.256), channel_id=1, source_target_pairs={{0,4},{4,8},{8,12},{12,16},{16,20},{20,24},{24,28},{28,32},{32,36}... | collective-permute-start | bytes 1572872 | tf_op jit(solution)/shard_map/while/body/eval_jaxpr/ppermute | solution.py:12
  789.7 0.8 copy-start.3
  790.5 12.6 %collective-permute-start = (f32[8,128,128]{2,1,0:T(8,128)S(1)}, f32[8,128,128]{2,1,0:T(8,128)S(1)}, u32[]{:S(2)}, u32[]{:S(2)}) collective-permute-start(f32[8,128,128]{2,1,0:T(8,128)S(1)} %get-tuple-element.256), channel_id=1, source_target_pairs={{0,4},{4,8},{8,12},{12,16},{16,20},{20,24},{24,28},{28,32},{32,36}... | collective-permute-start | bytes 1572872 | tf_op jit(solution)/shard_map/while/body/eval_jaxpr/ppermute | solution.py:12
  803.1 0.8 copy-start.3
  803.9 12.6 %collective-permute-start = (f32[8,128,128]{2,1,0:T(8,128)S(1)}, f32[8,128,128]{2,1,0:T(8,128)S(1)}, u32[]{:S(2)}, u32[]{:S(2)}) collective-permute-start(f32[8,128,128]{2,1,0:T(8,128)S(1)} %get-tuple-element.256), channel_id=1, source_target_pairs={{0,4},{4,8},{8,12},{12,16},{16,20},{20,24},{24,28},{28,32},{32,36}... | collective-permute-start | bytes 1572872 | tf_op jit(solution)/shard_map/while/body/eval_jaxpr/ppermute | solution.py:12
  817.3 12.6 %collective-permute-start = (f32[8,128,128]{2,1,0:T(8,128)S(1)}, f32[8,128,128]{2,1,0:T(8,128)S(1)}, u32[]{:S(2)}, u32[]{:S(2)}) collective-permute-start(f32[8,128,128]{2,1,0:T(8,128)S(1)} %get-tuple-element.256), channel_id=1, source_target_pairs={{0,4},{4,8},{8,12},{12,16},{16,20},{20,24},{24,28},{28,32},{32,36}... | collective-permute-start | bytes 1572872 | tf_op jit(solution)/shard_map/while/body/eval_jaxpr/ppermute | solution.py:12
  830.8 12.6 %collective-permute-start = (f32[8,128,128]{2,1,0:T(8,128)S(1)}, f32[8,128,128]{2,1,0:T(8,128)S(1)}, u32[]{:S(2)}, u32[]{:S(2)}) collective-permute-start(f32[8,128,128]{2,1,0:T(8,128)S(1)} %get-tuple-element.256), channel_id=1, source_target_pairs={{0,4},{4,8},{8,12},{12,16},{16,20},{20,24},{24,28},{28,32},{32,36}... | collective-permute-start | bytes 1572872 | tf_op jit(solution)/shard_map/while/body/eval_jaxpr/ppermute | solution.py:12
  843.4 0.8 copy-start.3
  844.2 12.6 %collective-permute-start = (f32[8,128,128]{2,1,0:T(8,128)S(1)}, f32[8,128,128]{2,1,0:T(8,128)S(1)}, u32[]{:S(2)}, u32[]{:S(2)}) collective-permute-start(f32[8,128,128]{2,1,0:T(8,128)S(1)} %get-tuple-element.256), channel_id=1, source_target_pairs={{0,4},{4,8},{8,12},{12,16},{16,20},{20,24},{24,28},{28,32},{32,36}... | collective-permute-start | bytes 1572872 | tf_op jit(solution)/shard_map/while/body/eval_jaxpr/ppermute | solution.py:12
  856.8 0.8 copy-start.3
  857.6 12.6 %collective-permute-start = (f32[8,128,128]{2,1,0:T(8,128)S(1)}, f32[8,128,128]{2,1,0:T(8,128)S(1)}, u32[]{:S(2)}, u32[]{:S(2)}) collective-permute-start(f32[8,128,128]{2,1,0:T(8,128)S(1)} %get-tuple-element.256), channel_id=1, source_target_pairs={{0,4},{4,8},{8,12},{12,16},{16,20},{20,24},{24,28},{28,32},{32,36}... | collective-permute-start | bytes 1572872 | tf_op jit(solution)/shard_map/while/body/eval_jaxpr/ppermute | solution.py:12
  870.2 0.8 copy-start.3
  883.6 21.2 %copy-start.5 = (f32[1024]{0:T(1024)S(1)}, f32[1024]{0:T(1024)}, u32[]{:S(2)}) copy-start(f32[1024]{0:T(1024)} %param.19) | copy-start | bytes 12292
  904.8 6.8 copy-start.1
  (6 other events, 4.9 us)
where the time goes:
time: 914 us; the launch traced here: 912 us
  waiting for transfers between devices  386 us (42%)
  blocking collectives  213 us (23%)
  local copies, waits for them, and re-layouts  97.8 us (11%)
  other arithmetic  97.4 us (11%)
  starting transfers between devices  74.8 us (8%)
  matrix products  41.7 us (5%)
    ppermute x31, waiting for transfers between devices, from_behind(): return lax.ppermute(x, axis, pairs)  331 us
    all_to_all x1, blocking collectives, body(): lax.all_to_all(outgoing(key_rows), 'ctx', split_axis=0, concat_axis=0, ti...  101 us
    all_to_all x1, blocking collectives, body(): lax.all_to_all(outgoing(queries), 'ctx', split_axis=0, concat_axis=0, til...  99.6 us
    ppermute x31, starting transfers between devices, from_behind(): return lax.ppermute(x, axis, pairs)  59.2 us
    all_to_all x1, waiting for transfers between devices, body(): lax.all_to_all(outgoing(value_rows), 'ctx', split_axis=0, concat_axis=0,...  54.6 us
    another operation x1, other arithmetic, state_pass(): block_log = jnp.cumsum(decay_blocks.astype(jnp.float32), axis=1)  23.3 us
    gather x4, local copies, waits for them, and re-layouts, outgoing(): picked = jnp.take(values.reshape(blocks, BLOCK, columns), source, axis=0)  22 us
    while x62, local copies, waits for them, and re-layouts  21.6 us
  transfers between devices with their start and end apart: 33, of which 32 were waited for; matrix products, arithmetic and copies ran while one was open for 9% of the time, Pallas kernels for 0%

commit v1 on v0

v1 whole, which is shorter than its diff:
```python
import jax
import jax.numpy as jnp
from jax import lax
from jax.experimental import pallas as pl
from jax.experimental.pallas import tpu as pltpu
from jax.sharding import PartitionSpec as P

BLOCK = 128
CHUNKS = 2
FAR = 1e9
F32 = jnp.float32
BF16 = jnp.bfloat16


def dot(a, b, contract):
    return lax.dot_general(a, b, ((contract[:1], contract[1:]), ((), ())), preferred_element_type=F32)


def triangle(upper):
    row = lax.broadcasted_iota(jnp.int32, (BLOCK, BLOCK), 0)
    column = lax.broadcasted_iota(jnp.int32, (BLOCK, BLOCK), 1)
    keep = row <= column if upper else column <= row
    return jnp.where(keep, 1.0, 0.0).astype(BF16)


def log_rows(decay):
    return dot(decay, triangle(True), (0, 0))


def log_columns(decay):
    return dot(triangle(False), decay, (1, 0))


def last_starts(starts, base):
    at = lax.broadcasted_iota(jnp.int32, (BLOCK, BLOCK), 0).astype(F32) + base
    begun = jnp.broadcast_to(starts, (BLOCK, BLOCK))
    return jnp.max(jnp.where(begun <= at, begun, -FAR), axis=1, keepdims=True)


def own_kernel(heads, chunk, packing, place, starts, keys, values, decay, *outs):
    block = pl.program_id(0)
    base = (packing[place[0] * pl.num_programs(0) + block] * BLOCK).astype(F32)
    logs = log_rows(decay[...])
    total = logs[:, BLOCK - 1 :]
    started = last_starts(starts[...], base)[BLOCK - 1 :, :]
    at = lax.broadcasted_iota(jnp.int32, (1, BLOCK), 1).astype(F32) + base
    keep = jnp.exp(total - logs) * jnp.where(at >= started, 1.0, 0.0)
    pieces = outs[0].shape[2]
    per_head = BLOCK // pieces
    for head in range(heads):
        span = slice(head * BLOCK, (head + 1) * BLOCK)
        wide = chunk * heads + head
        faded = keys[:, span].T.astype(F32) * keep[wide : wide + 1, :]
        own = dot(faded.astype(BF16), values[:, span], (1, 0)).astype(BF16)
        outs[0][head * per_head : (head + 1) * per_head, 0] = own.reshape(per_head, pieces, BLOCK)
    if len(outs) > 1:
        gate = jnp.exp(total) * jnp.where(started < base, 1.0, 0.0)
        lane = lax.broadcasted_iota(jnp.int32, outs[1].shape, 1)

        @pl.when(block == 0)
        def _():
            outs[1][...] = jnp.zeros(outs[1].shape, F32)

        outs[1][...] = jnp.where(lane == block, gate, outs[1][...])


def own_states(chunk, packing, place, starts, keys, values, decay):
    rows, width = keys.shape
    all_heads = decay.shape[1]
    blocks = rows // BLOCK
    heads = all_heads // CHUNKS
    columns = width // CHUNKS
    devices = packing.shape[0] // blocks
    pieces = heads * BLOCK // devices
    outs = [jax.ShapeDtypeStruct((devices, blocks, pieces, BLOCK), BF16)]
    specs = [pl.BlockSpec((devices, 1, pieces, BLOCK), lambda b, *_: (0, b, 0, 0))]
    if chunk == 0:
        outs.append(jax.ShapeDtypeStruct((all_heads, BLOCK), F32))
        specs.append(pl.BlockSpec((all_heads, BLOCK), lambda b, *_: (0, 0)))
    return pl.pallas_call(
        lambda *refs: own_kernel(heads, chunk, *refs),
        grid_spec=pltpu.PrefetchScalarGridSpec(
            num_scalar_prefetch=2,
            grid=(blocks,),
            in_specs=[
                pl.BlockSpec((1, BLOCK), lambda b, *_: (0, 0)),
                pl.BlockSpec((BLOCK, columns), lambda b, *_: (b, chunk)),
                pl.BlockSpec((BLOCK, columns), lambda b, *_: (b, chunk)),
                pl.BlockSpec((BLOCK, all_heads), lambda b, *_: (b, 0)),
            ],
            out_specs=specs,
        ),
        out_shape=outs,
        name=f"own{chunk}",
    )(packing, place, starts, keys, values, decay)


def intra_kernel(heads, packing, place, starts, queries, keys, values, decay, intra, faded):
    block = pl.program_id(0)
    base = (packing[place[0] * pl.num_programs(0) + block] * BLOCK).astype(F32)
    along = log_rows(decay[...])
    down = log_columns(decay[...])
    started = last_starts(starts[...], base)
    row = lax.broadcasted_iota(jnp.int32, (BLOCK, BLOCK), 0)
    column = lax.broadcasted_iota(jnp.int32, (BLOCK, BLOCK), 1)
    allowed = (column <= row) & (column.astype(F32) + base >= started)
    reach = jnp.exp(down) * jnp.where(started < base, 1.0, 0.0)
    for head in range(heads):
        span = slice(head * BLOCK, (head + 1) * BLOCK)
        query = queries[:, span]
        scores = dot(query, keys[:, span], (1, 1))
        gaps = jnp.minimum(down[:, head : head + 1] - along[head : head + 1, :], 0.0)
        weights = (scores * jnp.where(allowed, jnp.exp(gaps), 0.0)).astype(BF16)
        intra[:, span] = dot(weights, values[:, span], (1, 0))
        faded[:, span] = (query.astype(F32) * reach[:, head : head + 1]).astype(BF16)


def intra_pass(packing, place, starts, queries, keys, values, decay):
    rows, width = queries.shape
    heads = decay.shape[1]
    row_block = pl.BlockSpec((BLOCK, width), lambda b, *_: (b, 0))
    return pl.pallas_call(
        lambda *refs: intra_kernel(heads, *refs),
        grid_spec=pltpu.PrefetchScalarGridSpec(
            num_scalar_prefetch=2,
            grid=(rows // BLOCK,),
            in_specs=[
                pl.BlockSpec((1, BLOCK), lambda b, *_: (0, 0)),
                row_block,
                row_block,
                row_block,
                pl.BlockSpec((BLOCK, heads), lambda b, *_: (b, 0)),
            ],
            out_specs=[row_block, row_block],
        ),
        out_shape=[
            jax.ShapeDtypeStruct((rows, width), F32),
            jax.ShapeDtypeStruct((rows, width), BF16),
        ],
        name="intra",
    )(packing, place, starts, queries, keys, values, decay)


def scan_kernel(order, gates, own, prior):
    def step(j, state):
        at = order[j]
        prior[at] = state.astype(BF16)
        return gates[at] * state + own[at].astype(F32)

    lax.fori_loop(0, own.shape[0], step, jnp.zeros(own.shape[1:], F32), unroll=8)


def scan_pass(order, gates, own, name):
    devices, blocks, pieces, lanes = own.shape
    flat = own.reshape(devices * blocks, pieces, lanes)
    smem = pl.BlockSpec(memory_space=pltpu.SMEM)
    vmem = pl.BlockSpec(memory_space=pltpu.VMEM)
    prior = pl.pallas_call(
        scan_kernel,
        in_specs=[smem, smem, vmem],
        out_specs=vmem,
        out_shape=jax.ShapeDtypeStruct(flat.shape, BF16),
        name=name,
    )(order, gates, flat)
    return prior.reshape(own.shape)


def outgo_kernel(heads, packing, place, faded, intra, states, *refs):
    slots, squares = refs[-2:]
    sums = jnp.zeros((BLOCK, BLOCK), F32)
    per_head = states.shape[0] // heads
    for head in range(heads):
        span = slice(head * BLOCK, (head + 1) * BLOCK)
        state = states[head * per_head : (head + 1) * per_head, 0].reshape(BLOCK, BLOCK)
        out = intra[:, span] + dot(faded[:, span], state, (1, 0))
        sums = sums + out * out
        slots[0, :, span] = out.astype(BF16)
    mine = jnp.broadcast_to(jnp.sum(sums.T, axis=0, keepdims=True), squares.shape[1:])
    squares[0] = mine if len(refs) == 2 else mine + refs[0][0]


def outgo_pass(chunk, packing, place, faded, intra, states, earlier):
    rows, width = faded.shape
    blocks = rows // BLOCK
    devices, _, pieces, lanes = states.shape
    columns = width // CHUNKS
    heads = columns // BLOCK

    def owner(b, packing, place):
        return packing[place[0] * blocks + b] // blocks, 0, 0

    square_block = pl.BlockSpec((1, 8, BLOCK), owner)
    ins = [packing, place, faded, intra, states] + ([] if earlier is None else [earlier])
    return pl.pallas_call(
        lambda *refs: outgo_kernel(heads, *refs),
        grid_spec=pltpu.PrefetchScalarGridSpec(
            num_scalar_prefetch=2,
            grid=(blocks,),
            in_specs=[
                pl.BlockSpec((BLOCK, columns), lambda b, *_: (b, chunk)),
                pl.BlockSpec((BLOCK, columns), lambda b, *_: (b, chunk)),
                pl.BlockSpec((devices, 1, pieces, lanes), lambda b, *_: (0, b, 0, 0)),
            ]
            + ([] if earlier is None else [square_block]),
            out_specs=[pl.BlockSpec((1, BLOCK, columns), owner), square_block],
        ),
        out_shape=[
            jax.ShapeDtypeStruct((devices, BLOCK, columns), BF16),
            jax.ShapeDtypeStruct((devices, 8, BLOCK), F32),
        ],
        name=f"outgo{chunk}",
    )(*ins)


def finish_kernel(width_all, order, place, squares, gain, *refs):
    mixed = refs[-1]
    total = squares[0, 0, :1, :]
    for group in range(1, squares.shape[0]):
        total = total + squares[group, 0, :1, :]
    scale = lax.rsqrt(total / width_all + 1e-05)
    scale = jnp.broadcast_to(scale, (BLOCK, BLOCK)).T
    at = 0
    for part in refs[:-1]:
        for inside in range(part.shape[2] // BLOCK):
            span = slice(inside * BLOCK, (inside + 1) * BLOCK)
            wide = slice(at, at + BLOCK)
            out = part[0, :, span].astype(F32) * scale * gain[:, wide]
            mixed[:, wide] = out.astype(BF16)
            at += BLOCK


def finish_pass(order, place, squares, gain, parts, width_all):
    devices, _, columns = parts[0].shape
    blocks = order.shape[0] // devices
    width = gain.shape[1]

    def loader(b, order, place):
        return order[place[0] * blocks + b] // blocks

    return pl.pallas_call(
        lambda *refs: finish_kernel(width_all, *refs),
        grid_spec=pltpu.PrefetchScalarGridSpec(
            num_scalar_prefetch=2,
            grid=(blocks,),
            in_specs=[
                pl.BlockSpec(
                    (squares.shape[0], 1, 8, BLOCK), lambda b, *s: (0, loader(b, *s), 0, 0)
                ),
                pl.BlockSpec((1, width), lambda b, *_: (0, 0)),
            ]
            + [pl.BlockSpec((1, BLOCK, columns), lambda b, *s: (loader(b, *s), 0, 0))] * len(parts),
            out_specs=pl.BlockSpec((BLOCK, width), lambda b, *_: (b, 0)),
        ),
        out_shape=jax.ShapeDtypeStruct((blocks * BLOCK, width), BF16),
        name="finish",
    )(order, place, squares, gain, *parts)


def swap(x, axis):
    return lax.all_to_all(x, axis, split_axis=0, concat_axis=0, tiled=True)


def body(queries, key_rows, value_rows, log_decay, norm_gain, doc_lengths, packing):
    rows, width = queries.shape
    heads = log_decay.shape[1]
    blocks = rows // BLOCK
    devices = lax.axis_size("ctx")
    mine = lax.axis_index("ctx").astype(jnp.int32)
    place = mine.reshape(1)
    starts = (jnp.cumsum(doc_lengths) - doc_lengths).astype(F32)
    starts = jnp.pad(starts, (0, BLOCK - starts.shape[0]), constant_values=FAR)[None, :]

    own, gates = [], None
    for chunk in range(CHUNKS):
        made = own_states(chunk, packing, place, starts, key_rows, value_rows, log_decay)
        if chunk == 0:
            gates = swap(jnp.broadcast_to(made[1][None], (devices, heads, BLOCK)), "ctx")
        own.append(swap(made[0], "ctx"))
    intra, faded = intra_pass(packing, place, starts, queries, key_rows, value_rows, log_decay)

    total_blocks = packing.shape[0]
    index = jnp.arange(total_blocks, dtype=jnp.int32)
    hit = (packing[None, :] == index[:, None]).astype(jnp.int32)
    order = jnp.sum(hit * index[None, :], axis=1)

    per_head = devices * CHUNKS // heads
    states = []
    for chunk in range(CHUNKS):
        head = chunk * (heads // CHUNKS) + mine // per_head
        gate = lax.dynamic_index_in_dim(gates, head, 1, keepdims=False)[:, :blocks].reshape(-1)
        states.append(swap(scan_pass(order, gate, own[chunk], f"scan{chunk}"), "ctx"))

    parts, squares = [], None
    for chunk in range(CHUNKS):
        slots, squares = outgo_pass(chunk, packing, place, faded, intra, states[chunk], squares)
        parts.append(swap(slots, "ctx"))
    squares = swap(squares, "ctx")
    groups = lax.axis_size("head")
    squares = swap(jnp.broadcast_to(squares[None], (groups,) + squares.shape), "head")
    return finish_pass(order, place, squares, norm_gain[None, :], parts, width * groups)


def solution(mesh):
    placed = (
        P("ctx", "head"),
        P("ctx", "head"),
        P("ctx", "head"),
        P("ctx", "head"),
        P("head"),
        P(),
        P(),
    )
    return jax.shard_map(
        body, mesh=mesh, in_specs=placed, out_specs=P("ctx", "head"), check_vma=False
    )
```

time: 914 us -> 353 us (0.39)
  waiting for transfers between devices: 386 us -> 58.4 us
  Pallas kernels: 0 us -> 102 us
  other arithmetic: 97.4 us -> 1.6 us
  local copies, waits for them, and re-layouts: 97.8 us -> 7.87 us
  blocking collectives: 213 us -> 152 us
  starting transfers between devices: 74.8 us -> 26 us
  matrix products: 41.7 us -> 0 us
    ppermute x31 -> x0, waiting for transfers between devices: 331 us -> none  [from_behind(): return lax.ppermute(x, axis, pairs)]
    pallas_call x0 -> x8, Pallas kernels: none -> 102 us  [the longest x2 28.2 us: own_states(): pl.pallas_call(lambda *refs: own_kernel(heads, chunk, *refs), grid_spec=p...]
    ppermute x31 -> x0, starting transfers between devices: 59.2 us -> none  [from_behind(): return lax.ppermute(x, axis, pairs)]
    all_to_all x2 -> x5, blocking collectives: 201 us -> 152 us  [swap(): return lax.all_to_all(x, axis, split_axis=0, concat_axis=0, tiled=True)]
    gather x10 -> x0, local copies, waits for them, and re-layouts: 41.8 us -> none  [the longest x4 22 us: outgoing(): picked = jnp.take(values.reshape(blocks, BLOCK, columns), source, axis=0)]
    dot_general x4 -> x0, matrix products: 41.7 us -> none  [the longest x1 12.6 us: body(): jnp.einsum('nthd,hde->nthe', scaled, arrival.astype(jnp.bfloat16), prefer...]
    select_n x8 -> x0, other arithmetic: 27.2 us -> none  [the longest x2 17.3 us: outgoing(): kept = jnp.where(filled[:, None, None], picked, jnp.zeros((), values.dtype))]
    another operation x8 -> x2, other arithmetic: 23.8 us -> 0.2 us  [the longest x1 23.3 us: state_pass(): block_log = jnp.cumsum(decay_blocks.astype(jnp.float32), axis=1)]
  transfers between devices with their start and end apart: 33 -> 4, of which waited for: 32 -> 3; matrix products, arithmetic and copies ran while one was open for 9% -> 1% of each run, Pallas kernels for 0% -> 18%
where the time goes in v1:
time: 353 us; the launch traced here: 347 us
  blocking collectives  152 us (43%)
  Pallas kernels  102 us (29%)
  waiting for transfers between devices  58.4 us (17%)
  starting transfers between devices  26 us (7%)
  local copies, waits for them, and re-layouts  7.87 us (2%)
    all_to_all x5, blocking collectives, swap(): return lax.all_to_all(x, axis, split_axis=0, concat_axis=0, tiled=True)  152 us
    all_to_all x4, waiting for transfers between devices, swap(): return lax.all_to_all(x, axis, split_axis=0, concat_axis=0, tiled=True)  58.4 us
    pallas_call x2, Pallas kernels, own_states(): pl.pallas_call(lambda *refs: own_kernel(heads, chunk, *refs), grid_spec=p...  28.2 us
    pallas_call x1, Pallas kernels, intra_pass(): pl.pallas_call(lambda *refs: intra_kernel(heads, *refs), grid_spec=pltpu....  27 us
    all_to_all x4, starting transfers between devices, swap(): return lax.all_to_all(x, axis, split_axis=0, concat_axis=0, tiled=True)  26 us
    pallas_call x2, Pallas kernels, outgo_pass(): pl.pallas_call(lambda *refs: outgo_kernel(heads, *refs), grid_spec=pltpu....  25.8 us
    pallas_call x1, Pallas kernels, finish_pass(): pl.pallas_call(lambda *refs: finish_kernel(width_all, *refs), grid_spec=p...  12.1 us
    pallas_call x2, Pallas kernels, scan_pass(): pl.pallas_call(scan_kernel, in_specs=[smem, smem, vmem], out_specs=vmem,...  8.64 us
  transfers between devices with their start and end apart: 4, of which 3 were waited for; matrix products, arithmetic and copies ran while one was open for 1% of the time, Pallas kernels for 18%

profile of v1, /device:TPU:16, one launch (start us, length us, event | category | flops | bytes accessed | tf_op | source)
XLA Modules:
  0.0 347.4 jit_solution(15479367237301649786)
XLA Ops:
  0.0 0.7 copy.20
  0.7 0.1 reduce-window.9
  0.8 0.1 reduce
  0.9 0.7 subtract_convert_fusion
  1.6 0.6 pad_bitcast_fusion.refs_2_
  2.2 1.8 copy.21.refs_6_.refs_5_
  4.0 14.3 %own0.1 = (bf16[32,16,16,128]{3,2,1,0:T(8,128)(2,1)}, f32[8,128]{1,0:T(8,128)}) custom-call(s32[512]{0:T(512)} %refs_0_.9, s32[1]{0:T(128)} %bitcast.refs_1_, f32[1,128]{1,0:T(1,128)} %pad_bitcast_fusion.refs_2_, bf16[2048,1024]{1,0:T(8,128)(2,1)} %refs_3_.5, bf16[2048,1024]{1,0:T(8,128)(2,1)} %refs_4_.5, bf16[2048,8]{1,0:T(8,128)(2,1)} %copy.21.refs_6_.refs_5_), custom_call_target="tpu_custom_call" | custom-call | tf_op jit(solution)/shard_map/own0/pallas_call | solution.py:80
  18.3 0.7 broadcast_in_dim.9
  19.0 12.9 %all_to_all.45 = f32[32,8,128]{2,1,0:T(8,128)S(1)} all-to-all(f32[32,8,128]{2,1,0:T(8,128)S(1)} %broadcast_in_dim.9), channel_id=1, replica_groups=mesh['ctx'=32,'head'=4] {'ctx'}, dimensions={0} | all-to-all | bytes 262144 | tf_op jit(solution)/shard_map/all_to_all | solution.py:260
  31.9 6.1 %all-to-all-start.3 = ((bf16[32,16,16,128]{3,2,1,0:T(8,128)(2,1)}), bf16[32,16,16,128]{3,2,1,0:T(8,128)(2,1)S(1)}, u32[]{:S(2)}, u32[]{:S(2)}) async-start(bf16[32,16,16,128]{3,2,1,0:T(8,128)(2,1)} %get-tuple-element.16), calls=%async_computation.3 | async-start | bytes 4194304 | tf_op jit(solution)/shard_map/all_to_all | solution.py:260
  38.0 13.9 %own1.1 = bf16[32,16,16,128]{3,2,1,0:T(8,128)(2,1)} custom-call(s32[512]{0:T(512)} %refs_0_.9, s32[1]{0:T(128)} %bitcast.refs_1_, f32[1,128]{1,0:T(1,128)} %pad_bitcast_fusion.refs_2_, bf16[2048,1024]{1,0:T(8,128)(2,1)} %refs_3_.5, bf16[2048,1024]{1,0:T(8,128)(2,1)} %refs_4_.5, bf16[2048,8]{1,0:T(8,128)(2,1)} %copy.21.refs_6_.refs_5_), custom_call_target="tpu_custom_call" | custom-call | tf_op jit(solution)/shard_map/own1/pallas_call | solution.py:80
  51.9 0.0 copy-start.4
  51.9 13.8 %all-to-all-done.3 = bf16[32,16,16,128]{3,2,1,0:T(8,128)(2,1)S(1)} async-done(((bf16[32,16,16,128]{3,2,1,0:T(8,128)(2,1)}), bf16[32,16,16,128]{3,2,1,0:T(8,128)(2,1)S(1)}, u32[]{:S(2)}, u32[]{:S(2)}) %all-to-all-start.3) | async-done | bytes 2097184 | tf_op jit(solution)/shard_map/all_to_all | solution.py:260
  65.7 0.0 copy-start.2
  65.7 1.3 copy-done.2
  67.0 6.4 %all-to-all-start.1 = ((bf16[32,16,16,128]{3,2,1,0:T(8,128)(2,1)}), bf16[32,16,16,128]{3,2,1,0:T(8,128)(2,1)S(1)}, u32[]{:S(2)}, u32[]{:S(2)}) async-start(bf16[32,16,16,128]{3,2,1,0:T(8,128)(2,1)} %own1.1), calls=%async_computation.1 | async-start | bytes 4194304 | tf_op jit(solution)/shard_map/all_to_all | solution.py:260
  73.5 0.0 copy-done.4
  73.5 0.7 select_reduce_fusion.order.refs_0_
  74.2 0.7 reshape.56.gates
  74.9 4.3 %scan0.1 = bf16[512,16,128]{2,1,0:T(8,128)(2,1)} custom-call(s32[512]{0:T(512)} %select_reduce_fusion.order.refs_0_, f32[512]{0:T(512)} %reshape.56.gates, bf16[512,16,128]{2,1,0:T(8,128)(2,1)} %bitcast.14), custom_call_target="tpu_custom_call" | custom-call | tf_op jit(solution)/shard_map/scan0/pallas_call | solution.py:158
  79.2 21.9 %all-to-all-done.1 = bf16[32,16,16,128]{3,2,1,0:T(8,128)(2,1)S(1)} async-done(((bf16[32,16,16,128]{3,2,1,0:T(8,128)(2,1)}), bf16[32,16,16,128]{3,2,1,0:T(8,128)(2,1)S(1)}, u32[]{:S(2)}, u32[]{:S(2)}) %all-to-all-start.1) | async-done | bytes 2097184 | tf_op jit(solution)/shard_map/all_to_all | solution.py:260
  101.1 0.0 copy-start.1
  101.1 1.3 copy-done.1
  102.5 6.4 %all-to-all-start.4 = ((bf16[32,16,16,128]{3,2,1,0:T(8,128)(2,1)}), bf16[32,16,16,128]{3,2,1,0:T(8,128)(2,1)S(1)}, u32[]{:S(2)}, u32[]{:S(2)}) async-start(bf16[32,16,16,128]{3,2,1,0:T(8,128)(2,1)} %bitcast.16), calls=%async_computation.4 | async-start | bytes 4194304 | tf_op jit(solution)/shard_map/all_to_all | solution.py:260
  108.9 0.7 reshape.53.gates
  109.5 4.3 %scan1.1 = bf16[512,16,128]{2,1,0:T(8,128)(2,1)} custom-call(s32[512]{0:T(512)} %select_reduce_fusion.order.refs_0_, f32[512]{0:T(512)} %reshape.53.gates, bf16[512,16,128]{2,1,0:T(8,128)(2,1)} %bitcast.13), custom_call_target="tpu_custom_call" | custom-call | tf_op jit(solution)/shard_map/scan1/pallas_call | solution.py:158
  113.9 22.7 %all-to-all-done.4.refs_4_ = bf16[32,16,16,128]{3,2,1,0:T(8,128)(2,1)S(1)} async-done(((bf16[32,16,16,128]{3,2,1,0:T(8,128)(2,1)}), bf16[32,16,16,128]{3,2,1,0:T(8,128)(2,1)S(1)}, u32[]{:S(2)}, u32[]{:S(2)}) %all-to-all-start.4) | async-done | bytes 2097184 | tf_op jit(solution)/shard_map/all_to_all | solution.py:260
  136.6 0.0 copy-start
  136.6 7.1 %all-to-all-start.2 = ((bf16[32,16,16,128]{3,2,1,0:T(8,128)(2,1)}), bf16[32,16,16,128]{3,2,1,0:T(8,128)(2,1)}, u32[]{:S(2)}, u32[]{:S(2)}) async-start(bf16[32,16,16,128]{3,2,1,0:T(8,128)(2,1)} %bitcast.15), calls=%async_computation.2 | async-start | bytes 4194304 | tf_op jit(solution)/shard_map/all_to_all | solution.py:260
  143.7 27.0 %intra.1 = (f32[2048,1024]{1,0:T(8,128)}, bf16[2048,1024]{1,0:T(8,128)(2,1)}) custom-call(s32[512]{0:T(512)} %refs_0_.9, s32[1]{0:T(128)} %bitcast.refs_1_, f32[1,128]{1,0:T(1,128)} %pad_bitcast_fusion.refs_2_, bf16[2048,1024]{1,0:T(8,128)(2,1)} %refs_3_.3, bf16[2048,1024]{1,0:T(8,128)(2,1)} %refs_3_.5, bf16[2048,1024]{1,0:T(8,128)(2,1)} %refs_4_.5, ...), custom_call_target="tpu_custom_call" | custom-call | tf_op jit(solution)/shard_map/intra/pallas_call | solution.py:122
  170.7 0.0 copy-done
  170.7 12.9 %outgo0.1 = (bf16[32,128,512]{2,1,0:T(8,128)(2,1)}, f32[32,8,128]{2,1,0:T(8,128)}) custom-call(s32[512]{0:T(512)} %refs_0_.9, s32[1]{0:T(128)} %bitcast.refs_1_, bf16[2048,1024]{1,0:T(8,128)(2,1)} %get-tuple-element.13.refs_2_, f32[2048,1024]{1,0:T(8,128)} %get-tuple-element.14.refs_3_, bf16[32,16,16,128]{3,2,1,0:T(8,128)(2,1)} %copy-done), custom_call_target="tpu_custom_call" | custom-call | tf_op jit(solution)/shard_map/outgo0/pallas_call | solution.py:194
  183.6 0.0 all-to-all-done.2.refs_4_
  183.6 13.0 %outgo1.1 = (bf16[32,128,512]{2,1,0:T(8,128)(2,1)}, f32[32,8,128]{2,1,0:T(8,128)}) custom-call(s32[512]{0:T(512)} %refs_0_.9, s32[1]{0:T(128)} %bitcast.refs_1_, bf16[2048,1024]{1,0:T(8,128)(2,1)} %get-tuple-element.13.refs_2_, f32[2048,1024]{1,0:T(8,128)} %get-tuple-element.14.refs_3_, bf16[32,16,16,128]{3,2,1,0:T(8,128)(2,1)} %all-to-all-done.2.refs_4_, ...), custom_call_target="tpu_custom_call" | custom-call | tf_op jit(solution)/shard_map/outgo1/pallas_call | solution.py:194
  196.5 13.1 %all_to_all.46 = f32[32,8,128]{2,1,0:T(8,128)S(1)} all-to-all(f32[32,8,128]{2,1,0:T(8,128)} %get-tuple-element.18), channel_id=1, replica_groups=mesh['ctx'=32,'head'=4] {'ctx'}, dimensions={0} | all-to-all | bytes 262144 | tf_op jit(solution)/shard_map/all_to_all | solution.py:260
  209.7 15.0 %all_to_all.47.refs_2_ = f32[4,32,8,128]{3,2,1,0:T(8,128)} all-to-all(f32[4,32,8,128]{3,2,1,0:T(8,128)S(1)} %broadcast_in_dim.10), channel_id=1, replica_groups=mesh['ctx'=32,'head'=4] {'head'}, dimensions={0} | all-to-all | bytes 1048576 | tf_op jit(solution)/shard_map/all_to_all | solution.py:260
  224.7 0.0 copy-start.3
  224.7 55.4 %all_to_all.48.refs_5_ = bf16[32,128,512]{2,1,0:T(8,128)(2,1)} all-to-all(bf16[32,128,512]{2,1,0:T(8,128)(2,1)} %get-tuple-element.20), channel_id=1, replica_groups=mesh['ctx'=32,'head'=4] {'ctx'}, dimensions={0} | all-to-all | bytes 8388608 | tf_op jit(solution)/shard_map/all_to_all | solution.py:260
  280.1 0.0 copy-done.3
  280.1 55.2 %all_to_all.49.refs_4_ = bf16[32,128,512]{2,1,0:T(8,128)(2,1)} all-to-all(bf16[32,128,512]{2,1,0:T(8,128)(2,1)S(1)} %copy-done.3), channel_id=1, replica_groups=mesh['ctx'=32,'head'=4] {'ctx'}, dimensions={0} | all-to-all | bytes 8388608 | tf_op jit(solution)/shard_map/all_to_all | solution.py:260
  335.4 12.1 %finish.1 = bf16[2048,1024]{1,0:T(8,128)(2,1)} custom-call(s32[512]{0:T(512)} %select_reduce_fusion.order.refs_0_, s32[1]{0:T(128)} %bitcast.refs_1_, f32[4,32,8,128]{3,2,1,0:T(8,128)} %all_to_all.47.refs_2_, f32[1,1024]{1,0:T(1,128)} %bitcast.19, bf16[32,128,512]{2,1,0:T(8,128)(2,1)} %all_to_all.49.refs_4_, bf16[32,128,512]{2,1,0:T(8,128)(2,1)} %all_to_all.48.refs_5_), custom_call_target="tpu_custom_call" | custom-call | tf_op jit(solution)/shard_map/finish/pallas_call | solution.py:240
  (2 shorter events, 0.1 us)
Async XLA Ops:
  31.9 33.8 %all-to-all-start.3 = ((bf16[32,16,16,128]{3,2,1,0:T(8,128)(2,1)}), bf16[32,16,16,128]{3,2,1,0:T(8,128)(2,1)S(1)}, u32[]{:S(2)}, u32[]{:S(2)}) async-start(bf16[32,16,16,128]{3,2,1,0:T(8,128)(2,1)} %get-tuple-element.16), calls=%async_computation.3 | async-start | bytes 4194304 | tf_op jit(solution)/shard_map/all_to_all | solution.py:260
  51.9 21.6 %copy-start.4 = (s32[512]{0:T(512)S(1)}, s32[512]{0:T(512)}, u32[]{:S(2)}) copy-start(s32[512]{0:T(512)} %refs_0_.9) | copy-start | bytes 6148
  65.7 1.3 copy-start.2
  67.0 34.1 %all-to-all-start.1 = ((bf16[32,16,16,128]{3,2,1,0:T(8,128)(2,1)}), bf16[32,16,16,128]{3,2,1,0:T(8,128)(2,1)S(1)}, u32[]{:S(2)}, u32[]{:S(2)}) async-start(bf16[32,16,16,128]{3,2,1,0:T(8,128)(2,1)} %own1.1), calls=%async_computation.1 | async-start | bytes 4194304 | tf_op jit(solution)/shard_map/all_to_all | solution.py:260
  101.1 1.3 copy-start.1
  102.5 34.1 %all-to-all-start.4 = ((bf16[32,16,16,128]{3,2,1,0:T(8,128)(2,1)}), bf16[32,16,16,128]{3,2,1,0:T(8,128)(2,1)S(1)}, u32[]{:S(2)}, u32[]{:S(2)}) async-start(bf16[32,16,16,128]{3,2,1,0:T(8,128)(2,1)} %bitcast.16), calls=%async_computation.4 | async-start | bytes 4194304 | tf_op jit(solution)/shard_map/all_to_all | solution.py:260
  136.6 34.1 %copy-start = (bf16[32,16,16,128]{3,2,1,0:T(8,128)(2,1)}, bf16[32,16,16,128]{3,2,1,0:T(8,128)(2,1)S(1)}, u32[]{:S(2)}) copy-start(bf16[32,16,16,128]{3,2,1,0:T(8,128)(2,1)S(1)} %all-to-all-done.4.refs_4_) | copy-start | bytes 6291460
  136.6 47.0 %all-to-all-start.2 = ((bf16[32,16,16,128]{3,2,1,0:T(8,128)(2,1)}), bf16[32,16,16,128]{3,2,1,0:T(8,128)(2,1)}, u32[]{:S(2)}, u32[]{:S(2)}) async-start(bf16[32,16,16,128]{3,2,1,0:T(8,128)(2,1)} %bitcast.15), calls=%async_computation.2 | async-start | bytes 4194304 | tf_op jit(solution)/shard_map/all_to_all | solution.py:260
  224.7 55.4 %copy-start.3 = (bf16[32,128,512]{2,1,0:T(8,128)(2,1)S(1)}, bf16[32,128,512]{2,1,0:T(8,128)(2,1)}, u32[]{:S(2)}) copy-start(bf16[32,128,512]{2,1,0:T(8,128)(2,1)} %get-tuple-element.19) | copy-start | bytes 12582916

commit v2 on v1

v2 whole, which is shorter than its diff:
```python
import jax
import jax.numpy as jnp
from jax import lax
from jax.experimental import pallas as pl
from jax.experimental.pallas import tpu as pltpu
from jax.sharding import PartitionSpec as P

BLOCK = 128
EXTRA = 16
FAR = 1e9
F32 = jnp.float32
BF16 = jnp.bfloat16


def dot(a, b, contract):
    return lax.dot_general(a, b, ((contract[:1], contract[1:]), ((), ())), preferred_element_type=F32)


def triangle(upper):
    row = lax.broadcasted_iota(jnp.int32, (BLOCK, BLOCK), 0)
    column = lax.broadcasted_iota(jnp.int32, (BLOCK, BLOCK), 1)
    keep = row <= column if upper else column <= row
    return jnp.where(keep, 1.0, 0.0).astype(BF16)


def in_three(x):
    high = x.astype(BF16).astype(F32)
    middle = (x - high).astype(BF16).astype(F32)
    return high, middle, x - high - middle


def own_kernel(heads, blocks, each, packing, place, starts, keys, values, decay, own, made, fates, sems):
    step = pl.program_id(0)
    per_head = made.shape[0] // heads
    pieces = BLOCK // per_head
    steps = blocks // each
    upper = triangle(True)
    lane = lax.broadcasted_iota(jnp.int32, (1, BLOCK), 1).astype(F32)
    for inside in range(each):
        block = step * each + inside
        rows = slice(inside * BLOCK, (inside + 1) * BLOCK)
        base = (packing[place[0] * blocks + block] * BLOCK).astype(F32)
        logs = dot(decay[:, rows], upper, (1, 0))
        total = logs[:, BLOCK - 1 :]
        begun = jnp.where(starts[...] <= base + (BLOCK - 1), starts[...], -FAR)
        started = jnp.max(begun, axis=1, keepdims=True)
        keep = jnp.exp(total - logs) * jnp.where(lane + base >= started, 1.0, 0.0)
        gate = jnp.exp(total) * jnp.where(started < base, 1.0, 0.0)
        to = pl.ds(pl.multiple_of(block * pieces, pieces), pieces)
        for head in range(heads):
            span = slice(head * BLOCK, (head + 1) * BLOCK)
            faded = keys[rows, span].T.astype(F32) * keep[head : head + 1, :]
            state = dot(faded.astype(BF16), values[rows, span], (1, 0)).astype(BF16)
            made[head * per_head : (head + 1) * per_head, to] = state.reshape(per_head, pieces, BLOCK)
            fates[head, pl.ds(block, 1), :] = jnp.broadcast_to(gate[head : head + 1, :], (1, BLOCK))

    def copy(at, start, size):
        part = (slice(None), pl.ds(start, size))
        return pltpu.make_async_copy(made.at[part], own.at[part], sems.at[at])

    span = each * pieces
    copy(step, pl.multiple_of(step * span, span), span).start()

    @pl.when(step == steps - 1)
    def _():
        at = lax.broadcasted_iota(jnp.int32, (EXTRA, BLOCK), 1)
        for head in range(heads):
            high, middle, low = in_three(fates[head])
            tile = jnp.where(at == 0, high, jnp.where(at == 1, middle, low)).astype(BF16)
            for piece in range(per_head):
                made[head * per_head + piece, blocks * pieces :] = tile
        copy(steps, blocks * pieces, EXTRA).start()
        for earlier in range(steps):
            copy(earlier, earlier * span, span).wait()
        copy(steps, blocks * pieces, EXTRA).wait()


def own_states(packing, place, starts, keys, values, decay):
    rows, width = keys.shape
    heads = decay.shape[0]
    blocks = rows // BLOCK
    each = 4
    devices = packing.shape[0] // blocks
    pieces = heads * BLOCK // devices
    shape = (devices, blocks * pieces + EXTRA, BLOCK)
    row_block = pl.BlockSpec((each * BLOCK, width), lambda b, *_: (b, 0))
    return pl.pallas_call(
        lambda *refs: own_kernel(heads, blocks, each, *refs),
        grid_spec=pltpu.PrefetchScalarGridSpec(
            num_scalar_prefetch=2,
            grid=(blocks // each,),
            in_specs=[
                pl.BlockSpec((1, BLOCK), lambda b, *_: (0, 0)),
                row_block,
                row_block,
                pl.BlockSpec((heads, each * BLOCK), lambda b, *_: (0, b)),
            ],
            out_specs=pl.BlockSpec(memory_space=pl.ANY),
            scratch_shapes=[
                pltpu.VMEM(shape, BF16),
                pltpu.VMEM((heads, blocks, BLOCK), F32),
                pltpu.SemaphoreType.DMA((blocks // each + 1,)),
            ],
        ),
        out_shape=jax.ShapeDtypeStruct(shape, BF16),
        name="own",
    )(packing, place, starts, keys, values, decay)


def intra_kernel(heads, packing, place, starts, queries, keys, values, decay, intra, faded):
    block = pl.program_id(0)
    base = (packing[place[0] * pl.num_programs(0) + block] * BLOCK).astype(F32)
    along = dot(decay[...], triangle(True), (1, 0))
    down = dot(triangle(False), decay[...], (1, 1))
    row = lax.broadcasted_iota(jnp.int32, (BLOCK, BLOCK), 0)
    column = lax.broadcasted_iota(jnp.int32, (BLOCK, BLOCK), 1)
    begun = jnp.broadcast_to(starts[...], (BLOCK, BLOCK))
    begun = jnp.where(begun <= row.astype(F32) + base, begun, -FAR)
    started = jnp.max(begun, axis=1, keepdims=True)
    allowed = (column <= row) & (column.astype(F32) + base >= started)
    reach = jnp.exp(down) * jnp.where(started < base, 1.0, 0.0)
    for head in range(heads):
        span = slice(head * BLOCK, (head + 1) * BLOCK)
        query = queries[:, span]
        scores = dot(query, keys[:, span], (1, 1))
        gaps = jnp.minimum(down[:, head : head + 1] - along[head : head + 1, :], 0.0)
        weights = (scores * jnp.where(allowed, jnp.exp(gaps), 0.0)).astype(BF16)
        intra[:, span] = dot(weights, values[:, span], (1, 0))
        faded[:, span] = (query.astype(F32) * reach[:, head : head + 1]).astype(BF16)


def intra_pass(packing, place, starts, queries, keys, values, decay):
    rows, width = queries.shape
    heads = decay.shape[0]
    row_block = pl.BlockSpec((BLOCK, width), lambda b, *_: (b, 0))
    return pl.pallas_call(
        lambda *refs: intra_kernel(heads, *refs),
        grid_spec=pltpu.PrefetchScalarGridSpec(
            num_scalar_prefetch=2,
            grid=(rows // BLOCK,),
            in_specs=[
                pl.BlockSpec((1, BLOCK), lambda b, *_: (0, 0)),
                row_block,
                row_block,
                row_block,
                pl.BlockSpec((heads, BLOCK), lambda b, *_: (0, b)),
            ],
            out_specs=[row_block, row_block],
        ),
        out_shape=[
            jax.ShapeDtypeStruct((rows, width), F32),
            jax.ShapeDtypeStruct((rows, width), BF16),
        ],
        name="intra",
    )(packing, place, starts, queries, keys, values, decay)


def scan_kernel(blocks, order, own, prior, gates):
    devices, height, _ = prior.shape
    pieces = height // blocks
    for device in range(devices):
        tile = own[device, height:, :].astype(F32)
        gate = tile[:, 0:1] + tile[:, 1:2] + tile[:, 2:3]
        gates[device] = jnp.broadcast_to(gate[:blocks], (blocks, BLOCK))

    def step(j, state):
        at = order[j]
        device, block = at // blocks, at % blocks
        rows = pl.ds(pl.multiple_of(block * pieces, pieces), pieces)
        prior[device, rows, :] = state.astype(BF16)
        return gates[device, pl.ds(block, 1), :] * state + own[device, rows, :].astype(F32)

    lax.fori_loop(0, devices * blocks, step, jnp.zeros((pieces, BLOCK), F32), unroll=8)


def scan_pass(order, own):
    devices, height, lanes = own.shape
    blocks = order.shape[0] // devices
    vmem = pl.BlockSpec(memory_space=pltpu.VMEM)
    return pl.pallas_call(
        lambda *refs: scan_kernel(blocks, *refs),
        in_specs=[pl.BlockSpec(memory_space=pltpu.SMEM), vmem],
        out_specs=vmem,
        out_shape=jax.ShapeDtypeStruct((devices, height - EXTRA, lanes), BF16),
        scratch_shapes=[pltpu.VMEM((devices, blocks, BLOCK), F32)],
        name="scan",
    )(order, own)


def outgo_kernel(heads, blocks, each, packing, place, faded, intra, states, slots, made, sems):
    step = pl.program_id(0)
    per_head = states.shape[0] // heads
    pieces = BLOCK // per_head
    row = lax.broadcasted_iota(jnp.int32, (EXTRA, BLOCK), 0)

    def copy(block):
        owner = packing[place[0] * blocks + block] // blocks
        return pltpu.make_async_copy(made.at[block], slots.at[owner], sems.at[block])

    for inside in range(each):
        block = step * each + inside
        rows = slice(inside * BLOCK, (inside + 1) * BLOCK)
        sums = jnp.zeros((BLOCK, BLOCK), F32)
        for head in range(heads):
            span = slice(head * BLOCK, (head + 1) * BLOCK)
            state = states[
                head * per_head : (head + 1) * per_head, inside * pieces : (inside + 1) * pieces
            ].reshape(BLOCK, BLOCK)
            out = intra[rows, span] + dot(faded[rows, span], state, (1, 0))
            sums = sums + out * out
            made[block, span, :] = out.astype(BF16)
        high, middle, low = in_three(jnp.sum(sums.T, axis=0, keepdims=True))
        tile = jnp.where(row == 0, high, jnp.where(row == 1, middle, low))
        made[block, heads * BLOCK :, :] = tile.astype(BF16)
        copy(block).start()

    @pl.when(step == pl.num_programs(0) - 1)
    def _():
        for block in range(blocks):
            copy(block).wait()


def outgo_pass(packing, place, faded, intra, states):
    rows, width = faded.shape
    blocks = rows // BLOCK
    devices, height, lanes = states.shape
    each = 2
    heads = width // BLOCK
    row_block = pl.BlockSpec((each * BLOCK, width), lambda b, *_: (b, 0))
    return pl.pallas_call(
        lambda *refs: outgo_kernel(heads, blocks, each, *refs),
        grid_spec=pltpu.PrefetchScalarGridSpec(
            num_scalar_prefetch=2,
            grid=(blocks // each,),
            in_specs=[
                row_block,
                row_block,
                pl.BlockSpec((devices, height // blocks * each, lanes), lambda b, *_: (0, b, 0)),
            ],
            out_specs=pl.BlockSpec(memory_space=pl.ANY),
            scratch_shapes=[
                pltpu.VMEM((blocks, width + EXTRA, BLOCK), BF16),
                pltpu.SemaphoreType.DMA((blocks,)),
            ],
        ),
        out_shape=jax.ShapeDtypeStruct((devices, width + EXTRA, BLOCK), BF16),
        name="outgo",
    )(packing, place, faded, intra, states)


def squares_kernel(order, place, came, squares, tiles, sems):
    blocks, extra, _ = tiles.shape
    height = came.shape[1] - extra

    def copy(block):
        loader = order[place[0] * blocks + block] // blocks
        return pltpu.make_async_copy(came.at[loader, height:], tiles.at[block], sems.at[block])

    for block in range(blocks):
        copy(block).start()
    for block in range(blocks):
        copy(block).wait()
        tile = tiles[block].astype(F32)
        squares[block : block + 1, :] = tile[0:1, :] + tile[1:2, :] + tile[2:3, :]


def squares_pass(order, place, came):
    blocks = order.shape[0] // came.shape[0]
    smem = pl.BlockSpec(memory_space=pltpu.SMEM)
    return pl.pallas_call(
        squares_kernel,
        in_specs=[smem, smem, pl.BlockSpec(memory_space=pl.ANY)],
        out_specs=pl.BlockSpec(memory_space=pltpu.VMEM),
        out_shape=jax.ShapeDtypeStruct((blocks, BLOCK), F32),
        scratch_shapes=[
            pltpu.VMEM((blocks, EXTRA, BLOCK), BF16),
            pltpu.SemaphoreType.DMA((blocks,)),
        ],
        name="squares",
    )(order, place, came)


def finish_kernel(groups, each, order, place, *refs):
    squares, gain, parts, mixed = refs[:groups], refs[groups], refs[groups + 1 : -1], refs[-1]
    width = gain.shape[1]
    for inside in range(each):
        block = pl.ds(pl.program_id(0) * each + inside, 1)
        total = squares[0][block, :]
        for other in squares[1:]:
            total = total + other[block, :]
        scale = lax.rsqrt(total / (width * groups) + 1e-05)
        scale = jnp.broadcast_to(scale, (BLOCK, BLOCK)).T
        rows = slice(inside * BLOCK, (inside + 1) * BLOCK)
        for head in range(width // BLOCK):
            span = slice(head * BLOCK, (head + 1) * BLOCK)
            out = parts[inside][0, span, :].astype(F32) * scale * gain[:, span]
            mixed[rows, span] = out.astype(BF16)


def finish_pass(order, place, squares, gain, came):
    devices, height, lanes = came.shape
    blocks = order.shape[0] // devices
    width = gain.shape[1]
    each = 4

    def part(inside):
        def loader(b, order, place):
            return order[place[0] * blocks + b * each + inside] // blocks, 0, 0

        return pl.BlockSpec((1, width, lanes), loader)

    return pl.pallas_call(
        lambda *refs: finish_kernel(len(squares), each, *refs),
        grid_spec=pltpu.PrefetchScalarGridSpec(
            num_scalar_prefetch=2,
            grid=(blocks // each,),
            in_specs=[pl.BlockSpec((blocks, BLOCK), lambda b, *_: (0, 0))] * len(squares)
            + [pl.BlockSpec((1, width), lambda b, *_: (0, 0))]
            + [part(inside) for inside in range(each)],
            out_specs=pl.BlockSpec((each * BLOCK, width), lambda b, *_: (b, 0)),
        ),
        out_shape=jax.ShapeDtypeStruct((blocks * BLOCK, width), BF16),
        name="finish",
    )(order, place, *squares, gain, *[came] * each)


def swap(x, axis):
    return lax.all_to_all(x, axis, split_axis=0, concat_axis=0, tiled=True)


def body(queries, key_rows, value_rows, log_decay, norm_gain, doc_lengths, packing):
    mine = lax.axis_index("ctx").astype(jnp.int32)
    place = mine.reshape(1)
    decay = log_decay.T
    document = jnp.arange(doc_lengths.shape[0], dtype=jnp.int32)
    ahead = document[:, None] < jnp.arange(BLOCK, dtype=jnp.int32)[None, :]
    starts = jnp.sum(jnp.where(ahead, doc_lengths[:, None], 0), axis=0, keepdims=True).astype(F32)

    own = swap(own_states(packing, place, starts, key_rows, value_rows, decay), "ctx")
    intra, faded = intra_pass(packing, place, starts, queries, key_rows, value_rows, decay)

    index = jnp.arange(packing.shape[0], dtype=jnp.int32)
    hit = (packing[None, :] == index[:, None]).astype(jnp.int32)
    order = jnp.sum(hit * index[None, :], axis=1)

    states = swap(scan_pass(order, own), "ctx")
    came = swap(outgo_pass(packing, place, faded, intra, states), "ctx")
    part = squares_pass(order, place, came)
    groups = lax.axis_size("head")
    squares = [part]
    for shift in range(1, groups):
        pairs = [(i, (i + shift) % groups) for i in range(groups)]
        squares.append(lax.ppermute(part, "head", pairs))
    return finish_pass(order, place, squares, norm_gain[None, :], came)


def solution(mesh):
    placed = (
        P("ctx", "head"),
        P("ctx", "head"),
        P("ctx", "head"),
        P("ctx", "head"),
        P("head"),
        P(),
        P(),
    )
    return jax.shard_map(
        body, mesh=mesh, in_specs=placed, out_specs=P("ctx", "head"), check_vma=False
    )
```

time: 353 us -> 275 us (0.78)
  blocking collectives: 152 us -> 103 us
  Pallas kernels: 102 us -> 65.1 us
  waiting for transfers between devices: 58.4 us -> 81.5 us
  local copies, waits for them, and re-layouts: 7.87 us -> 0.61 us
  starting transfers between devices: 26 us -> 20.1 us
    all_to_all x5 -> x1, blocking collectives: 152 us -> 103 us  [swap(): return lax.all_to_all(x, axis, split_axis=0, concat_axis=0, tiled=True)]
    pallas_call x7 -> x5, Pallas kernels: 74.7 us -> 38.8 us  [the longest x1 11.2 us: outgo_pass(): pl.pallas_call(lambda *refs: outgo_kernel(heads, blocks, each, *refs), gr...]
    all_to_all x4 -> x2, waiting for transfers between devices: 58.4 us -> 77.4 us  [swap(): return lax.all_to_all(x, axis, split_axis=0, concat_axis=0, tiled=True)]
    all_to_all x4 -> x2, starting transfers between devices: 26 us -> 14.8 us  [swap(): return lax.all_to_all(x, axis, split_axis=0, concat_axis=0, tiled=True)]
    ppermute x0 -> x3, starting transfers between devices: none -> 5.37 us  [body(): squares.append(lax.ppermute(part, 'head', pairs))]
    ppermute x0 -> x3, waiting for transfers between devices: none -> 4.1 us  [body(): squares.append(lax.ppermute(part, 'head', pairs))]
    unnamed x11 -> x8, local copies, waits for them, and re-layouts: 4.46 us -> 0.61 us
  transfers between devices with their start and end apart: 4 -> 5, of which waited for: 3 -> 4; matrix products, arithmetic and copies ran while one was open for 1% -> 0% of each run, Pallas kernels for 18% -> 10%
where the time goes in v2:
time: 275 us; the launch traced here: 273 us
  blocking collectives  103 us (37%)
  waiting for transfers between devices  81.5 us (30%)
  Pallas kernels  65.1 us (24%)
  starting transfers between devices  20.1 us (7%)
    all_to_all x1, blocking collectives, swap(): return lax.all_to_all(x, axis, split_axis=0, concat_axis=0, tiled=True)  103 us
    all_to_all x2, waiting for transfers between devices, swap(): return lax.all_to_all(x, axis, split_axis=0, concat_axis=0, tiled=True)  77.4 us
    pallas_call x1, Pallas kernels, intra_pass(): pl.pallas_call(lambda *refs: intra_kernel(heads, *refs), grid_spec=pltpu....  26.4 us
    all_to_all x2, starting transfers between devices, swap(): return lax.all_to_all(x, axis, split_axis=0, concat_axis=0, tiled=True)  14.8 us
    pallas_call x1, Pallas kernels, outgo_pass(): pl.pallas_call(lambda *refs: outgo_kernel(heads, blocks, each, *refs), gr...  11.2 us
    pallas_call x1, Pallas kernels, scan_pass(): pl.pallas_call(lambda *refs: scan_kernel(blocks, *refs), in_specs=[pl.Blo...  9.82 us
    pallas_call x1, Pallas kernels, own_states(): pl.pallas_call(lambda *refs: own_kernel(heads, blocks, each, *refs), grid...  9.47 us
    pallas_call x1, Pallas kernels, finish_pass(): pl.pallas_call(lambda *refs: finish_kernel(len(squares), each, *refs), gr...  6.08 us
  transfers between devices with their start and end apart: 5, of which 4 were waited for; matrix products, arithmetic and copies ran while one was open for 0% of the time, Pallas kernels for 10%

profile of v2, /device:TPU:16, one launch (start us, length us, event | category | flops | bytes accessed | tf_op | source)
XLA Modules:
  0.0 272.6 jit_solution(5670094068307824012)
XLA Ops:
  0.0 0.7 select_reduce_fusion.1
  0.7 0.6 convert_bitcast_fusion.refs_2_
  1.3 9.5 %own.1 = bf16[32,528,128]{2,1,0:T(8,128)(2,1)} custom-call(s32[512]{0:T(512)} %refs_0_.5, s32[1]{0:T(128)} %bitcast.refs_1_.place, f32[1,128]{1,0:T(1,128)} %convert_bitcast_fusion.refs_2_, bf16[2048,1024]{1,0:T(8,128)(2,1)} %refs_3_.3, bf16[2048,1024]{1,0:T(8,128)(2,1)} %refs_4_.3, bf16[8,2048]{1,0:T(8,128)(2,1)} %bitcast.5), custom_call_target="tpu_custom_call" | custom-call | tf_op jit(solution)/shard_map/own/pallas_call | solution.py:87
  10.8 0.0 copy-start
  10.8 7.5 %all-to-all-start = ((bf16[32,528,128]{2,1,0:T(8,128)(2,1)}), bf16[32,528,128]{2,1,0:T(8,128)(2,1)}, u32[]{:S(2)}, u32[]{:S(2)}) async-start(bf16[32,528,128]{2,1,0:T(8,128)(2,1)} %own.1), calls=%async_computation | async-start | bytes 8650752 | tf_op jit(solution)/shard_map/all_to_all | solution.py:328
  18.3 0.0 copy-done
  18.3 0.8 select_reduce_fusion.refs_0_.order
  19.1 52.2 %all-to-all-done.refs_1_ = bf16[32,528,128]{2,1,0:T(8,128)(2,1)} async-done(((bf16[32,528,128]{2,1,0:T(8,128)(2,1)}), bf16[32,528,128]{2,1,0:T(8,128)(2,1)}, u32[]{:S(2)}, u32[]{:S(2)}) %all-to-all-start) | async-done | bytes 4325408 | tf_op jit(solution)/shard_map/all_to_all | solution.py:328
  71.3 9.8 %scan.1 = bf16[32,512,128]{2,1,0:T(8,128)(2,1)} custom-call(s32[512]{0:T(512)} %select_reduce_fusion.refs_0_.order, bf16[32,528,128]{2,1,0:T(8,128)(2,1)} %all-to-all-done.refs_1_), custom_call_target="tpu_custom_call" | custom-call | tf_op jit(solution)/shard_map/scan/pallas_call | solution.py:180
  81.2 7.3 %all-to-all-start.1 = ((bf16[32,512,128]{2,1,0:T(8,128)(2,1)}), bf16[32,512,128]{2,1,0:T(8,128)(2,1)}, u32[]{:S(2)}, u32[]{:S(2)}) async-start(bf16[32,512,128]{2,1,0:T(8,128)(2,1)} %scan.1), calls=%async_computation.1 | async-start | bytes 8388608 | tf_op jit(solution)/shard_map/all_to_all | solution.py:328
  88.4 26.4 %intra.1 = (f32[2048,1024]{1,0:T(8,128)}, bf16[2048,1024]{1,0:T(8,128)(2,1)}) custom-call(s32[512]{0:T(512)} %refs_0_.5, s32[1]{0:T(128)} %bitcast.refs_1_.place, f32[1,128]{1,0:T(1,128)} %convert_bitcast_fusion.refs_2_, bf16[2048,1024]{1,0:T(8,128)(2,1)} %refs_3_.2, bf16[2048,1024]{1,0:T(8,128)(2,1)} %refs_3_.3, bf16[2048,1024]{1,0:T(8,128)(2,1)} %refs_4_.3, ...), custom_call_target="tpu_custom_call" | custom-call | tf_op jit(solution)/shard_map/intra/pallas_call | solution.py:136
  114.8 25.1 %all-to-all-done.1.refs_4_ = bf16[32,512,128]{2,1,0:T(8,128)(2,1)} async-done(((bf16[32,512,128]{2,1,0:T(8,128)(2,1)}), bf16[32,512,128]{2,1,0:T(8,128)(2,1)}, u32[]{:S(2)}, u32[]{:S(2)}) %all-to-all-start.1) | async-done | bytes 4194336 | tf_op jit(solution)/shard_map/all_to_all | solution.py:328
  139.9 11.2 %outgo.1 = bf16[32,1040,128]{2,1,0:T(8,128)(2,1)} custom-call(s32[512]{0:T(512)} %refs_0_.5, s32[1]{0:T(128)} %bitcast.refs_1_.place, bf16[2048,1024]{1,0:T(8,128)(2,1)} %get-tuple-element.7.refs_2_, f32[2048,1024]{1,0:T(8,128)} %get-tuple-element.8.refs_3_, bf16[32,512,128]{2,1,0:T(8,128)(2,1)} %all-to-all-done.1.refs_4_), custom_call_target="tpu_custom_call" | custom-call | tf_op jit(solution)/shard_map/outgo/pallas_call | solution.py:230
  151.1 103.1 %all_to_all.15.came.refs_7_.refs_8_.refs_9_.refs_10_ = bf16[32,1040,128]{2,1,0:T(8,128)(2,1)} all-to-all(bf16[32,1040,128]{2,1,0:T(8,128)(2,1)} %outgo.1), channel_id=1, replica_groups=mesh['ctx'=32,'head'=4] {'ctx'}, dimensions={0} | all-to-all | bytes 17039360 | tf_op jit(solution)/shard_map/all_to_all | solution.py:328
  254.2 2.2 squares.1.refs_2_
  256.4 4.1 %collective-permute-start.2 = (f32[16,128]{1,0:T(8,128)}, f32[16,128]{1,0:T(8,128)S(1)}, u32[]{:S(2)}, u32[]{:S(2)}) collective-permute-start(f32[16,128]{1,0:T(8,128)} %squares.1.refs_2_), channel_id=1, source_target_pairs={{0,3},{1,0},{2,1},{3,2},{4,7},{5,4},{6,5},{7,6},{8,11},{9,8},{10,9... | collective-permute-start | bytes 24584 | tf_op jit(solution)/shard_map/ppermute | solution.py:353
  260.5 0.0 collective-permute-start.1
  260.5 1.3 collective-permute-start
  261.8 0.3 collective-permute-done.2.refs_5_
  262.1 0.0 copy-start.1
  262.1 3.8 %collective-permute-done.1.refs_4_ = f32[16,128]{1,0:T(8,128)S(1)} collective-permute-done((f32[16,128]{1,0:T(8,128)}, f32[16,128]{1,0:T(8,128)S(1)}, u32[]{:S(2)}, u32[]{:S(2)}) %collective-permute-start.1) | collective-permute-done | bytes 8224 | tf_op jit(solution)/shard_map/ppermute | solution.py:353
  265.9 0.0 copy-start.2
  265.9 0.0 collective-permute-done.refs_3_
  265.9 0.0 copy-start.3
  265.9 0.0 copy-done.1
  265.9 0.6 copy-done.2
  266.5 0.0 copy-done.3
  266.5 6.1 %finish.1 = bf16[2048,1024]{1,0:T(8,128)(2,1)} custom-call(s32[512]{0:T(512)} %select_reduce_fusion.refs_0_.order, s32[1]{0:T(128)} %bitcast.refs_1_.place, f32[16,128]{1,0:T(8,128)} %squares.1.refs_2_, f32[16,128]{1,0:T(8,128)} %copy-done.3, f32[16,128]{1,0:T(8,128)} %copy-done.2, f32[16,128]{1,0:T(8,128)} %copy-done.1, f32[1,1024]{1,0:T(1,128)} %bitcast.7, ...), custom_call_target="tpu_custom_call" | custom-call | tf_op jit(solution)/shard_map/finish/pallas_call | solution.py:312
Async XLA Ops:
  10.8 7.5 %copy-start = (s32[512]{0:T(512)S(1)}, s32[512]{0:T(512)}, u32[]{:S(2)}) copy-start(s32[512]{0:T(512)} %refs_0_.5) | copy-start | bytes 6148
  10.8 60.5 %all-to-all-start = ((bf16[32,528,128]{2,1,0:T(8,128)(2,1)}), bf16[32,528,128]{2,1,0:T(8,128)(2,1)}, u32[]{:S(2)}, u32[]{:S(2)}) async-start(bf16[32,528,128]{2,1,0:T(8,128)(2,1)} %own.1), calls=%async_computation | async-start | bytes 8650752 | tf_op jit(solution)/shard_map/all_to_all | solution.py:328
  81.2 58.8 %all-to-all-start.1 = ((bf16[32,512,128]{2,1,0:T(8,128)(2,1)}), bf16[32,512,128]{2,1,0:T(8,128)(2,1)}, u32[]{:S(2)}, u32[]{:S(2)}) async-start(bf16[32,512,128]{2,1,0:T(8,128)(2,1)} %scan.1), calls=%async_computation.1 | async-start | bytes 8388608 | tf_op jit(solution)/shard_map/all_to_all | solution.py:328
  256.4 5.7 %collective-permute-start.2 = (f32[16,128]{1,0:T(8,128)}, f32[16,128]{1,0:T(8,128)S(1)}, u32[]{:S(2)}, u32[]{:S(2)}) collective-permute-start(f32[16,128]{1,0:T(8,128)} %squares.1.refs_2_), channel_id=1, source_target_pairs={{0,3},{1,0},{2,1},{3,2},{4,7},{5,4},{6,5},{7,6},{8,11},{9,8},{10,9... | collective-permute-start | bytes 24584 | tf_op jit(solution)/shard_map/ppermute | solution.py:353
  260.5 5.4 %collective-permute-start.1 = (f32[16,128]{1,0:T(8,128)}, f32[16,128]{1,0:T(8,128)S(1)}, u32[]{:S(2)}, u32[]{:S(2)}) collective-permute-start(f32[16,128]{1,0:T(8,128)} %squares.1.refs_2_), channel_id=1, source_target_pairs={{0,2},{1,3},{2,0},{3,1},{4,6},{5,7},{6,4},{7,5},{8,10},{9,11},{10,... | collective-permute-start | bytes 24584 | tf_op jit(solution)/shard_map/ppermute | solution.py:353
  260.5 5.4 %collective-permute-start = (f32[16,128]{1,0:T(8,128)}, f32[16,128]{1,0:T(8,128)S(1)}, u32[]{:S(2)}, u32[]{:S(2)}) collective-permute-start(f32[16,128]{1,0:T(8,128)} %squares.1.refs_2_), channel_id=1, source_target_pairs={{0,1},{1,2},{2,3},{3,0},{4,5},{5,6},{6,7},{7,4},{8,9},{9,10},{10,1... | collective-permute-start | bytes 24584 | tf_op jit(solution)/shard_map/ppermute | solution.py:353
  262.1 3.8 %copy-start.1 = (f32[16,128]{1,0:T(8,128)}, f32[16,128]{1,0:T(8,128)S(1)}, u32[]{:S(2)}) copy-start(f32[16,128]{1,0:T(8,128)S(1)} %collective-permute-done.2.refs_5_) | copy-start | bytes 24580
  265.9 0.6 copy-start.2
  265.9 0.6 copy-start.3

commit v3 on v2

--- a/solution.py
+++ b/solution.py
@@ -8,6 +8,9 @@
 BLOCK = 128
 EXTRA = 16
 FAR = 1e9
+OWN_EACH = 4
+OUTGO_EACH = 4
+FINISH_EACH = 8
 F32 = jnp.float32
 BF16 = jnp.bfloat16
 
@@ -29,12 +32,23 @@
     return high, middle, x - high - middle
 
 
-def own_kernel(heads, blocks, each, packing, place, starts, keys, values, decay, own, made, fates, sems):
+def start_row(lengths):
+    count = lengths.shape[1]
+    row = lax.broadcasted_iota(jnp.int32, (count, BLOCK), 0)
+    ahead = jnp.where(row < lax.broadcasted_iota(jnp.int32, (count, BLOCK), 1), 1.0, 0.0)
+    wide = jnp.broadcast_to(lengths.astype(F32), (8, count))
+    return lax.dot_general(
+        wide, ahead, (((1,), (0,)), ((), ())), precision=lax.Precision.HIGHEST, preferred_element_type=F32
+    )[:1]
+
+
+def own_kernel(heads, blocks, each, packing, place, lengths, keys, values, decay, own, made, fates, sems):
     step = pl.program_id(0)
     per_head = made.shape[0] // heads
     pieces = BLOCK // per_head
     steps = blocks // each
     upper = triangle(True)
+    starts = start_row(lengths[...])
     lane = lax.broadcasted_iota(jnp.int32, (1, BLOCK), 1).astype(F32)
     for inside in range(each):
         block = step * each + inside
@@ -42,7 +56,7 @@
         base = (packing[place[0] * blocks + block] * BLOCK).astype(F32)
         logs = dot(decay[:, rows], upper, (1, 0))
         total = logs[:, BLOCK - 1 :]
-        begun = jnp.where(starts[...] <= base + (BLOCK - 1), starts[...], -FAR)
+        begun = jnp.where(starts <= base + (BLOCK - 1), starts, -FAR)
         started = jnp.max(begun, axis=1, keepdims=True)
         keep = jnp.exp(total - logs) * jnp.where(lane + base >= started, 1.0, 0.0)
         gate = jnp.exp(total) * jnp.where(started < base, 1.0, 0.0)
@@ -75,11 +89,11 @@
         copy(steps, blocks * pieces, EXTRA).wait()
 
 
-def own_states(packing, place, starts, keys, values, decay):
+def own_states(packing, place, lengths, keys, values, decay):
     rows, width = keys.shape
     heads = decay.shape[0]
     blocks = rows // BLOCK
-    each = 4
+    each = OWN_EACH
     devices = packing.shape[0] // blocks
     pieces = heads * BLOCK // devices
     shape = (devices, blocks * pieces + EXTRA, BLOCK)
@@ -90,7 +104,7 @@
             num_scalar_prefetch=2,
             grid=(blocks // each,),
             in_specs=[
-                pl.BlockSpec((1, BLOCK), lambda b, *_: (0, 0)),
+                pl.BlockSpec(lengths.shape, lambda b, *_: (0, 0)),
                 row_block,
                 row_block,
                 pl.BlockSpec((heads, each * BLOCK), lambda b, *_: (0, b)),
@@ -104,17 +118,17 @@
         ),
         out_shape=jax.ShapeDtypeStruct(shape, BF16),
         name="own",
-    )(packing, place, starts, keys, values, decay)
-
-
-def intra_kernel(heads, packing, place, starts, queries, keys, values, decay, intra, faded):
+    )(packing, place, lengths, keys, values, decay)
+
+
+def intra_kernel(heads, packing, place, lengths, queries, keys, values, decay, intra, faded):
     block = pl.program_id(0)
     base = (packing[place[0] * pl.num_programs(0) + block] * BLOCK).astype(F32)
     along = dot(decay[...], triangle(True), (1, 0))
     down = dot(triangle(False), decay[...], (1, 1))
     row = lax.broadcasted_iota(jnp.int32, (BLOCK, BLOCK), 0)
     column = lax.broadcasted_iota(jnp.int32, (BLOCK, BLOCK), 1)
-    begun = jnp.broadcast_to(starts[...], (BLOCK, BLOCK))
+    begun = jnp.broadcast_to(start_row(lengths[...]), (BLOCK, BLOCK))
     begun = jnp.where(begun <= row.astype(F32) + base, begun, -FAR)
     started = jnp.max(begun, axis=1, keepdims=True)
     allowed = (column <= row) & (column.astype(F32) + base >= started)
@@ -129,7 +143,7 @@
         faded[:, span] = (query.astype(F32) * reach[:, head : head + 1]).astype(BF16)
 
 
-def intra_pass(packing, place, starts, queries, keys, values, decay):
+def intra_pass(packing, place, lengths, queries, keys, values, decay):
     rows, width = queries.shape
     heads = decay.shape[0]
     row_block = pl.BlockSpec((BLOCK, width), lambda b, *_: (b, 0))
@@ -139,7 +153,7 @@
             num_scalar_prefetch=2,
             grid=(rows // BLOCK,),
             in_specs=[
-                pl.BlockSpec((1, BLOCK), lambda b, *_: (0, 0)),
+                pl.BlockSpec(lengths.shape, lambda b, *_: (0, 0)),
                 row_block,
                 row_block,
                 row_block,
@@ -152,39 +166,46 @@
             jax.ShapeDtypeStruct((rows, width), BF16),
         ],
         name="intra",
-    )(packing, place, starts, queries, keys, values, decay)
-
-
-def scan_kernel(blocks, order, own, prior, gates):
-    devices, height, _ = prior.shape
-    pieces = height // blocks
+    )(packing, place, lengths, queries, keys, values, decay)
+
+
+def scan_kernel(devices, blocks, order, own, prior, gates):
+    each = own.shape[0] // devices
+    parts = (each - 1) // blocks
     for device in range(devices):
-        tile = own[device, height:, :].astype(F32)
+        tile = own[(device + 1) * each - 1].astype(F32)
         gate = tile[:, 0:1] + tile[:, 1:2] + tile[:, 2:3]
-        gates[device] = jnp.broadcast_to(gate[:blocks], (blocks, BLOCK))
+        gates[device * blocks : (device + 1) * blocks, :] = jnp.broadcast_to(gate[:blocks], (blocks, BLOCK))
 
     def step(j, state):
         at = order[j]
-        device, block = at // blocks, at % blocks
-        rows = pl.ds(pl.multiple_of(block * pieces, pieces), pieces)
-        prior[device, rows, :] = state.astype(BF16)
-        return gates[device, pl.ds(block, 1), :] * state + own[device, rows, :].astype(F32)
-
-    lax.fori_loop(0, devices * blocks, step, jnp.zeros((pieces, BLOCK), F32), unroll=8)
+        ahead = at * parts
+        source = ahead + lax.shift_right_logical(at, blocks.bit_length() - 1)
+        gate = gates[pl.ds(at, 1), :]
+        after = []
+        for part in range(parts):
+            prior[ahead + part] = state[part].astype(BF16)
+            after.append(gate * state[part] + own[source + part].astype(F32))
+        return tuple(after)
+
+    zero = jnp.zeros(own.shape[1:], F32)
+    lax.fori_loop(0, devices * blocks, step, (zero,) * parts, unroll=16)
 
 
 def scan_pass(order, own):
     devices, height, lanes = own.shape
     blocks = order.shape[0] // devices
+    tiles = own.reshape(devices * height // EXTRA, EXTRA, lanes)
     vmem = pl.BlockSpec(memory_space=pltpu.VMEM)
-    return pl.pallas_call(
-        lambda *refs: scan_kernel(blocks, *refs),
+    prior = pl.pallas_call(
+        lambda *refs: scan_kernel(devices, blocks, *refs),
         in_specs=[pl.BlockSpec(memory_space=pltpu.SMEM), vmem],
         out_specs=vmem,
-        out_shape=jax.ShapeDtypeStruct((devices, height - EXTRA, lanes), BF16),
-        scratch_shapes=[pltpu.VMEM((devices, blocks, BLOCK), F32)],
+        out_shape=jax.ShapeDtypeStruct((tiles.shape[0] - devices, EXTRA, lanes), BF16),
+        scratch_shapes=[pltpu.VMEM((devices * blocks, BLOCK), F32)],
         name="scan",
-    )(order, own)
+    )(order, tiles)
+    return prior.reshape(devices, height - EXTRA, lanes)
 
 
 def outgo_kernel(heads, blocks, each, packing, place, faded, intra, states, slots, made, sems):
@@ -212,7 +233,8 @@
         high, middle, low = in_three(jnp.sum(sums.T, axis=0, keepdims=True))
         tile = jnp.where(row == 0, high, jnp.where(row == 1, middle, low))
         made[block, heads * BLOCK :, :] = tile.astype(BF16)
-        copy(block).start()
+    for inside in range(each):
+        copy(step * each + inside).start()
 
     @pl.when(step == pl.num_programs(0) - 1)
     def _():
@@ -224,7 +246,7 @@
     rows, width = faded.shape
     blocks = rows // BLOCK
     devices, height, lanes = states.shape
-    each = 2
+    each = OUTGO_EACH
     heads = width // BLOCK
     row_block = pl.BlockSpec((each * BLOCK, width), lambda b, *_: (b, 0))
     return pl.pallas_call(
@@ -301,7 +323,7 @@
     devices, height, lanes = came.shape
     blocks = order.shape[0] // devices
     width = gain.shape[1]
-    each = 4
+    each = FINISH_EACH
 
     def part(inside):
         def loader(b, order, place):
@@ -332,12 +354,10 @@
     mine = lax.axis_index("ctx").astype(jnp.int32)
     place = mine.reshape(1)
     decay = log_decay.T
-    document = jnp.arange(doc_lengths.shape[0], dtype=jnp.int32)
-    ahead = document[:, None] < jnp.arange(BLOCK, dtype=jnp.int32)[None, :]
-    starts = jnp.sum(jnp.where(ahead, doc_lengths[:, None], 0), axis=0, keepdims=True).astype(F32)
-
-    own = swap(own_states(packing, place, starts, key_rows, value_rows, decay), "ctx")
-    intra, faded = intra_pass(packing, place, starts, queries, key_rows, value_rows, decay)
+    lengths = doc_lengths[None, :]
+
+    own = swap(own_states(packing, place, lengths, key_rows, value_rows, decay), "ctx")
+    intra, faded = intra_pass(packing, place, lengths, queries, key_rows, value_rows, decay)
 
     index = jnp.arange(packing.shape[0], dtype=jnp.int32)
     hit = (packing[None, :] == index[:, None]).astype(jnp.int32)

time: 275 us -> 268 us (0.975)
  Pallas kernels: 65.1 us -> 57.3 us
    pallas_call x1, Pallas kernels: 9.82 us -> 6.5 us  [scan_pass(): pl.pallas_call(lambda *refs: scan_kernel(devices, blocks, *refs), in_spec...]
  transfers between devices with their start and end apart: 5 -> 5, of which waited for: 4 -> 4; matrix products, arithmetic and copies ran while one was open for 0% -> 0% of each run, Pallas kernels for 10% -> 9%
where the time goes in v3:
time: 268 us; the launch traced here: 265 us
  blocking collectives  103 us (38%)
  waiting for transfers between devices  83.3 us (31%)
  Pallas kernels  57.3 us (21%)
  starting transfers between devices  20.1 us (8%)
    all_to_all x1, blocking collectives, swap(): return lax.all_to_all(x, axis, split_axis=0, concat_axis=0, tiled=True)  103 us
    all_to_all x2, waiting for transfers between devices, swap(): return lax.all_to_all(x, axis, split_axis=0, concat_axis=0, tiled=True)  79.2 us
    pallas_call x1, Pallas kernels, intra_pass(): pl.pallas_call(lambda *refs: intra_kernel(heads, *refs), grid_spec=pltpu....  24.5 us
    all_to_all x2, starting transfers between devices, swap(): return lax.all_to_all(x, axis, split_axis=0, concat_axis=0, tiled=True)  14.7 us
    pallas_call x1, Pallas kernels, own_states(): pl.pallas_call(lambda *refs: own_kernel(heads, blocks, each, *refs), grid...  9.45 us
    pallas_call x1, Pallas kernels, outgo_pass(): pl.pallas_call(lambda *refs: outgo_kernel(heads, blocks, each, *refs), gr...  9.37 us
    pallas_call x1, Pallas kernels, scan_pass(): pl.pallas_call(lambda *refs: scan_kernel(devices, blocks, *refs), in_spec...  6.5 us
    ppermute x3, starting transfers between devices, body(): squares.append(lax.ppermute(part, 'head', pairs))  5.37 us
  transfers between devices with their start and end apart: 5, of which 4 were waited for; matrix products, arithmetic and copies ran while one was open for 0% of the time, Pallas kernels for 9%

profile of v3, /device:TPU:16, one launch (start us, length us, event | category | flops | bytes accessed | tf_op | source)
XLA Modules:
  0.0 265.2 jit_solution(15407384796275916967)
XLA Ops:
  0.0 9.5 %own.1 = bf16[32,528,128]{2,1,0:T(8,128)(2,1)} custom-call(s32[512]{0:T(512)} %refs_0_.5, s32[1]{0:T(128)} %bitcast.refs_1_.place, s32[1,64]{1,0:T(1,128)} %bitcast.10, bf16[2048,1024]{1,0:T(8,128)(2,1)} %refs_3_.3, bf16[2048,1024]{1,0:T(8,128)(2,1)} %refs_4_.3, bf16[8,2048]{1,0:T(8,128)(2,1)} %bitcast.7), custom_call_target="tpu_custom_call" | custom-call | tf_op jit(solution)/shard_map/own/pallas_call | solution.py:101
  9.5 0.0 copy-start
  9.5 7.5 %all-to-all-start = ((bf16[32,528,128]{2,1,0:T(8,128)(2,1)}), bf16[32,528,128]{2,1,0:T(8,128)(2,1)}, u32[]{:S(2)}, u32[]{:S(2)}) async-start(bf16[32,528,128]{2,1,0:T(8,128)(2,1)} %own.1), calls=%async_computation | async-start | bytes 8650752 | tf_op jit(solution)/shard_map/all_to_all | solution.py:350
  17.0 0.0 copy-done
  17.0 0.7 select_reduce_fusion.refs_0_.order
  17.7 52.3 %all-to-all-done = bf16[32,528,128]{2,1,0:T(8,128)(2,1)} async-done(((bf16[32,528,128]{2,1,0:T(8,128)(2,1)}), bf16[32,528,128]{2,1,0:T(8,128)(2,1)}, u32[]{:S(2)}, u32[]{:S(2)}) %all-to-all-start) | async-done | bytes 4325408 | tf_op jit(solution)/shard_map/all_to_all | solution.py:350
  70.0 6.5 %scan.1 = bf16[1024,16,128]{2,1,0:T(8,128)(2,1)} custom-call(s32[512]{0:T(512)} %select_reduce_fusion.refs_0_.order, bf16[1056,16,128]{2,1,0:T(8,128)(2,1)} %bitcast.3.refs_1_), custom_call_target="tpu_custom_call" | custom-call | tf_op jit(solution)/shard_map/scan/pallas_call | solution.py:200
  76.5 7.3 %all-to-all-start.1 = ((bf16[32,512,128]{2,1,0:T(8,128)(2,1)}), bf16[32,512,128]{2,1,0:T(8,128)(2,1)}, u32[]{:S(2)}, u32[]{:S(2)}) async-start(bf16[32,512,128]{2,1,0:T(8,128)(2,1)} %bitcast.6), calls=%async_computation.1 | async-start | bytes 8388608 | tf_op jit(solution)/shard_map/all_to_all | solution.py:350
  83.8 24.5 %intra.1 = (f32[2048,1024]{1,0:T(8,128)}, bf16[2048,1024]{1,0:T(8,128)(2,1)}) custom-call(s32[512]{0:T(512)} %refs_0_.5, s32[1]{0:T(128)} %bitcast.refs_1_.place, s32[1,64]{1,0:T(1,128)} %bitcast.11, bf16[2048,1024]{1,0:T(8,128)(2,1)} %refs_3_.2, bf16[2048,1024]{1,0:T(8,128)(2,1)} %refs_3_.3, bf16[2048,1024]{1,0:T(8,128)(2,1)} %refs_4_.3, ...), custom_call_target="tpu_custom_call" | custom-call | tf_op jit(solution)/shard_map/intra/pallas_call | solution.py:150
  108.3 27.0 %all-to-all-done.1.refs_4_ = bf16[32,512,128]{2,1,0:T(8,128)(2,1)} async-done(((bf16[32,512,128]{2,1,0:T(8,128)(2,1)}), bf16[32,512,128]{2,1,0:T(8,128)(2,1)}, u32[]{:S(2)}, u32[]{:S(2)}) %all-to-all-start.1) | async-done | bytes 4194336 | tf_op jit(solution)/shard_map/all_to_all | solution.py:350
  135.2 9.4 %outgo.1 = bf16[32,1040,128]{2,1,0:T(8,128)(2,1)} custom-call(s32[512]{0:T(512)} %refs_0_.5, s32[1]{0:T(128)} %bitcast.refs_1_.place, bf16[2048,1024]{1,0:T(8,128)(2,1)} %get-tuple-element.7.refs_2_, f32[2048,1024]{1,0:T(8,128)} %get-tuple-element.8.refs_3_, bf16[32,512,128]{2,1,0:T(8,128)(2,1)} %all-to-all-done.1.refs_4_), custom_call_target="tpu_custom_call" | custom-call | tf_op jit(solution)/shard_map/outgo/pallas_call | solution.py:252
  144.6 103.1 %all_to_all.15.came.refs_7_.refs_8_.refs_9_.refs_10_.refs_11_.refs_12_.refs_13_.refs_14_ = bf16[32,1040,128]{2,1,0:T(8,128)(2,1)} all-to-all(bf16[32,1040,128]{2,1,0:T(8,128)(2,1)} %outgo.1), channel_id=1, replica_groups=mesh['ctx'=32,'head'=4] {'ctx'}, dimensions={0} | all-to-all | bytes 17039360 | tf_op jit(solution)/shard_map/all_to_all | solution.py:350
  247.7 2.3 squares.1.refs_2_
  250.0 4.1 %collective-permute-start.2 = (f32[16,128]{1,0:T(8,128)}, f32[16,128]{1,0:T(8,128)S(1)}, u32[]{:S(2)}, u32[]{:S(2)}) collective-permute-start(f32[16,128]{1,0:T(8,128)} %squares.1.refs_2_), channel_id=1, source_target_pairs={{0,3},{1,0},{2,1},{3,2},{4,7},{5,4},{6,5},{7,6},{8,11},{9,8},{10,9... | collective-permute-start | bytes 24584 | tf_op jit(solution)/shard_map/ppermute | solution.py:373
  254.1 0.0 collective-permute-start.1
  254.1 1.2 collective-permute-start
  255.4 0.3 collective-permute-done.2.refs_5_
  255.7 0.0 copy-start.1
  255.7 3.8 %collective-permute-done.1.refs_4_ = f32[16,128]{1,0:T(8,128)S(1)} collective-permute-done((f32[16,128]{1,0:T(8,128)}, f32[16,128]{1,0:T(8,128)S(1)}, u32[]{:S(2)}, u32[]{:S(2)}) %collective-permute-start.1) | collective-permute-done | bytes 8224 | tf_op jit(solution)/shard_map/ppermute | solution.py:373
  259.5 0.0 copy-start.2
  259.5 0.0 collective-permute-done.refs_3_
  259.5 0.0 copy-start.3
  259.5 0.0 copy-done.1
  259.5 0.6 copy-done.2
  260.1 0.0 copy-done.3
  260.1 5.2 %finish.1 = bf16[2048,1024]{1,0:T(8,128)(2,1)} custom-call(s32[512]{0:T(512)} %select_reduce_fusion.refs_0_.order, s32[1]{0:T(128)} %bitcast.refs_1_.place, f32[16,128]{1,0:T(8,128)} %squares.1.refs_2_, f32[16,128]{1,0:T(8,128)} %copy-done.3, f32[16,128]{1,0:T(8,128)} %copy-done.2, f32[16,128]{1,0:T(8,128)} %copy-done.1, f32[1,1024]{1,0:T(1,128)} %bitcast.9, ...), custom_call_target="tpu_custom_call" | custom-call | tf_op jit(solution)/shard_map/finish/pallas_call | solution.py:334
Async XLA Ops:
  9.5 7.5 %copy-start = (s32[512]{0:T(512)S(1)}, s32[512]{0:T(512)}, u32[]{:S(2)}) copy-start(s32[512]{0:T(512)} %refs_0_.5) | copy-start | bytes 6148
  9.5 60.5 %all-to-all-start = ((bf16[32,528,128]{2,1,0:T(8,128)(2,1)}), bf16[32,528,128]{2,1,0:T(8,128)(2,1)}, u32[]{:S(2)}, u32[]{:S(2)}) async-start(bf16[32,528,128]{2,1,0:T(8,128)(2,1)} %own.1), calls=%async_computation | async-start | bytes 8650752 | tf_op jit(solution)/shard_map/all_to_all | solution.py:350
  76.5 58.8 %all-to-all-start.1 = ((bf16[32,512,128]{2,1,0:T(8,128)(2,1)}), bf16[32,512,128]{2,1,0:T(8,128)(2,1)}, u32[]{:S(2)}, u32[]{:S(2)}) async-start(bf16[32,512,128]{2,1,0:T(8,128)(2,1)} %bitcast.6), calls=%async_computation.1 | async-start | bytes 8388608 | tf_op jit(solution)/shard_map/all_to_all | solution.py:350
  250.0 5.7 %collective-permute-start.2 = (f32[16,128]{1,0:T(8,128)}, f32[16,128]{1,0:T(8,128)S(1)}, u32[]{:S(2)}, u32[]{:S(2)}) collective-permute-start(f32[16,128]{1,0:T(8,128)} %squares.1.refs_2_), channel_id=1, source_target_pairs={{0,3},{1,0},{2,1},{3,2},{4,7},{5,4},{6,5},{7,6},{8,11},{9,8},{10,9... | collective-permute-start | bytes 24584 | tf_op jit(solution)/shard_map/ppermute | solution.py:373
  254.1 5.4 %collective-permute-start.1 = (f32[16,128]{1,0:T(8,128)}, f32[16,128]{1,0:T(8,128)S(1)}, u32[]{:S(2)}, u32[]{:S(2)}) collective-permute-start(f32[16,128]{1,0:T(8,128)} %squares.1.refs_2_), channel_id=1, source_target_pairs={{0,2},{1,3},{2,0},{3,1},{4,6},{5,7},{6,4},{7,5},{8,10},{9,11},{10,... | collective-permute-start | bytes 24584 | tf_op jit(solution)/shard_map/ppermute | solution.py:373
  254.1 5.4 %collective-permute-start = (f32[16,128]{1,0:T(8,128)}, f32[16,128]{1,0:T(8,128)S(1)}, u32[]{:S(2)}, u32[]{:S(2)}) collective-permute-start(f32[16,128]{1,0:T(8,128)} %squares.1.refs_2_), channel_id=1, source_target_pairs={{0,1},{1,2},{2,3},{3,0},{4,5},{5,6},{6,7},{7,4},{8,9},{9,10},{10,1... | collective-permute-start | bytes 24584 | tf_op jit(solution)/shard_map/ppermute | solution.py:373
  255.7 3.8 %copy-start.1 = (f32[16,128]{1,0:T(8,128)}, f32[16,128]{1,0:T(8,128)S(1)}, u32[]{:S(2)}) copy-start(f32[16,128]{1,0:T(8,128)S(1)} %collective-permute-done.2.refs_5_) | copy-start | bytes 24580
  259.5 0.6 copy-start.2
  259.5 0.6 copy-start.3

commit v4 on v3

--- a/solution.py
+++ b/solution.py
@@ -117,6 +117,7 @@
             ],
         ),
         out_shape=jax.ShapeDtypeStruct(shape, BF16),
+        compiler_params=pltpu.CompilerParams(vmem_limit_bytes=14 * 2**20),
         name="own",
     )(packing, place, lengths, keys, values, decay)
 
@@ -203,6 +204,7 @@
         out_specs=vmem,
         out_shape=jax.ShapeDtypeStruct((tiles.shape[0] - devices, EXTRA, lanes), BF16),
         scratch_shapes=[pltpu.VMEM((devices * blocks, BLOCK), F32)],
+        compiler_params=pltpu.CompilerParams(vmem_limit_bytes=20 * 2**20),
         name="scan",
     )(order, tiles)
     return prior.reshape(devices, height - EXTRA, lanes)
@@ -266,6 +268,7 @@
             ],
         ),
         out_shape=jax.ShapeDtypeStruct((devices, width + EXTRA, BLOCK), BF16),
+        compiler_params=pltpu.CompilerParams(vmem_limit_bytes=18 * 2**20),
         name="outgo",
     )(packing, place, faded, intra, states)
 
@@ -298,6 +301,7 @@
             pltpu.VMEM((blocks, EXTRA, BLOCK), BF16),
             pltpu.SemaphoreType.DMA((blocks,)),
         ],
+        compiler_params=pltpu.CompilerParams(vmem_limit_bytes=2 * 2**20),
         name="squares",
     )(order, place, came)
 
@@ -342,6 +346,7 @@
             out_specs=pl.BlockSpec((each * BLOCK, width), lambda b, *_: (b, 0)),
         ),
         out_shape=jax.ShapeDtypeStruct((blocks * BLOCK, width), BF16),
+        compiler_params=pltpu.CompilerParams(vmem_limit_bytes=14 * 2**20),
         name="finish",
     )(order, place, *squares, gain, *[came] * each)
 
@@ -356,14 +361,17 @@
     decay = log_decay.T
     lengths = doc_lengths[None, :]
 
-    own = swap(own_states(packing, place, lengths, key_rows, value_rows, decay), "ctx")
-    intra, faded = intra_pass(packing, place, lengths, queries, key_rows, value_rows, decay)
-
     index = jnp.arange(packing.shape[0], dtype=jnp.int32)
     hit = (packing[None, :] == index[:, None]).astype(jnp.int32)
     order = jnp.sum(hit * index[None, :], axis=1)
 
+    packing, order = lax.optimization_barrier((packing, order))
+    held = [pltpu.with_memory_space_constraint(x, pltpu.HBM) for x in (key_rows, value_rows)]
+    own = swap(own_states(packing, place, lengths, *held, decay), "ctx")
+    intra, faded = intra_pass(packing, place, lengths, queries, key_rows, value_rows, decay)
+
     states = swap(scan_pass(order, own), "ctx")
+    faded, intra = (pltpu.with_memory_space_constraint(x, pltpu.HBM) for x in (faded, intra))
     came = swap(outgo_pass(packing, place, faded, intra, states), "ctx")
     part = squares_pass(order, place, came)
     groups = lax.axis_size("head")

time: 268 us -> 257 us (0.959)
  blocking collectives: 103 us -> 159 us
  waiting for transfers between devices: 83.3 us -> 30.8 us
  Pallas kernels: 57.3 us -> 47.7 us
  starting transfers between devices: 20.1 us -> 12.2 us
  local copies, waits for them, and re-layouts: 0.6 us -> 4.02 us
    all_to_all x1 -> x2, blocking collectives: 103 us -> 159 us  [swap(): return lax.all_to_all(x, axis, split_axis=0, concat_axis=0, tiled=True)]
    all_to_all x2 -> x1, waiting for transfers between devices: 79.2 us -> 26.9 us  [swap(): return lax.all_to_all(x, axis, split_axis=0, concat_axis=0, tiled=True)]
    all_to_all x2 -> x1, starting transfers between devices: 14.7 us -> 6.84 us  [swap(): return lax.all_to_all(x, axis, split_axis=0, concat_axis=0, tiled=True)]
    pallas_call x1, Pallas kernels: 6.5 us -> 2.83 us  [scan_pass(): pl.pallas_call(lambda *refs: scan_kernel(devices, blocks, *refs), in_spec...]
    unnamed x8 -> x12, local copies, waits for them, and re-layouts: 0.6 us -> 4.02 us
  transfers between devices with their start and end apart: 5 -> 4, of which waited for: 4 -> 3; matrix products, arithmetic and copies ran while one was open for 0% -> 0% of each run, Pallas kernels for 9% -> 10%
where the time goes in v4:
time: 257 us; the launch traced here: 255 us
  blocking collectives  159 us (62%)
  Pallas kernels  47.7 us (19%)
  waiting for transfers between devices  30.8 us (12%)
  starting transfers between devices  12.2 us (5%)
  local copies, waits for them, and re-layouts  4.02 us (2%)
    all_to_all x2, blocking collectives, swap(): return lax.all_to_all(x, axis, split_axis=0, concat_axis=0, tiled=True)  159 us
    all_to_all x1, waiting for transfers between devices, swap(): return lax.all_to_all(x, axis, split_axis=0, concat_axis=0, tiled=True)  26.9 us
    pallas_call x1, Pallas kernels, intra_pass(): pl.pallas_call(lambda *refs: intra_kernel(heads, *refs), grid_spec=pltpu....  24.6 us
    pallas_call x1, Pallas kernels, own_states(): pl.pallas_call(lambda *refs: own_kernel(heads, blocks, each, *refs), grid...  7.94 us
    pallas_call x1, Pallas kernels, outgo_pass(): pl.pallas_call(lambda *refs: outgo_kernel(heads, blocks, each, *refs), gr...  7.94 us
    all_to_all x1, starting transfers between devices, swap(): return lax.all_to_all(x, axis, split_axis=0, concat_axis=0, tiled=True)  6.84 us
    ppermute x3, starting transfers between devices, body(): squares.append(lax.ppermute(part, 'head', pairs))  5.37 us
  transfers between devices with their start and end apart: 4, of which 3 were waited for; matrix products, arithmetic and copies ran while one was open for 0% of the time, Pallas kernels for 10%

profile of v4, /device:TPU:16, one launch (start us, length us, event | category | flops | bytes accessed | tf_op | source)
XLA Modules:
  0.0 254.7 jit_solution(4239191440969876592)
XLA Ops:
  0.0 0.9 select_reduce_fusion.refs_0_.order
  0.9 0.0 copy-start.1
  0.9 0.7 copy-done.1
  1.6 0.0 copy-start.2
  1.6 0.7 copy-done.2
  2.3 0.0 copy-start.5
  2.3 0.7 copy-done.5
  3.0 7.9 %own.1 = bf16[32,528,128]{2,1,0:T(8,128)(2,1)S(1)} custom-call(s32[512]{0:T(512)S(1)} %copy-done.2, s32[1]{0:T(128)} %bitcast.refs_1_.place, s32[1,64]{1,0:T(1,128)S(1)} %bitcast.12, bf16[2048,1024]{1,0:T(8,128)(2,1)} %refs_3_.3, bf16[2048,1024]{1,0:T(8,128)(2,1)} %refs_4_.3, bf16[8,2048]{1,0:T(8,128)(2,1)S(1)} %bitcast.9), custom_call_target="tpu_custom_call" | custom-call | tf_op jit(solution)/shard_map/own/pallas_call | solution.py:101
  10.9 57.9 %all_to_all.15 = bf16[32,528,128]{2,1,0:T(8,128)(2,1)S(1)} all-to-all(bf16[32,528,128]{2,1,0:T(8,128)(2,1)S(1)} %own.1), channel_id=1, replica_groups=mesh['ctx'=32,'head'=4] {'ctx'}, dimensions={0} | all-to-all | bytes 8650752 | tf_op jit(solution)/shard_map/all_to_all | solution.py:355
  68.8 2.8 %scan.1 = bf16[1024,16,128]{2,1,0:T(8,128)(2,1)S(1)} custom-call(s32[512]{0:T(512)S(1)} %select_reduce_fusion.refs_0_.order, bf16[1056,16,128]{2,1,0:T(8,128)(2,1)S(1)} %bitcast.6), custom_call_target="tpu_custom_call" | custom-call | tf_op jit(solution)/shard_map/scan/pallas_call | solution.py:201
  71.6 0.0 copy-start
  71.6 1.9 copy-done
  73.6 6.8 %all-to-all-start.1 = ((bf16[32,512,128]{2,1,0:T(8,128)(2,1)}), bf16[32,512,128]{2,1,0:T(8,128)(2,1)}, u32[]{:S(2)}, u32[]{:S(2)}) async-start(bf16[32,512,128]{2,1,0:T(8,128)(2,1)} %bitcast.7), calls=%async_computation.1 | async-start | bytes 8388608 | tf_op jit(solution)/shard_map/all_to_all | solution.py:355
  80.4 0.0 copy-start.3
  80.4 24.6 %intra.1 = (f32[2048,1024]{1,0:T(8,128)}, bf16[2048,1024]{1,0:T(8,128)(2,1)}) custom-call(s32[512]{0:T(512)} %refs_0_.2, s32[1]{0:T(128)} %bitcast.refs_1_.place, s32[1,64]{1,0:T(1,128)} %bitcast.11, bf16[2048,1024]{1,0:T(8,128)(2,1)} %refs_3_.2, bf16[2048,1024]{1,0:T(8,128)(2,1)} %refs_3_.3, bf16[2048,1024]{1,0:T(8,128)(2,1)} %refs_4_.3, ...), custom_call_target="tpu_custom_call" | custom-call | tf_op jit(solution)/shard_map/intra/pallas_call | solution.py:151
  105.0 26.9 %all-to-all-done.1.refs_4_ = bf16[32,512,128]{2,1,0:T(8,128)(2,1)} async-done(((bf16[32,512,128]{2,1,0:T(8,128)(2,1)}), bf16[32,512,128]{2,1,0:T(8,128)(2,1)}, u32[]{:S(2)}, u32[]{:S(2)}) %all-to-all-start.1) | async-done | bytes 4194336 | tf_op jit(solution)/shard_map/all_to_all | solution.py:355
  131.9 0.0 copy-done.3
  131.9 7.9 %outgo.1 = bf16[32,1040,128]{2,1,0:T(8,128)(2,1)S(1)} custom-call(s32[512]{0:T(512)S(1)} %copy-done.3, s32[1]{0:T(128)} %bitcast.refs_1_.place, bf16[2048,1024]{1,0:T(8,128)(2,1)} %get-tuple-element.11.refs_2_, f32[2048,1024]{1,0:T(8,128)} %get-tuple-element.12.refs_3_, bf16[32,512,128]{2,1,0:T(8,128)(2,1)} %all-to-all-done.1.refs_4_), custom_call_target="tpu_custom_call" | custom-call | tf_op jit(solution)/shard_map/outgo/pallas_call | solution.py:254
  139.8 101.2 %all_to_all.16.came.refs_7_.refs_8_.refs_9_.refs_10_.refs_11_.refs_12_.refs_13_.refs_14_ = bf16[32,1040,128]{2,1,0:T(8,128)(2,1)S(1)} all-to-all(bf16[32,1040,128]{2,1,0:T(8,128)(2,1)S(1)} %outgo.1), channel_id=1, replica_groups=mesh['ctx'=32,'head'=4] {'ctx'}, dimensions={0} | all-to-all | bytes 17039360 | tf_op jit(solution)/shard_map/all_to_all | solution.py:355
  241.0 0.0 copy-start.4
  241.0 1.1 squares.1.refs_2_
  242.2 4.1 %collective-permute-start.2 = (f32[16,128]{1,0:T(8,128)S(1)}, f32[16,128]{1,0:T(8,128)S(1)}, u32[]{:S(2)}, u32[]{:S(2)}) collective-permute-start(f32[16,128]{1,0:T(8,128)S(1)} %squares.1.refs_2_), channel_id=1, source_target_pairs={{0,3},{1,0},{2,1},{3,2},{4,7},{5,4},{6,5},{7,6},{8,11},{9,8},{10,9... | collective-permute-start | bytes 24584 | tf_op jit(solution)/shard_map/ppermute | solution.py:381
  246.3 0.0 collective-permute-start.1
  246.3 1.3 collective-permute-start
  247.5 0.1 collective-permute-done.2.refs_5_
  247.6 3.8 %collective-permute-done.1.refs_4_ = f32[16,128]{1,0:T(8,128)S(1)} collective-permute-done((f32[16,128]{1,0:T(8,128)S(1)}, f32[16,128]{1,0:T(8,128)S(1)}, u32[]{:S(2)}, u32[]{:S(2)}) %collective-permute-start.1) | collective-permute-done | bytes 8224 | tf_op jit(solution)/shard_map/ppermute | solution.py:381
  251.4 0.0 collective-permute-done.refs_3_
  251.4 0.0 copy-done.4
  251.4 3.2 %finish.1 = bf16[2048,1024]{1,0:T(8,128)(2,1)} custom-call(s32[512]{0:T(512)S(1)} %select_reduce_fusion.refs_0_.order, s32[1]{0:T(128)} %bitcast.refs_1_.place, f32[16,128]{1,0:T(8,128)S(1)} %squares.1.refs_2_, f32[16,128]{1,0:T(8,128)S(1)} %collective-permute-done.refs_3_, f32[16,128]{1,0:T(8,128)S(1)} %collective-permute-done.1.refs_4_, ...), custom_call_target="tpu_custom_call" | custom-call | tf_op jit(solution)/shard_map/finish/pallas_call | solution.py:338
Async XLA Ops:
  0.9 0.8 copy-start.1
  1.6 0.7 copy-start.2
  2.3 0.7 copy-start.5
  71.6 1.9 copy-start
  73.6 58.3 %all-to-all-start.1 = ((bf16[32,512,128]{2,1,0:T(8,128)(2,1)}), bf16[32,512,128]{2,1,0:T(8,128)(2,1)}, u32[]{:S(2)}, u32[]{:S(2)}) async-start(bf16[32,512,128]{2,1,0:T(8,128)(2,1)} %bitcast.7), calls=%async_computation.1 | async-start | bytes 8388608 | tf_op jit(solution)/shard_map/all_to_all | solution.py:355
  80.4 51.5 %copy-start.3 = (s32[512]{0:T(512)S(1)}, s32[512]{0:T(512)}, u32[]{:S(2)}) copy-start(s32[512]{0:T(512)} %refs_0_.2) | copy-start | bytes 6148
  241.0 10.4 %copy-start.4 = (f32[1024]{0:T(1024)S(1)}, f32[1024]{0:T(1024)}, u32[]{:S(2)}) copy-start(f32[1024]{0:T(1024)} %param.11) | copy-start | bytes 12292
  242.2 5.5 %collective-permute-start.2 = (f32[16,128]{1,0:T(8,128)S(1)}, f32[16,128]{1,0:T(8,128)S(1)}, u32[]{:S(2)}, u32[]{:S(2)}) collective-permute-start(f32[16,128]{1,0:T(8,128)S(1)} %squares.1.refs_2_), channel_id=1, source_target_pairs={{0,3},{1,0},{2,1},{3,2},{4,7},{5,4},{6,5},{7,6},{8,11},{9,8},{10,9... | collective-permute-start | bytes 24584 | tf_op jit(solution)/shard_map/ppermute | solution.py:381
  246.3 5.2 %collective-permute-start.1 = (f32[16,128]{1,0:T(8,128)S(1)}, f32[16,128]{1,0:T(8,128)S(1)}, u32[]{:S(2)}, u32[]{:S(2)}) collective-permute-start(f32[16,128]{1,0:T(8,128)S(1)} %squares.1.refs_2_), channel_id=1, source_target_pairs={{0,2},{1,3},{2,0},{3,1},{4,6},{5,7},{6,4},{7,5},{8,10},{9,11},{10,... | collective-permute-start | bytes 24584 | tf_op jit(solution)/shard_map/ppermute | solution.py:381
  246.3 5.2 %collective-permute-start = (f32[16,128]{1,0:T(8,128)S(1)}, f32[16,128]{1,0:T(8,128)S(1)}, u32[]{:S(2)}, u32[]{:S(2)}) collective-permute-start(f32[16,128]{1,0:T(8,128)S(1)} %squares.1.refs_2_), channel_id=1, source_target_pairs={{0,1},{1,2},{2,3},{3,0},{4,5},{5,6},{6,7},{7,4},{8,9},{9,10},{10,1... | collective-permute-start | bytes 24584 | tf_op jit(solution)/shard_map/ppermute | solution.py:381

commit v5 on v4

--- a/solution.py
+++ b/solution.py
@@ -117,7 +117,6 @@
             ],
         ),
         out_shape=jax.ShapeDtypeStruct(shape, BF16),
-        compiler_params=pltpu.CompilerParams(vmem_limit_bytes=14 * 2**20),
         name="own",
     )(packing, place, lengths, keys, values, decay)
 
@@ -365,13 +364,11 @@
     hit = (packing[None, :] == index[:, None]).astype(jnp.int32)
     order = jnp.sum(hit * index[None, :], axis=1)
 
-    packing, order = lax.optimization_barrier((packing, order))
-    held = [pltpu.with_memory_space_constraint(x, pltpu.HBM) for x in (key_rows, value_rows)]
-    own = swap(own_states(packing, place, lengths, *held, decay), "ctx")
+    own = swap(own_states(packing, place, lengths, key_rows, value_rows, decay), "ctx")
     intra, faded = intra_pass(packing, place, lengths, queries, key_rows, value_rows, decay)
 
+    own, order, intra, faded = lax.optimization_barrier((own, order, intra, faded))
     states = swap(scan_pass(order, own), "ctx")
-    faded, intra = (pltpu.with_memory_space_constraint(x, pltpu.HBM) for x in (faded, intra))
     came = swap(outgo_pass(packing, place, faded, intra, states), "ctx")
     part = squares_pass(order, place, came)
     groups = lax.axis_size("head")

time: 257 us -> 251 us (0.977)
  local copies, waits for them, and re-layouts: 4.02 us -> 0.02 us
    pallas_call x1, Pallas kernels: 7.94 us -> 3.9 us  [outgo_pass(): pl.pallas_call(lambda *refs: outgo_kernel(heads, blocks, each, *refs), gr...]
    unnamed x12 -> x8, local copies, waits for them, and re-layouts: 4.02 us -> 0.02 us
where the time goes in v5:
time: 251 us; the launch traced here: 249 us
  blocking collectives  157 us (63%)
  Pallas kernels  46.9 us (19%)
  waiting for transfers between devices  32.1 us (13%)
  starting transfers between devices  12.9 us (5%)
    all_to_all x2, blocking collectives, swap(): return lax.all_to_all(x, axis, split_axis=0, concat_axis=0, tiled=True)  157 us
    all_to_all x1, waiting for transfers between devices, swap(): return lax.all_to_all(x, axis, split_axis=0, concat_axis=0, tiled=True)  28.2 us
    pallas_call x1, Pallas kernels, intra_pass(): pl.pallas_call(lambda *refs: intra_kernel(heads, *refs), grid_spec=pltpu....  24.6 us
    pallas_call x1, Pallas kernels, own_states(): pl.pallas_call(lambda *refs: own_kernel(heads, blocks, each, *refs), grid...  9.37 us
    all_to_all x1, starting transfers between devices, swap(): return lax.all_to_all(x, axis, split_axis=0, concat_axis=0, tiled=True)  7.49 us
    ppermute x3, starting transfers between devices, body(): squares.append(lax.ppermute(part, 'head', pairs))  5.36 us
  transfers between devices with their start and end apart: 4, of which 3 were waited for; matrix products, arithmetic and copies ran while one was open for 0% of the time, Pallas kernels for 10%

profile of v5, /device:TPU:16, one launch (start us, length us, event | category | flops | bytes accessed | tf_op | source)
XLA Modules:
  0.0 248.8 jit_solution(17250983365006317717)
XLA Ops:
  0.0 9.4 %own.1 = bf16[32,528,128]{2,1,0:T(8,128)(2,1)} custom-call(s32[512]{0:T(512)} %refs_0_.5, s32[1]{0:T(128)} %bitcast.refs_1_.place, s32[1,64]{1,0:T(1,128)} %bitcast.10, bf16[2048,1024]{1,0:T(8,128)(2,1)} %refs_4_.3, bf16[2048,1024]{1,0:T(8,128)(2,1)} %refs_5_.1, bf16[8,2048]{1,0:T(8,128)(2,1)} %bitcast.8), custom_call_target="tpu_custom_call" | custom-call | tf_op jit(solution)/shard_map/own/pallas_call | solution.py:101
  9.4 7.5 %all-to-all-start = ((bf16[32,528,128]{2,1,0:T(8,128)(2,1)}), bf16[32,528,128]{2,1,0:T(8,128)(2,1)}, u32[]{:S(2)}, u32[]{:S(2)}) async-start(bf16[32,528,128]{2,1,0:T(8,128)(2,1)} %own.1), calls=%async_computation | async-start | bytes 8650752 | tf_op jit(solution)/shard_map/all_to_all | solution.py:354
  16.9 0.0 copy-start.2
  16.9 24.6 %intra.1 = (f32[2048,1024]{1,0:T(8,128)}, bf16[2048,1024]{1,0:T(8,128)(2,1)}) custom-call(s32[512]{0:T(512)} %refs_0_.5, s32[1]{0:T(128)} %bitcast.refs_1_.place, s32[1,64]{1,0:T(1,128)} %bitcast.11, bf16[2048,1024]{1,0:T(8,128)(2,1)} %refs_3_.3, bf16[2048,1024]{1,0:T(8,128)(2,1)} %refs_4_.3, bf16[2048,1024]{1,0:T(8,128)(2,1)} %refs_5_.1, ...), custom_call_target="tpu_custom_call" | custom-call | tf_op jit(solution)/shard_map/intra/pallas_call | solution.py:150
  41.5 0.0 copy-done.2
  41.5 0.2 select_reduce_fusion.refs_0_.order
  41.7 28.2 %all-to-all-done = bf16[32,528,128]{2,1,0:T(8,128)(2,1)} async-done(((bf16[32,528,128]{2,1,0:T(8,128)(2,1)}), bf16[32,528,128]{2,1,0:T(8,128)(2,1)}, u32[]{:S(2)}, u32[]{:S(2)}) %all-to-all-start) | async-done | bytes 4325408 | tf_op jit(solution)/shard_map/all_to_all | solution.py:354
  69.9 0.0 copy-start.1
  69.9 4.7 %scan.1 = bf16[1024,16,128]{2,1,0:T(8,128)(2,1)S(1)} custom-call(s32[512]{0:T(512)S(1)} %select_reduce_fusion.refs_0_.order, bf16[1056,16,128]{2,1,0:T(8,128)(2,1)} %bitcast.3.refs_1_), custom_call_target="tpu_custom_call" | custom-call | tf_op jit(solution)/shard_map/scan/pallas_call | solution.py:200
  74.6 0.0 copy-start
  74.6 54.3 %all_to_all.15.refs_4_ = bf16[32,512,128]{2,1,0:T(8,128)(2,1)S(1)} all-to-all(bf16[32,512,128]{2,1,0:T(8,128)(2,1)S(1)} %bitcast.6), channel_id=1, replica_groups=mesh['ctx'=32,'head'=4] {'ctx'}, dimensions={0} | all-to-all | bytes 8388608 | tf_op jit(solution)/shard_map/all_to_all | solution.py:354
  128.9 0.0 copy-done.1
  128.9 0.0 copy-done
  128.9 3.9 %outgo.1 = bf16[32,1040,128]{2,1,0:T(8,128)(2,1)S(1)} custom-call(s32[512]{0:T(512)S(1)} %copy-done.2, s32[1]{0:T(128)} %bitcast.refs_1_.place, bf16[2048,1024]{1,0:T(8,128)(2,1)S(1)} %copy-done.1, f32[2048,1024]{1,0:T(8,128)S(1)} %copy-done, bf16[32,512,128]{2,1,0:T(8,128)(2,1)S(1)} %all_to_all.15.refs_4_), custom_call_target="tpu_custom_call" | custom-call | tf_op jit(solution)/shard_map/outgo/pallas_call | solution.py:253
  132.8 102.3 %all_to_all.16.came.refs_7_.refs_8_.refs_9_.refs_10_.refs_11_.refs_12_.refs_13_.refs_14_ = bf16[32,1040,128]{2,1,0:T(8,128)(2,1)S(1)} all-to-all(bf16[32,1040,128]{2,1,0:T(8,128)(2,1)S(1)} %outgo.1), channel_id=1, replica_groups=mesh['ctx'=32,'head'=4] {'ctx'}, dimensions={0} | all-to-all | bytes 17039360 | tf_op jit(solution)/shard_map/all_to_all | solution.py:354
  235.1 0.0 copy-start.3
  235.1 1.1 squares.1.refs_2_
  236.3 4.1 %collective-permute-start.2 = (f32[16,128]{1,0:T(8,128)S(1)}, f32[16,128]{1,0:T(8,128)S(1)}, u32[]{:S(2)}, u32[]{:S(2)}) collective-permute-start(f32[16,128]{1,0:T(8,128)S(1)} %squares.1.refs_2_), channel_id=1, source_target_pairs={{0,3},{1,0},{2,1},{3,2},{4,7},{5,4},{6,5},{7,6},{8,11},{9,8},{10,9... | collective-permute-start | bytes 24584 | tf_op jit(solution)/shard_map/ppermute | solution.py:378
  240.4 0.0 collective-permute-start.1
  240.4 1.3 collective-permute-start
  241.6 0.1 collective-permute-done.2.refs_5_
  241.7 3.8 %collective-permute-done.1.refs_4_ = f32[16,128]{1,0:T(8,128)S(1)} collective-permute-done((f32[16,128]{1,0:T(8,128)S(1)}, f32[16,128]{1,0:T(8,128)S(1)}, u32[]{:S(2)}, u32[]{:S(2)}) %collective-permute-start.1) | collective-permute-done | bytes 8224 | tf_op jit(solution)/shard_map/ppermute | solution.py:378
  245.5 0.0 collective-permute-done.refs_3_
  245.5 0.0 copy-done.3
  245.5 3.2 %finish.1 = bf16[2048,1024]{1,0:T(8,128)(2,1)} custom-call(s32[512]{0:T(512)S(1)} %select_reduce_fusion.refs_0_.order, s32[1]{0:T(128)} %bitcast.refs_1_.place, f32[16,128]{1,0:T(8,128)S(1)} %squares.1.refs_2_, f32[16,128]{1,0:T(8,128)S(1)} %collective-permute-done.refs_3_, f32[16,128]{1,0:T(8,128)S(1)} %collective-permute-done.1.refs_4_, ...), custom_call_target="tpu_custom_call" | custom-call | tf_op jit(solution)/shard_map/finish/pallas_call | solution.py:337
Async XLA Ops:
  9.4 60.5 %all-to-all-start = ((bf16[32,528,128]{2,1,0:T(8,128)(2,1)}), bf16[32,528,128]{2,1,0:T(8,128)(2,1)}, u32[]{:S(2)}, u32[]{:S(2)}) async-start(bf16[32,528,128]{2,1,0:T(8,128)(2,1)} %own.1), calls=%async_computation | async-start | bytes 8650752 | tf_op jit(solution)/shard_map/all_to_all | solution.py:354
  16.9 24.6 %copy-start.2 = (s32[512]{0:T(512)S(1)}, s32[512]{0:T(512)}, u32[]{:S(2)}) copy-start(s32[512]{0:T(512)} %refs_0_.5) | copy-start | bytes 6148
  69.9 59.0 %copy-start.1 = (bf16[2048,1024]{1,0:T(8,128)(2,1)S(1)}, bf16[2048,1024]{1,0:T(8,128)(2,1)}, u32[]{:S(2)}) copy-start(bf16[2048,1024]{1,0:T(8,128)(2,1)} %get-tuple-element.14.refs_2_) | copy-start | bytes 12582916
  74.6 54.3 %copy-start = (f32[2048,1024]{1,0:T(8,128)S(1)}, f32[2048,1024]{1,0:T(8,128)}, u32[]{:S(2)}) copy-start(f32[2048,1024]{1,0:T(8,128)} %get-tuple-element.15.refs_3_) | copy-start | bytes 25165828
  235.1 10.4 %copy-start.3 = (f32[1024]{0:T(1024)S(1)}, f32[1024]{0:T(1024)}, u32[]{:S(2)}) copy-start(f32[1024]{0:T(1024)} %param.11) | copy-start | bytes 12292
  236.3 5.5 %collective-permute-start.2 = (f32[16,128]{1,0:T(8,128)S(1)}, f32[16,128]{1,0:T(8,128)S(1)}, u32[]{:S(2)}, u32[]{:S(2)}) collective-permute-start(f32[16,128]{1,0:T(8,128)S(1)} %squares.1.refs_2_), channel_id=1, source_target_pairs={{0,3},{1,0},{2,1},{3,2},{4,7},{5,4},{6,5},{7,6},{8,11},{9,8},{10,9... | collective-permute-start | bytes 24584 | tf_op jit(solution)/shard_map/ppermute | solution.py:378
  240.4 5.2 %collective-permute-start.1 = (f32[16,128]{1,0:T(8,128)S(1)}, f32[16,128]{1,0:T(8,128)S(1)}, u32[]{:S(2)}, u32[]{:S(2)}) collective-permute-start(f32[16,128]{1,0:T(8,128)S(1)} %squares.1.refs_2_), channel_id=1, source_target_pairs={{0,2},{1,3},{2,0},{3,1},{4,6},{5,7},{6,4},{7,5},{8,10},{9,11},{10,... | collective-permute-start | bytes 24584 | tf_op jit(solution)/shard_map/ppermute | solution.py:378
  240.4 5.2 %collective-permute-start = (f32[16,128]{1,0:T(8,128)S(1)}, f32[16,128]{1,0:T(8,128)S(1)}, u32[]{:S(2)}, u32[]{:S(2)}) collective-permute-start(f32[16,128]{1,0:T(8,128)S(1)} %squares.1.refs_2_), channel_id=1, source_target_pairs={{0,1},{1,2},{2,3},{3,0},{4,5},{5,6},{6,7},{7,4},{8,9},{9,10},{10,1... | collective-permute-start | bytes 24584 | tf_op jit(solution)/shard_map/ppermute | solution.py:378

commit v6 on v5

--- a/solution.py
+++ b/solution.py
@@ -7,8 +7,9 @@
 
 BLOCK = 128
 EXTRA = 16
+TAIL = 8
 FAR = 1e9
-OWN_EACH = 4
+OWN_EACH = 8
 OUTGO_EACH = 4
 FINISH_EACH = 8
 F32 = jnp.float32
@@ -42,7 +43,7 @@
     )[:1]
 
 
-def own_kernel(heads, blocks, each, packing, place, lengths, keys, values, decay, own, made, fates, sems):
+def own_kernel(heads, blocks, each, packing, place, lengths, keys, values, decay, own, made, fates, faded, sems):
     step = pl.program_id(0)
     per_head = made.shape[0] // heads
     pieces = BLOCK // per_head
@@ -50,6 +51,7 @@
     upper = triangle(True)
     starts = start_row(lengths[...])
     lane = lax.broadcasted_iota(jnp.int32, (1, BLOCK), 1).astype(F32)
+    keeps = []
     for inside in range(each):
         block = step * each + inside
         rows = slice(inside * BLOCK, (inside + 1) * BLOCK)
@@ -58,15 +60,30 @@
         total = logs[:, BLOCK - 1 :]
         begun = jnp.where(starts <= base + (BLOCK - 1), starts, -FAR)
         started = jnp.max(begun, axis=1, keepdims=True)
-        keep = jnp.exp(total - logs) * jnp.where(lane + base >= started, 1.0, 0.0)
+        keeps.append(jnp.exp(total - logs) * jnp.where(lane + base >= started, 1.0, 0.0))
         gate = jnp.exp(total) * jnp.where(started < base, 1.0, 0.0)
-        to = pl.ds(pl.multiple_of(block * pieces, pieces), pieces)
         for head in range(heads):
-            span = slice(head * BLOCK, (head + 1) * BLOCK)
-            faded = keys[rows, span].T.astype(F32) * keep[head : head + 1, :]
-            state = dot(faded.astype(BF16), values[rows, span], (1, 0)).astype(BF16)
-            made[head * per_head : (head + 1) * per_head, to] = state.reshape(per_head, pieces, BLOCK)
             fates[head, pl.ds(block, 1), :] = jnp.broadcast_to(gate[head : head + 1, :], (1, BLOCK))
+
+    def fade(inside, head):
+        rows = slice(inside * BLOCK, (inside + 1) * BLOCK)
+        span = slice(head * BLOCK, (head + 1) * BLOCK)
+        turned = keys[rows, span].T.astype(F32) * keeps[inside][head : head + 1, :]
+        faded[inside, head] = turned.astype(BF16)
+
+    def multiply(inside, head):
+        rows = slice(inside * BLOCK, (inside + 1) * BLOCK)
+        span = slice(head * BLOCK, (head + 1) * BLOCK)
+        state = dot(faded[inside, head], values[rows, span], (1, 0)).astype(BF16)
+        to = pl.ds(pl.multiple_of((step * each + inside) * pieces, pieces), pieces)
+        made[head * per_head : (head + 1) * per_head, to] = state.reshape(per_head, pieces, BLOCK)
+
+    for inside in range(each + 1):
+        for head in range(heads):
+            if inside < each:
+                fade(inside, head)
+            if inside:
+                multiply(inside - 1, head)
 
     def copy(at, start, size):
         part = (slice(None), pl.ds(start, size))
@@ -113,6 +130,7 @@
             scratch_shapes=[
                 pltpu.VMEM(shape, BF16),
                 pltpu.VMEM((heads, blocks, BLOCK), F32),
+                pltpu.VMEM((each, heads, BLOCK, BLOCK), BF16),
                 pltpu.SemaphoreType.DMA((blocks // each + 1,)),
             ],
         ),
@@ -213,7 +231,7 @@
     step = pl.program_id(0)
     per_head = states.shape[0] // heads
     pieces = BLOCK // per_head
-    row = lax.broadcasted_iota(jnp.int32, (EXTRA, BLOCK), 0)
+    row = lax.broadcasted_iota(jnp.int32, (TAIL, BLOCK), 0)
 
     def copy(block):
         owner = packing[place[0] * blocks + block] // blocks
@@ -262,11 +280,11 @@
             ],
             out_specs=pl.BlockSpec(memory_space=pl.ANY),
             scratch_shapes=[
-                pltpu.VMEM((blocks, width + EXTRA, BLOCK), BF16),
+                pltpu.VMEM((blocks, width + TAIL, BLOCK), BF16),
                 pltpu.SemaphoreType.DMA((blocks,)),
             ],
         ),
-        out_shape=jax.ShapeDtypeStruct((devices, width + EXTRA, BLOCK), BF16),
+        out_shape=jax.ShapeDtypeStruct((devices, width + TAIL, BLOCK), BF16),
         compiler_params=pltpu.CompilerParams(vmem_limit_bytes=18 * 2**20),
         name="outgo",
     )(packing, place, faded, intra, states)
@@ -297,7 +315,7 @@
         out_specs=pl.BlockSpec(memory_space=pltpu.VMEM),
         out_shape=jax.ShapeDtypeStruct((blocks, BLOCK), F32),
         scratch_shapes=[
-            pltpu.VMEM((blocks, EXTRA, BLOCK), BF16),
+            pltpu.VMEM((blocks, TAIL, BLOCK), BF16),
             pltpu.SemaphoreType.DMA((blocks,)),
         ],
         compiler_params=pltpu.CompilerParams(vmem_limit_bytes=2 * 2**20),
@@ -368,7 +386,9 @@
     intra, faded = intra_pass(packing, place, lengths, queries, key_rows, value_rows, decay)
 
     own, order, intra, faded = lax.optimization_barrier((own, order, intra, faded))
-    states = swap(scan_pass(order, own), "ctx")
+    prior = scan_pass(order, own)
+    prior, intra, faded = lax.optimization_barrier((prior, intra, faded))
+    states = swap(prior, "ctx")
     came = swap(outgo_pass(packing, place, faded, intra, states), "ctx")
     part = squares_pass(order, place, came)
     groups = lax.axis_size("head")

time: 251 us -> 248 us (0.988)
  Pallas kernels: 46.9 us -> 44.1 us
    pallas_call x1, Pallas kernels: 9.37 us -> 6.79 us  [own_states(): pl.pallas_call(lambda *refs: own_kernel(heads, blocks, each, *refs), grid...]
where the time goes in v6:
time: 248 us; the launch traced here: 245 us
  blocking collectives  156 us (63%)
  Pallas kernels  44.1 us (18%)
  waiting for transfers between devices  32.1 us (13%)
  starting transfers between devices  12.9 us (5%)
    all_to_all x2, blocking collectives, swap(): return lax.all_to_all(x, axis, split_axis=0, concat_axis=0, tiled=True)  156 us
    all_to_all x1, waiting for transfers between devices, swap(): return lax.all_to_all(x, axis, split_axis=0, concat_axis=0, tiled=True)  28.2 us
    pallas_call x1, Pallas kernels, intra_pass(): pl.pallas_call(lambda *refs: intra_kernel(heads, *refs), grid_spec=pltpu....  24.6 us
    all_to_all x1, starting transfers between devices, swap(): return lax.all_to_all(x, axis, split_axis=0, concat_axis=0, tiled=True)  7.49 us
    pallas_call x1, Pallas kernels, own_states(): pl.pallas_call(lambda *refs: own_kernel(heads, blocks, each, *refs), grid...  6.79 us
    ppermute x3, starting transfers between devices, body(): squares.append(lax.ppermute(part, 'head', pairs))  5.36 us
  transfers between devices with their start and end apart: 4, of which 3 were waited for; matrix products, arithmetic and copies ran while one was open for 0% of the time, Pallas kernels for 10%

profile of v6, /device:TPU:16, one launch (start us, length us, event | category | flops | bytes accessed | tf_op | source)
XLA Modules:
  0.0 245.5 jit_solution(4047039131272836193)
XLA Ops:
  0.0 6.8 %own.1 = bf16[32,528,128]{2,1,0:T(8,128)(2,1)} custom-call(s32[512]{0:T(512)} %refs_0_.5, s32[1]{0:T(128)} %bitcast.refs_1_.place, s32[1,64]{1,0:T(1,128)} %bitcast.10, bf16[2048,1024]{1,0:T(8,128)(2,1)} %refs_4_.3, bf16[2048,1024]{1,0:T(8,128)(2,1)} %refs_5_.1, bf16[8,2048]{1,0:T(8,128)(2,1)} %bitcast.8), custom_call_target="tpu_custom_call" | custom-call | tf_op jit(solution)/shard_map/own/pallas_call | solution.py:118
  6.8 7.5 %all-to-all-start = ((bf16[32,528,128]{2,1,0:T(8,128)(2,1)}), bf16[32,528,128]{2,1,0:T(8,128)(2,1)}, u32[]{:S(2)}, u32[]{:S(2)}) async-start(bf16[32,528,128]{2,1,0:T(8,128)(2,1)} %own.1), calls=%async_computation | async-start | bytes 8650752 | tf_op jit(solution)/shard_map/all_to_all | solution.py:372
  14.3 0.0 copy-start.2
  14.3 24.6 %intra.1 = (f32[2048,1024]{1,0:T(8,128)}, bf16[2048,1024]{1,0:T(8,128)(2,1)}) custom-call(s32[512]{0:T(512)} %refs_0_.5, s32[1]{0:T(128)} %bitcast.refs_1_.place, s32[1,64]{1,0:T(1,128)} %bitcast.11, bf16[2048,1024]{1,0:T(8,128)(2,1)} %refs_3_.3, bf16[2048,1024]{1,0:T(8,128)(2,1)} %refs_4_.3, bf16[2048,1024]{1,0:T(8,128)(2,1)} %refs_5_.1, ...), custom_call_target="tpu_custom_call" | custom-call | tf_op jit(solution)/shard_map/intra/pallas_call | solution.py:168
  38.9 0.0 copy-done.2
  38.9 0.2 select_reduce_fusion.refs_0_.order
  39.1 28.2 %all-to-all-done = bf16[32,528,128]{2,1,0:T(8,128)(2,1)} async-done(((bf16[32,528,128]{2,1,0:T(8,128)(2,1)}), bf16[32,528,128]{2,1,0:T(8,128)(2,1)}, u32[]{:S(2)}, u32[]{:S(2)}) %all-to-all-start) | async-done | bytes 4325408 | tf_op jit(solution)/shard_map/all_to_all | solution.py:372
  67.3 0.0 copy-start.1
  67.3 4.7 %scan.1 = bf16[1024,16,128]{2,1,0:T(8,128)(2,1)S(1)} custom-call(s32[512]{0:T(512)S(1)} %select_reduce_fusion.refs_0_.order, bf16[1056,16,128]{2,1,0:T(8,128)(2,1)} %bitcast.3.refs_1_), custom_call_target="tpu_custom_call" | custom-call | tf_op jit(solution)/shard_map/scan/pallas_call | solution.py:218
  72.0 0.0 copy-start
  72.0 54.3 %all_to_all.15.refs_4_ = bf16[32,512,128]{2,1,0:T(8,128)(2,1)S(1)} all-to-all(bf16[32,512,128]{2,1,0:T(8,128)(2,1)S(1)} %bitcast.6), channel_id=1, replica_groups=mesh['ctx'=32,'head'=4] {'ctx'}, dimensions={0} | all-to-all | bytes 8388608 | tf_op jit(solution)/shard_map/all_to_all | solution.py:372
  126.3 0.0 copy-done.1
  126.3 0.0 copy-done
  126.3 3.8 %outgo.1 = bf16[32,1032,128]{2,1,0:T(8,128)(2,1)S(1)} custom-call(s32[512]{0:T(512)S(1)} %copy-done.2, s32[1]{0:T(128)} %bitcast.refs_1_.place, bf16[2048,1024]{1,0:T(8,128)(2,1)S(1)} %copy-done.1, f32[2048,1024]{1,0:T(8,128)S(1)} %copy-done, bf16[32,512,128]{2,1,0:T(8,128)(2,1)S(1)} %all_to_all.15.refs_4_), custom_call_target="tpu_custom_call" | custom-call | tf_op jit(solution)/shard_map/outgo/pallas_call | solution.py:271
  130.1 101.8 %all_to_all.16.came.refs_7_.refs_8_.refs_9_.refs_10_.refs_11_.refs_12_.refs_13_.refs_14_ = bf16[32,1032,128]{2,1,0:T(8,128)(2,1)S(1)} all-to-all(bf16[32,1032,128]{2,1,0:T(8,128)(2,1)S(1)} %outgo.1), channel_id=1, replica_groups=mesh['ctx'=32,'head'=4] {'ctx'}, dimensions={0} | all-to-all | bytes 16908288 | tf_op jit(solution)/shard_map/all_to_all | solution.py:372
  232.0 0.0 copy-start.3
  232.0 1.0 squares.1.refs_2_
  233.0 4.1 %collective-permute-start.2 = (f32[16,128]{1,0:T(8,128)S(1)}, f32[16,128]{1,0:T(8,128)S(1)}, u32[]{:S(2)}, u32[]{:S(2)}) collective-permute-start(f32[16,128]{1,0:T(8,128)S(1)} %squares.1.refs_2_), channel_id=1, source_target_pairs={{0,3},{1,0},{2,1},{3,2},{4,7},{5,4},{6,5},{7,6},{8,11},{9,8},{10,9... | collective-permute-start | bytes 24584 | tf_op jit(solution)/shard_map/ppermute | solution.py:398
  237.1 0.0 collective-permute-start.1
  237.1 1.3 collective-permute-start
  238.4 0.1 collective-permute-done.2.refs_5_
  238.5 3.8 %collective-permute-done.1.refs_4_ = f32[16,128]{1,0:T(8,128)S(1)} collective-permute-done((f32[16,128]{1,0:T(8,128)S(1)}, f32[16,128]{1,0:T(8,128)S(1)}, u32[]{:S(2)}, u32[]{:S(2)}) %collective-permute-start.1) | collective-permute-done | bytes 8224 | tf_op jit(solution)/shard_map/ppermute | solution.py:398
  242.2 0.0 collective-permute-done.refs_3_
  242.3 0.0 copy-done.3
  242.3 3.2 %finish.1 = bf16[2048,1024]{1,0:T(8,128)(2,1)} custom-call(s32[512]{0:T(512)S(1)} %select_reduce_fusion.refs_0_.order, s32[1]{0:T(128)} %bitcast.refs_1_.place, f32[16,128]{1,0:T(8,128)S(1)} %squares.1.refs_2_, f32[16,128]{1,0:T(8,128)S(1)} %collective-permute-done.refs_3_, f32[16,128]{1,0:T(8,128)S(1)} %collective-permute-done.1.refs_4_, ...), custom_call_target="tpu_custom_call" | custom-call | tf_op jit(solution)/shard_map/finish/pallas_call | solution.py:355
Async XLA Ops:
  6.8 60.5 %all-to-all-start = ((bf16[32,528,128]{2,1,0:T(8,128)(2,1)}), bf16[32,528,128]{2,1,0:T(8,128)(2,1)}, u32[]{:S(2)}, u32[]{:S(2)}) async-start(bf16[32,528,128]{2,1,0:T(8,128)(2,1)} %own.1), calls=%async_computation | async-start | bytes 8650752 | tf_op jit(solution)/shard_map/all_to_all | solution.py:372
  14.3 24.6 %copy-start.2 = (s32[512]{0:T(512)S(1)}, s32[512]{0:T(512)}, u32[]{:S(2)}) copy-start(s32[512]{0:T(512)} %refs_0_.5) | copy-start | bytes 6148
  67.3 59.0 %copy-start.1 = (bf16[2048,1024]{1,0:T(8,128)(2,1)S(1)}, bf16[2048,1024]{1,0:T(8,128)(2,1)}, u32[]{:S(2)}) copy-start(bf16[2048,1024]{1,0:T(8,128)(2,1)} %get-tuple-element.20.refs_2_) | copy-start | bytes 12582916
  72.0 54.3 %copy-start = (f32[2048,1024]{1,0:T(8,128)S(1)}, f32[2048,1024]{1,0:T(8,128)}, u32[]{:S(2)}) copy-start(f32[2048,1024]{1,0:T(8,128)} %get-tuple-element.21.refs_3_) | copy-start | bytes 25165828
  232.0 10.3 %copy-start.3 = (f32[1024]{0:T(1024)S(1)}, f32[1024]{0:T(1024)}, u32[]{:S(2)}) copy-start(f32[1024]{0:T(1024)} %param.11) | copy-start | bytes 12292
  233.0 5.5 %collective-permute-start.2 = (f32[16,128]{1,0:T(8,128)S(1)}, f32[16,128]{1,0:T(8,128)S(1)}, u32[]{:S(2)}, u32[]{:S(2)}) collective-permute-start(f32[16,128]{1,0:T(8,128)S(1)} %squares.1.refs_2_), channel_id=1, source_target_pairs={{0,3},{1,0},{2,1},{3,2},{4,7},{5,4},{6,5},{7,6},{8,11},{9,8},{10,9... | collective-permute-start | bytes 24584 | tf_op jit(solution)/shard_map/ppermute | solution.py:398
  237.1 5.2 %collective-permute-start.1 = (f32[16,128]{1,0:T(8,128)S(1)}, f32[16,128]{1,0:T(8,128)S(1)}, u32[]{:S(2)}, u32[]{:S(2)}) collective-permute-start(f32[16,128]{1,0:T(8,128)S(1)} %squares.1.refs_2_), channel_id=1, source_target_pairs={{0,2},{1,3},{2,0},{3,1},{4,6},{5,7},{6,4},{7,5},{8,10},{9,11},{10,... | collective-permute-start | bytes 24584 | tf_op jit(solution)/shard_map/ppermute | solution.py:398
  237.1 5.2 %collective-permute-start = (f32[16,128]{1,0:T(8,128)S(1)}, f32[16,128]{1,0:T(8,128)S(1)}, u32[]{:S(2)}, u32[]{:S(2)}) collective-permute-start(f32[16,128]{1,0:T(8,128)S(1)} %squares.1.refs_2_), channel_id=1, source_target_pairs={{0,1},{1,2},{2,3},{3,0},{4,5},{5,6},{6,7},{7,4},{8,9},{9,10},{10,1... | collective-permute-start | bytes 24584 | tf_op jit(solution)/shard_map/ppermute | solution.py:398

commit v7 on v6

--- a/solution.py
+++ b/solution.py
@@ -10,7 +10,7 @@
 TAIL = 8
 FAR = 1e9
 OWN_EACH = 8
-OUTGO_EACH = 4
+OUTGO_EACH = 8
 FINISH_EACH = 8
 F32 = jnp.float32
 BF16 = jnp.bfloat16
@@ -285,7 +285,7 @@
             ],
         ),
         out_shape=jax.ShapeDtypeStruct((devices, width + TAIL, BLOCK), BF16),
-        compiler_params=pltpu.CompilerParams(vmem_limit_bytes=18 * 2**20),
+        compiler_params=pltpu.CompilerParams(vmem_limit_bytes=24 * 2**20),
         name="outgo",
     )(packing, place, faded, intra, states)
 

time: 248 us -> 247 us (level)
  no operation moved by 1% of the time
where the time goes in v7:
time: 247 us; the launch traced here: 245 us
  blocking collectives  156 us (63%)
  Pallas kernels  43.7 us (18%)
  waiting for transfers between devices  32.1 us (13%)
  starting transfers between devices  12.8 us (5%)
    all_to_all x2, blocking collectives, swap(): return lax.all_to_all(x, axis, split_axis=0, concat_axis=0, tiled=True)  156 us
    all_to_all x1, waiting for transfers between devices, swap(): return lax.all_to_all(x, axis, split_axis=0, concat_axis=0, tiled=True)  28.2 us
    pallas_call x1, Pallas kernels, intra_pass(): pl.pallas_call(lambda *refs: intra_kernel(heads, *refs), grid_spec=pltpu....  24.6 us
    all_to_all x1, starting transfers between devices, swap(): return lax.all_to_all(x, axis, split_axis=0, concat_axis=0, tiled=True)  7.49 us
    pallas_call x1, Pallas kernels, own_states(): pl.pallas_call(lambda *refs: own_kernel(heads, blocks, each, *refs), grid...  6.79 us
    ppermute x3, starting transfers between devices, body(): squares.append(lax.ppermute(part, 'head', pairs))  5.36 us
  transfers between devices with their start and end apart: 4, of which 3 were waited for; matrix products, arithmetic and copies ran while one was open for 0% of the time, Pallas kernels for 10%

profile of v7, /device:TPU:16, one launch (start us, length us, event | category | flops | bytes accessed | tf_op | source)
XLA Modules:
  0.0 245.0 jit_solution(8528572666019754478)
XLA Ops:
  0.0 6.8 %own.1 = bf16[32,528,128]{2,1,0:T(8,128)(2,1)} custom-call(s32[512]{0:T(512)} %refs_0_.5, s32[1]{0:T(128)} %bitcast.refs_1_.place, s32[1,64]{1,0:T(1,128)} %bitcast.10, bf16[2048,1024]{1,0:T(8,128)(2,1)} %refs_4_.3, bf16[2048,1024]{1,0:T(8,128)(2,1)} %refs_5_.1, bf16[8,2048]{1,0:T(8,128)(2,1)} %bitcast.8), custom_call_target="tpu_custom_call" | custom-call | tf_op jit(solution)/shard_map/own/pallas_call | solution.py:118
  6.8 7.5 %all-to-all-start = ((bf16[32,528,128]{2,1,0:T(8,128)(2,1)}), bf16[32,528,128]{2,1,0:T(8,128)(2,1)}, u32[]{:S(2)}, u32[]{:S(2)}) async-start(bf16[32,528,128]{2,1,0:T(8,128)(2,1)} %own.1), calls=%async_computation | async-start | bytes 8650752 | tf_op jit(solution)/shard_map/all_to_all | solution.py:372
  14.3 0.0 copy-start.2
  14.3 24.6 %intra.1 = (f32[2048,1024]{1,0:T(8,128)}, bf16[2048,1024]{1,0:T(8,128)(2,1)}) custom-call(s32[512]{0:T(512)} %refs_0_.5, s32[1]{0:T(128)} %bitcast.refs_1_.place, s32[1,64]{1,0:T(1,128)} %bitcast.11, bf16[2048,1024]{1,0:T(8,128)(2,1)} %refs_3_.3, bf16[2048,1024]{1,0:T(8,128)(2,1)} %refs_4_.3, bf16[2048,1024]{1,0:T(8,128)(2,1)} %refs_5_.1, ...), custom_call_target="tpu_custom_call" | custom-call | tf_op jit(solution)/shard_map/intra/pallas_call | solution.py:168
  38.9 0.0 copy-done.2
  38.9 0.2 select_reduce_fusion.refs_0_.order
  39.1 28.2 %all-to-all-done = bf16[32,528,128]{2,1,0:T(8,128)(2,1)} async-done(((bf16[32,528,128]{2,1,0:T(8,128)(2,1)}), bf16[32,528,128]{2,1,0:T(8,128)(2,1)}, u32[]{:S(2)}, u32[]{:S(2)}) %all-to-all-start) | async-done | bytes 4325408 | tf_op jit(solution)/shard_map/all_to_all | solution.py:372
  67.3 0.0 copy-start.1
  67.3 4.7 %scan.1 = bf16[1024,16,128]{2,1,0:T(8,128)(2,1)S(1)} custom-call(s32[512]{0:T(512)S(1)} %select_reduce_fusion.refs_0_.order, bf16[1056,16,128]{2,1,0:T(8,128)(2,1)} %bitcast.3.refs_1_), custom_call_target="tpu_custom_call" | custom-call | tf_op jit(solution)/shard_map/scan/pallas_call | solution.py:218
  72.0 0.0 copy-start
  72.0 54.3 %all_to_all.15.refs_4_ = bf16[32,512,128]{2,1,0:T(8,128)(2,1)S(1)} all-to-all(bf16[32,512,128]{2,1,0:T(8,128)(2,1)S(1)} %bitcast.6), channel_id=1, replica_groups=mesh['ctx'=32,'head'=4] {'ctx'}, dimensions={0} | all-to-all | bytes 8388608 | tf_op jit(solution)/shard_map/all_to_all | solution.py:372
  126.3 0.0 copy-done.1
  126.3 0.0 copy-done
  126.3 3.4 %outgo.1 = bf16[32,1032,128]{2,1,0:T(8,128)(2,1)S(1)} custom-call(s32[512]{0:T(512)S(1)} %copy-done.2, s32[1]{0:T(128)} %bitcast.refs_1_.place, bf16[2048,1024]{1,0:T(8,128)(2,1)S(1)} %copy-done.1, f32[2048,1024]{1,0:T(8,128)S(1)} %copy-done, bf16[32,512,128]{2,1,0:T(8,128)(2,1)S(1)} %all_to_all.15.refs_4_), custom_call_target="tpu_custom_call" | custom-call | tf_op jit(solution)/shard_map/outgo/pallas_call | solution.py:271
  129.7 101.8 %all_to_all.16.came.refs_7_.refs_8_.refs_9_.refs_10_.refs_11_.refs_12_.refs_13_.refs_14_ = bf16[32,1032,128]{2,1,0:T(8,128)(2,1)S(1)} all-to-all(bf16[32,1032,128]{2,1,0:T(8,128)(2,1)S(1)} %outgo.1), channel_id=1, replica_groups=mesh['ctx'=32,'head'=4] {'ctx'}, dimensions={0} | all-to-all | bytes 16908288 | tf_op jit(solution)/shard_map/all_to_all | solution.py:372
  231.5 0.0 copy-start.3
  231.5 1.0 squares.1.refs_2_
  232.5 4.1 %collective-permute-start.2 = (f32[16,128]{1,0:T(8,128)S(1)}, f32[16,128]{1,0:T(8,128)S(1)}, u32[]{:S(2)}, u32[]{:S(2)}) collective-permute-start(f32[16,128]{1,0:T(8,128)S(1)} %squares.1.refs_2_), channel_id=1, source_target_pairs={{0,3},{1,0},{2,1},{3,2},{4,7},{5,4},{6,5},{7,6},{8,11},{9,8},{10,9... | collective-permute-start | bytes 24584 | tf_op jit(solution)/shard_map/ppermute | solution.py:398
  236.6 0.0 collective-permute-start.1
  236.6 1.3 collective-permute-start
  237.9 0.1 collective-permute-done.2.refs_5_
  238.0 3.8 %collective-permute-done.1.refs_4_ = f32[16,128]{1,0:T(8,128)S(1)} collective-permute-done((f32[16,128]{1,0:T(8,128)S(1)}, f32[16,128]{1,0:T(8,128)S(1)}, u32[]{:S(2)}, u32[]{:S(2)}) %collective-permute-start.1) | collective-permute-done | bytes 8224 | tf_op jit(solution)/shard_map/ppermute | solution.py:398
  241.8 0.0 collective-permute-done.refs_3_
  241.8 0.0 copy-done.3
  241.8 3.2 %finish.1 = bf16[2048,1024]{1,0:T(8,128)(2,1)} custom-call(s32[512]{0:T(512)S(1)} %select_reduce_fusion.refs_0_.order, s32[1]{0:T(128)} %bitcast.refs_1_.place, f32[16,128]{1,0:T(8,128)S(1)} %squares.1.refs_2_, f32[16,128]{1,0:T(8,128)S(1)} %collective-permute-done.refs_3_, f32[16,128]{1,0:T(8,128)S(1)} %collective-permute-done.1.refs_4_, ...), custom_call_target="tpu_custom_call" | custom-call | tf_op jit(solution)/shard_map/finish/pallas_call | solution.py:355
Async XLA Ops:
  6.8 60.5 %all-to-all-start = ((bf16[32,528,128]{2,1,0:T(8,128)(2,1)}), bf16[32,528,128]{2,1,0:T(8,128)(2,1)}, u32[]{:S(2)}, u32[]{:S(2)}) async-start(bf16[32,528,128]{2,1,0:T(8,128)(2,1)} %own.1), calls=%async_computation | async-start | bytes 8650752 | tf_op jit(solution)/shard_map/all_to_all | solution.py:372
  14.3 24.6 %copy-start.2 = (s32[512]{0:T(512)S(1)}, s32[512]{0:T(512)}, u32[]{:S(2)}) copy-start(s32[512]{0:T(512)} %refs_0_.5) | copy-start | bytes 6148
  67.3 59.0 %copy-start.1 = (bf16[2048,1024]{1,0:T(8,128)(2,1)S(1)}, bf16[2048,1024]{1,0:T(8,128)(2,1)}, u32[]{:S(2)}) copy-start(bf16[2048,1024]{1,0:T(8,128)(2,1)} %get-tuple-element.20.refs_2_) | copy-start | bytes 12582916
  72.0 54.3 %copy-start = (f32[2048,1024]{1,0:T(8,128)S(1)}, f32[2048,1024]{1,0:T(8,128)}, u32[]{:S(2)}) copy-start(f32[2048,1024]{1,0:T(8,128)} %get-tuple-element.21.refs_3_) | copy-start | bytes 25165828
  231.5 10.3 %copy-start.3 = (f32[1024]{0:T(1024)S(1)}, f32[1024]{0:T(1024)}, u32[]{:S(2)}) copy-start(f32[1024]{0:T(1024)} %param.11) | copy-start | bytes 12292
  232.5 5.5 %collective-permute-start.2 = (f32[16,128]{1,0:T(8,128)S(1)}, f32[16,128]{1,0:T(8,128)S(1)}, u32[]{:S(2)}, u32[]{:S(2)}) collective-permute-start(f32[16,128]{1,0:T(8,128)S(1)} %squares.1.refs_2_), channel_id=1, source_target_pairs={{0,3},{1,0},{2,1},{3,2},{4,7},{5,4},{6,5},{7,6},{8,11},{9,8},{10,9... | collective-permute-start | bytes 24584 | tf_op jit(solution)/shard_map/ppermute | solution.py:398
  236.6 5.2 %collective-permute-start.1 = (f32[16,128]{1,0:T(8,128)S(1)}, f32[16,128]{1,0:T(8,128)S(1)}, u32[]{:S(2)}, u32[]{:S(2)}) collective-permute-start(f32[16,128]{1,0:T(8,128)S(1)} %squares.1.refs_2_), channel_id=1, source_target_pairs={{0,2},{1,3},{2,0},{3,1},{4,6},{5,7},{6,4},{7,5},{8,10},{9,11},{10,... | collective-permute-start | bytes 24584 | tf_op jit(solution)/shard_map/ppermute | solution.py:398
  236.6 5.2 %collective-permute-start = (f32[16,128]{1,0:T(8,128)S(1)}, f32[16,128]{1,0:T(8,128)S(1)}, u32[]{:S(2)}, u32[]{:S(2)}) collective-permute-start(f32[16,128]{1,0:T(8,128)S(1)} %squares.1.refs_2_), channel_id=1, source_target_pairs={{0,1},{1,2},{2,3},{3,0},{4,5},{5,6},{6,7},{7,4},{8,9},{9,10},{10,1... | collective-permute-start | bytes 24584 | tf_op jit(solution)/shard_map/ppermute | solution.py:398

commit v8 on v6

--- a/solution.py
+++ b/solution.py
@@ -207,7 +207,7 @@
         return tuple(after)
 
     zero = jnp.zeros(own.shape[1:], F32)
-    lax.fori_loop(0, devices * blocks, step, (zero,) * parts, unroll=16)
+    lax.fori_loop(0, devices * blocks, step, (zero,) * parts, unroll=32)
 
 
 def scan_pass(order, own):

time: 248 us -> 248 us (level)
  no operation moved by 1% of the time
where the time goes in v8:
time: 248 us; the launch traced here: 246 us
  blocking collectives  156 us (63%)
  Pallas kernels  44.2 us (18%)
  waiting for transfers between devices  32.1 us (13%)
  starting transfers between devices  12.9 us (5%)
    all_to_all x2, blocking collectives, swap(): return lax.all_to_all(x, axis, split_axis=0, concat_axis=0, tiled=True)  156 us
    all_to_all x1, waiting for transfers between devices, swap(): return lax.all_to_all(x, axis, split_axis=0, concat_axis=0, tiled=True)  28.2 us
    pallas_call x1, Pallas kernels, intra_pass(): pl.pallas_call(lambda *refs: intra_kernel(heads, *refs), grid_spec=pltpu....  24.6 us
    all_to_all x1, starting transfers between devices, swap(): return lax.all_to_all(x, axis, split_axis=0, concat_axis=0, tiled=True)  7.49 us
    pallas_call x1, Pallas kernels, own_states(): pl.pallas_call(lambda *refs: own_kernel(heads, blocks, each, *refs), grid...  6.79 us
    ppermute x3, starting transfers between devices, body(): squares.append(lax.ppermute(part, 'head', pairs))  5.37 us
  transfers between devices with their start and end apart: 4, of which 3 were waited for; matrix products, arithmetic and copies ran while one was open for 0% of the time, Pallas kernels for 10%

profile of v8, /device:TPU:16, one launch (start us, length us, event | category | flops | bytes accessed | tf_op | source)
XLA Modules:
  0.0 245.6 jit_solution(11383071078157688122)
XLA Ops:
  0.0 6.8 %own.1 = bf16[32,528,128]{2,1,0:T(8,128)(2,1)} custom-call(s32[512]{0:T(512)} %refs_0_.5, s32[1]{0:T(128)} %bitcast.refs_1_.place, s32[1,64]{1,0:T(1,128)} %bitcast.10, bf16[2048,1024]{1,0:T(8,128)(2,1)} %refs_4_.3, bf16[2048,1024]{1,0:T(8,128)(2,1)} %refs_5_.1, bf16[8,2048]{1,0:T(8,128)(2,1)} %bitcast.8), custom_call_target="tpu_custom_call" | custom-call | tf_op jit(solution)/shard_map/own/pallas_call | solution.py:118
  6.8 7.5 %all-to-all-start = ((bf16[32,528,128]{2,1,0:T(8,128)(2,1)}), bf16[32,528,128]{2,1,0:T(8,128)(2,1)}, u32[]{:S(2)}, u32[]{:S(2)}) async-start(bf16[32,528,128]{2,1,0:T(8,128)(2,1)} %own.1), calls=%async_computation | async-start | bytes 8650752 | tf_op jit(solution)/shard_map/all_to_all | solution.py:372
  14.3 0.0 copy-start.2
  14.3 24.6 %intra.1 = (f32[2048,1024]{1,0:T(8,128)}, bf16[2048,1024]{1,0:T(8,128)(2,1)}) custom-call(s32[512]{0:T(512)} %refs_0_.5, s32[1]{0:T(128)} %bitcast.refs_1_.place, s32[1,64]{1,0:T(1,128)} %bitcast.11, bf16[2048,1024]{1,0:T(8,128)(2,1)} %refs_3_.3, bf16[2048,1024]{1,0:T(8,128)(2,1)} %refs_4_.3, bf16[2048,1024]{1,0:T(8,128)(2,1)} %refs_5_.1, ...), custom_call_target="tpu_custom_call" | custom-call | tf_op jit(solution)/shard_map/intra/pallas_call | solution.py:168
  38.9 0.0 copy-done.2
  38.9 0.2 select_reduce_fusion.refs_0_.order
  39.1 28.2 %all-to-all-done = bf16[32,528,128]{2,1,0:T(8,128)(2,1)} async-done(((bf16[32,528,128]{2,1,0:T(8,128)(2,1)}), bf16[32,528,128]{2,1,0:T(8,128)(2,1)}, u32[]{:S(2)}, u32[]{:S(2)}) %all-to-all-start) | async-done | bytes 4325408 | tf_op jit(solution)/shard_map/all_to_all | solution.py:372
  67.3 0.0 copy-start.1
  67.3 4.7 %scan.1 = bf16[1024,16,128]{2,1,0:T(8,128)(2,1)S(1)} custom-call(s32[512]{0:T(512)S(1)} %select_reduce_fusion.refs_0_.order, bf16[1056,16,128]{2,1,0:T(8,128)(2,1)} %bitcast.3.refs_1_), custom_call_target="tpu_custom_call" | custom-call | tf_op jit(solution)/shard_map/scan/pallas_call | solution.py:218
  72.0 0.0 copy-start
  72.1 54.3 %all_to_all.15.refs_4_ = bf16[32,512,128]{2,1,0:T(8,128)(2,1)S(1)} all-to-all(bf16[32,512,128]{2,1,0:T(8,128)(2,1)S(1)} %bitcast.6), channel_id=1, replica_groups=mesh['ctx'=32,'head'=4] {'ctx'}, dimensions={0} | all-to-all | bytes 8388608 | tf_op jit(solution)/shard_map/all_to_all | solution.py:372
  126.3 0.0 copy-done.1
  126.3 0.0 copy-done
  126.3 3.8 %outgo.1 = bf16[32,1032,128]{2,1,0:T(8,128)(2,1)S(1)} custom-call(s32[512]{0:T(512)S(1)} %copy-done.2, s32[1]{0:T(128)} %bitcast.refs_1_.place, bf16[2048,1024]{1,0:T(8,128)(2,1)S(1)} %copy-done.1, f32[2048,1024]{1,0:T(8,128)S(1)} %copy-done, bf16[32,512,128]{2,1,0:T(8,128)(2,1)S(1)} %all_to_all.15.refs_4_), custom_call_target="tpu_custom_call" | custom-call | tf_op jit(solution)/shard_map/outgo/pallas_call | solution.py:271
  130.2 101.8 %all_to_all.16.came.refs_7_.refs_8_.refs_9_.refs_10_.refs_11_.refs_12_.refs_13_.refs_14_ = bf16[32,1032,128]{2,1,0:T(8,128)(2,1)S(1)} all-to-all(bf16[32,1032,128]{2,1,0:T(8,128)(2,1)S(1)} %outgo.1), channel_id=1, replica_groups=mesh['ctx'=32,'head'=4] {'ctx'}, dimensions={0} | all-to-all | bytes 16908288 | tf_op jit(solution)/shard_map/all_to_all | solution.py:372
  232.0 0.0 copy-start.3
  232.0 1.0 squares.1.refs_2_
  233.0 4.1 %collective-permute-start.2 = (f32[16,128]{1,0:T(8,128)S(1)}, f32[16,128]{1,0:T(8,128)S(1)}, u32[]{:S(2)}, u32[]{:S(2)}) collective-permute-start(f32[16,128]{1,0:T(8,128)S(1)} %squares.1.refs_2_), channel_id=1, source_target_pairs={{0,3},{1,0},{2,1},{3,2},{4,7},{5,4},{6,5},{7,6},{8,11},{9,8},{10,9... | collective-permute-start | bytes 24584 | tf_op jit(solution)/shard_map/ppermute | solution.py:398
  237.1 0.0 collective-permute-start.1
  237.2 1.3 collective-permute-start
  238.4 0.1 collective-permute-done.2.refs_5_
  238.5 3.8 %collective-permute-done.1.refs_4_ = f32[16,128]{1,0:T(8,128)S(1)} collective-permute-done((f32[16,128]{1,0:T(8,128)S(1)}, f32[16,128]{1,0:T(8,128)S(1)}, u32[]{:S(2)}, u32[]{:S(2)}) %collective-permute-start.1) | collective-permute-done | bytes 8224 | tf_op jit(solution)/shard_map/ppermute | solution.py:398
  242.3 0.0 collective-permute-done.refs_3_
  242.3 0.0 copy-done.3
  242.3 3.2 %finish.1 = bf16[2048,1024]{1,0:T(8,128)(2,1)} custom-call(s32[512]{0:T(512)S(1)} %select_reduce_fusion.refs_0_.order, s32[1]{0:T(128)} %bitcast.refs_1_.place, f32[16,128]{1,0:T(8,128)S(1)} %squares.1.refs_2_, f32[16,128]{1,0:T(8,128)S(1)} %collective-permute-done.refs_3_, f32[16,128]{1,0:T(8,128)S(1)} %collective-permute-done.1.refs_4_, ...), custom_call_target="tpu_custom_call" | custom-call | tf_op jit(solution)/shard_map/finish/pallas_call | solution.py:355
Async XLA Ops:
  6.8 60.5 %all-to-all-start = ((bf16[32,528,128]{2,1,0:T(8,128)(2,1)}), bf16[32,528,128]{2,1,0:T(8,128)(2,1)}, u32[]{:S(2)}, u32[]{:S(2)}) async-start(bf16[32,528,128]{2,1,0:T(8,128)(2,1)} %own.1), calls=%async_computation | async-start | bytes 8650752 | tf_op jit(solution)/shard_map/all_to_all | solution.py:372
  14.3 24.6 %copy-start.2 = (s32[512]{0:T(512)S(1)}, s32[512]{0:T(512)}, u32[]{:S(2)}) copy-start(s32[512]{0:T(512)} %refs_0_.5) | copy-start | bytes 6148
  67.3 59.0 %copy-start.1 = (bf16[2048,1024]{1,0:T(8,128)(2,1)S(1)}, bf16[2048,1024]{1,0:T(8,128)(2,1)}, u32[]{:S(2)}) copy-start(bf16[2048,1024]{1,0:T(8,128)(2,1)} %get-tuple-element.20.refs_2_) | copy-start | bytes 12582916
  72.0 54.3 %copy-start = (f32[2048,1024]{1,0:T(8,128)S(1)}, f32[2048,1024]{1,0:T(8,128)}, u32[]{:S(2)}) copy-start(f32[2048,1024]{1,0:T(8,128)} %get-tuple-element.21.refs_3_) | copy-start | bytes 25165828
  232.0 10.3 %copy-start.3 = (f32[1024]{0:T(1024)S(1)}, f32[1024]{0:T(1024)}, u32[]{:S(2)}) copy-start(f32[1024]{0:T(1024)} %param.11) | copy-start | bytes 12292
  233.0 5.5 %collective-permute-start.2 = (f32[16,128]{1,0:T(8,128)S(1)}, f32[16,128]{1,0:T(8,128)S(1)}, u32[]{:S(2)}, u32[]{:S(2)}) collective-permute-start(f32[16,128]{1,0:T(8,128)S(1)} %squares.1.refs_2_), channel_id=1, source_target_pairs={{0,3},{1,0},{2,1},{3,2},{4,7},{5,4},{6,5},{7,6},{8,11},{9,8},{10,9... | collective-permute-start | bytes 24584 | tf_op jit(solution)/shard_map/ppermute | solution.py:398
  237.1 5.2 %collective-permute-start.1 = (f32[16,128]{1,0:T(8,128)S(1)}, f32[16,128]{1,0:T(8,128)S(1)}, u32[]{:S(2)}, u32[]{:S(2)}) collective-permute-start(f32[16,128]{1,0:T(8,128)S(1)} %squares.1.refs_2_), channel_id=1, source_target_pairs={{0,2},{1,3},{2,0},{3,1},{4,6},{5,7},{6,4},{7,5},{8,10},{9,11},{10,... | collective-permute-start | bytes 24584 | tf_op jit(solution)/shard_map/ppermute | solution.py:398
  237.2 5.2 %collective-permute-start = (f32[16,128]{1,0:T(8,128)S(1)}, f32[16,128]{1,0:T(8,128)S(1)}, u32[]{:S(2)}, u32[]{:S(2)}) collective-permute-start(f32[16,128]{1,0:T(8,128)S(1)} %squares.1.refs_2_), channel_id=1, source_target_pairs={{0,1},{1,2},{2,3},{3,0},{4,5},{5,6},{6,7},{7,4},{8,9},{9,10},{10,1... | collective-permute-start | bytes 24584 | tf_op jit(solution)/shard_map/ppermute | solution.py:398
